TPU v7x, 32 devices: a whole 2x2x4 slice. The times are simulated.
32 devices in a mesh: fsdp: 16 (over z, y, x), rep: 2 (over core).
Axes of the slice: x: 2, y: 2, z: 4, core: 2. Of those that a mesh axis runs over, the one named last changes fastest.
Arguments:
- tokens: bfloat16 [2, 16, 1024, 1024], P('rep', None, 'fsdp'), may hold values from -6 to 6
- cotangent: bfloat16 [2, 16, 1024, 1024], P('rep', None, 'fsdp'), may hold values from -6 to 6
- w_qkv: bfloat16 [1024, 3072], P('fsdp'), may hold values from -0.1875 to 0.1875
- w_out: bfloat16 [1024, 1024], P('fsdp'), may hold values from -1.5 to 1.5
- w_up: bfloat16 [1024, 4096], P('fsdp'), may hold values from -0.1875 to 0.1875
- w_down: bfloat16 [4096, 1024], P('fsdp'), may hold values from -0.09375 to 0.09375
- w_router: bfloat16 [1024], P('fsdp'), may hold values from -0.1875 to 0.1875
- gain_attn: bfloat16 [1024], P('fsdp'), may hold values from 0.5 to 1.5
- gain_mlp: bfloat16 [1024], P('fsdp'), may hold values from 0.5 to 1.5
- lengths: int32 [2, 16], P('rep'), may hold values from 512 to 1024, as said below
- routed: int32 [2, 16, 128], P('rep'), may hold values from -1 to 1023, as said below
- dealing: int32 [2, 16], P('rep'), may hold values from 0 to 15, each once within a row
Outputs:
- output: bfloat16 [2, 16, 1024, 1024], P('rep', None, 'fsdp')
- grad_input: bfloat16 [2, 16, 1024, 1024], P('rep', None, 'fsdp')
- grad_qkv: float32 [1024, 3072], P('fsdp')
- grad_out: float32 [1024, 1024], P('fsdp')
- grad_up: float32 [1024, 4096], P('fsdp')
- grad_down: float32 [4096, 1024], P('fsdp')
- grad_router: float32 [1024], P('fsdp')
- grad_gain_attn: float32 [1024], P('fsdp')
- grad_gain_mlp: float32 [1024], P('fsdp')
Inputs may be any that keep to these rules, and one draw needn't show every extreme that they name: `lengths`: in each group one sequence has length exactly 1024 and another exactly 512. `routed`: for sequence s of group g, slots c < lengths[g, s] // 8 hold distinct positions below lengths[g, s] in rising order, the last of them lengths[g, s] - 1; the other slots hold -1.
All inputs are finite; a program needn't handle non-finite values.
Results may differ from a plain program's by a relative error of at most 0.013.
Values may be sent and summed in bfloat16 or wider, within the bound.
A program may use at most 192 MiB of HBM per device.

v0:
```python
import math

import jax
import jax.numpy as jnp
from jax import lax
from jax.sharding import PartitionSpec as P

D = 1024
HEADS = 16
HEAD_DIM = 64
SEQ_MAX = 1024
CAP = 128


EPSILON = 1e-06
EXACT_PRECISION = lax.Precision.HIGHEST


def normalize(values, gain):
    inverse = lax.rsqrt(jnp.mean(values * values, axis=-1, keepdims=True) + EPSILON)
    return (values * inverse * gain, inverse)


def rms_back(values, inverse, gain, grad_normed):
    scaled = gain * grad_normed
    grad_values = inverse * scaled - values * inverse**3 * jnp.mean(
        scaled * values, axis=-1, keepdims=True
    )
    grad_gain = jnp.sum(grad_normed * values * inverse, axis=(0, 1))
    return (grad_values, grad_gain)


def split_heads(packed, offset):
    return packed[..., offset : offset + D].reshape(packed.shape[:2] + (HEADS, HEAD_DIM))


def body(
    tokens,
    cotangent,
    w_qkv,
    w_out,
    w_up,
    w_down,
    w_router,
    gain_attn,
    gain_mlp,
    lengths,
    routed,
    dealing,
):
    factor = 1.0 / math.sqrt(HEAD_DIM)
    group_seqs = tokens.shape[1]
    per_device = group_seqs // lax.axis_size("fsdp")
    first_seq = lax.axis_index("fsdp") * per_device
    my_ids = lax.dynamic_slice_in_dim(dealing[0], first_seq, per_device)
    picker = my_ids[:, None] == jnp.arange(group_seqs, dtype=jnp.int32)[None, :]
    seq_lengths = jnp.sum(jnp.where(picker, lengths[0][None, :], 0), axis=1)
    seq_routes = jnp.sum(jnp.where(picker[:, :, None], routed[0][None, :, :], 0), axis=1)
    whole_tokens, whole_cot = (
        lax.all_to_all(tokens, "fsdp", split_axis=1, concat_axis=2, tiled=True),
        lax.all_to_all(cotangent, "fsdp", split_axis=1, concat_axis=2, tiled=True),
    )
    sequence_tokens = whole_tokens[0]
    sequence_cotangent = whole_cot[0]
    positions = jnp.arange(SEQ_MAX, dtype=jnp.int32)
    slot_ids = jnp.arange(CAP, dtype=jnp.int32)
    valid_slot = slot_ids[None, :] < (seq_lengths // 8)[:, None]
    selected_slots = (seq_routes[:, :, None] == positions[None, None, :]) & valid_slot[:, :, None]
    one_hot_matrix = selected_slots.astype(jnp.bfloat16)
    touched = jnp.any(selected_slots, axis=1)
    living = positions[None, :] < seq_lengths[:, None]
    incoming_rows = jnp.einsum(
        "puf,pfy->puy", one_hot_matrix, sequence_tokens, preferred_element_type=jnp.float32
    )
    row_gradient = jnp.einsum(
        "puf,pfy->puy", one_hot_matrix, sequence_cotangent, preferred_element_type=jnp.float32
    )
    gathered = (
        lax.all_gather(w_qkv, "fsdp", axis=0, tiled=True),
        lax.all_gather(w_out, "fsdp", axis=0, tiled=True),
        lax.all_gather(w_up, "fsdp", axis=0, tiled=True),
        lax.all_gather(w_down, "fsdp", axis=0, tiled=True),
        lax.all_gather(w_router, "fsdp", axis=0, tiled=True),
        lax.all_gather(gain_attn, "fsdp", axis=0, tiled=True),
        lax.all_gather(gain_mlp, "fsdp", axis=0, tiled=True),
    )
    rows_low = incoming_rows.astype(jnp.bfloat16)
    router_val = jnp.einsum("scd,d->sc", rows_low, gathered[4], preferred_element_type=jnp.float32)
    normed_attn, inverse_attn = normalize(incoming_rows, gathered[5].astype(jnp.float32))
    normed_low = normed_attn.astype(jnp.bfloat16)
    packed = jnp.einsum(
        "scd,de->sce", normed_low, gathered[0], preferred_element_type=jnp.float32
    ).astype(jnp.bfloat16)
    queries = split_heads(packed, 0)
    keys_heads = split_heads(packed, D)
    values_heads = split_heads(packed, 2 * D)
    scores = (
        jnp.einsum("sqhe,skhe->shqk", queries, keys_heads, preferred_element_type=jnp.float32)
        * factor
    )
    allowed = (slot_ids[None, :] <= slot_ids[:, None])[None, None] & valid_slot[:, None, None, :]
    scores = jnp.where(allowed, scores, -1e30)
    probs = jax.nn.softmax(scores, axis=-1)
    probs_low = probs.astype(jnp.bfloat16)
    attended = jnp.einsum(
        "shqk,skhe->sqhe", probs_low, values_heads, preferred_element_type=jnp.float32
    ).astype(jnp.bfloat16)
    attended = attended.reshape(incoming_rows.shape)
    branch_attn = jnp.einsum(
        "sce,ed->scd", attended, gathered[1], preferred_element_type=jnp.float32
    )
    middle = incoming_rows + branch_attn
    normed_mid, inverse_mid = normalize(middle, gathered[6].astype(jnp.float32))
    normed_mid_low = normed_mid.astype(jnp.bfloat16)
    upward = jnp.einsum(
        "scd,df->scf", normed_mid_low, gathered[2], preferred_element_type=jnp.float32
    )
    activated = jax.nn.gelu(upward).astype(jnp.bfloat16)
    branch_mlp = jnp.einsum(
        "scf,fd->scd", activated, gathered[3], preferred_element_type=jnp.float32
    )
    combined = branch_attn + branch_mlp
    refreshed_rows = (incoming_rows + router_val[..., None] * combined).astype(jnp.bfloat16)
    scattered = jnp.einsum(
        "jyv,jyi->jvi", one_hot_matrix, refreshed_rows, preferred_element_type=jnp.float32
    ).astype(jnp.bfloat16)
    output_seq = jnp.where(touched[..., None], scattered, sequence_tokens)
    output_seq = jnp.where(living[..., None], output_seq, jnp.zeros_like(output_seq))
    back_weights = (
        lax.all_gather(w_qkv, "fsdp", axis=0, tiled=True),
        lax.all_gather(w_out, "fsdp", axis=0, tiled=True),
        lax.all_gather(w_up, "fsdp", axis=0, tiled=True),
        lax.all_gather(w_down, "fsdp", axis=0, tiled=True),
        lax.all_gather(w_router, "fsdp", axis=0, tiled=True),
        lax.all_gather(gain_attn, "fsdp", axis=0, tiled=True),
        lax.all_gather(gain_mlp, "fsdp", axis=0, tiled=True),
    )
    grad_comb = router_val[..., None] * row_gradient
    grad_router_val = jnp.sum(row_gradient * combined, axis=-1)
    total_gradient = row_gradient + grad_router_val[..., None] * back_weights[4].astype(jnp.float32)
    grad_mlp_low = grad_comb.astype(jnp.bfloat16)
    grad_act = jnp.einsum(
        "scd,fd->scf", grad_mlp_low, back_weights[3], preferred_element_type=jnp.float32
    )
    grad_downw = jnp.einsum(
        "scf,scd->fd", activated, grad_mlp_low, preferred_element_type=jnp.float32
    )
    unused, gelu_pull = jax.vjp(jax.nn.gelu, upward)
    grad_up_low = gelu_pull(grad_act)[0].astype(jnp.bfloat16)
    grad_normed_mid = jnp.einsum(
        "scf,df->scd", grad_up_low, back_weights[2], preferred_element_type=jnp.float32
    )
    grad_upw = jnp.einsum(
        "scd,scf->df", normed_mid_low, grad_up_low, preferred_element_type=jnp.float32
    )
    grad_middle, grad_gain_second = rms_back(
        middle, inverse_mid, back_weights[6].astype(jnp.float32), grad_normed_mid
    )
    grad_attn_low = (grad_comb + grad_middle).astype(jnp.bfloat16)
    total_gradient = total_gradient + grad_middle
    grad_attended = jnp.einsum(
        "scd,ed->sce", grad_attn_low, back_weights[1], preferred_element_type=jnp.float32
    ).astype(jnp.bfloat16)
    grad_outw = jnp.einsum(
        "sce,scd->ed", attended, grad_attn_low, preferred_element_type=jnp.float32
    )
    grad_att_heads = grad_attended.reshape(queries.shape)
    grad_probs = jnp.einsum(
        "sqhe,skhe->shqk", grad_att_heads, values_heads, preferred_element_type=jnp.float32
    )
    grad_values = jnp.einsum(
        "shqk,sqhe->skhe", probs_low, grad_att_heads, preferred_element_type=jnp.float32
    )
    grad_scores = probs * (grad_probs - jnp.sum(probs * grad_probs, axis=-1, keepdims=True))
    grad_scores_low = grad_scores.astype(jnp.bfloat16)
    grad_queries = (
        jnp.einsum(
            "shqk,skhe->sqhe", grad_scores_low, keys_heads, preferred_element_type=jnp.float32
        )
        * factor
    )
    grad_keys = (
        jnp.einsum("shqk,sqhe->skhe", grad_scores_low, queries, preferred_element_type=jnp.float32)
        * factor
    )
    flat_shape = incoming_rows.shape
    grad_packed = jnp.concatenate(
        [
            grad_queries.reshape(flat_shape),
            grad_keys.reshape(flat_shape),
            grad_values.reshape(flat_shape),
        ],
        axis=-1,
    ).astype(jnp.bfloat16)
    grad_qkvw = jnp.einsum(
        "scd,sce->de", normed_low, grad_packed, preferred_element_type=jnp.float32
    )
    grad_normed_attn = jnp.einsum(
        "sce,de->scd", grad_packed, back_weights[0], preferred_element_type=jnp.float32
    )
    grad_first_rows, grad_gain_first = rms_back(
        incoming_rows, inverse_attn, back_weights[5].astype(jnp.float32), grad_normed_attn
    )
    total_gradient = total_gradient + grad_first_rows
    grad_routerw = jnp.einsum(
        "scd,sc->d", incoming_rows, grad_router_val, precision=EXACT_PRECISION
    )
    spread_back = jnp.einsum(
        "jyv,jyi->jvi",
        selected_slots.astype(jnp.float32),
        total_gradient,
        precision=EXACT_PRECISION,
    )
    grad_seq = jnp.where(touched[..., None], spread_back, sequence_cotangent.astype(jnp.float32))
    grad_seq = jnp.where(living[..., None], grad_seq, jnp.zeros_like(grad_seq)).astype(jnp.bfloat16)
    shares = (
        lax.psum_scatter(grad_qkvw, "fsdp", scatter_dimension=0, tiled=True),
        lax.psum_scatter(grad_outw, "fsdp", scatter_dimension=0, tiled=True),
        lax.psum_scatter(grad_upw, "fsdp", scatter_dimension=0, tiled=True),
        lax.psum_scatter(grad_downw, "fsdp", scatter_dimension=0, tiled=True),
        lax.psum_scatter(grad_routerw, "fsdp", scatter_dimension=0, tiled=True),
        lax.psum_scatter(grad_gain_first, "fsdp", scatter_dimension=0, tiled=True),
        lax.psum_scatter(grad_gain_second, "fsdp", scatter_dimension=0, tiled=True),
    )
    totals = (
        lax.psum(shares[0].astype(jnp.bfloat16), "rep").astype(jnp.float32),
        lax.psum(shares[1].astype(jnp.bfloat16), "rep").astype(jnp.float32),
        lax.psum(shares[2].astype(jnp.bfloat16), "rep").astype(jnp.float32),
        lax.psum(shares[3].astype(jnp.bfloat16), "rep").astype(jnp.float32),
        lax.psum(shares[4].astype(jnp.bfloat16), "rep").astype(jnp.float32),
        lax.psum(shares[5].astype(jnp.bfloat16), "rep").astype(jnp.float32),
        lax.psum(shares[6].astype(jnp.bfloat16), "rep").astype(jnp.float32),
    )
    back_out, back_grad = (
        lax.all_to_all(output_seq[None], "fsdp", split_axis=2, concat_axis=1, tiled=True),
        lax.all_to_all(grad_seq[None], "fsdp", split_axis=2, concat_axis=1, tiled=True),
    )
    return (
        back_out,
        back_grad,
        totals[0],
        totals[1],
        totals[2],
        totals[3],
        totals[4],
        totals[5],
        totals[6],
    )


def solution(mesh):
    placed = (
        P("rep", None, "fsdp", None),
        P("rep", None, "fsdp", None),
        P("fsdp", None),
        P("fsdp", None),
        P("fsdp", None),
        P("fsdp", None),
        P("fsdp"),
        P("fsdp"),
        P("fsdp"),
        P("rep", None),
        P("rep", None, None),
        P("rep", None),
    )
    return jax.shard_map(
        body,
        mesh=mesh,
        in_specs=placed,
        out_specs=(
            P("rep", None, "fsdp", None),
            P("rep", None, "fsdp", None),
            P("fsdp", None),
            P("fsdp", None),
            P("fsdp", None),
            P("fsdp", None),
            P("fsdp"),
            P("fsdp"),
            P("fsdp"),
        ),
        check_vma=False,
    )
```

profile of v0, /device:TPU:0, one launch (start us, length us, event | category | flops | bytes accessed | tf_op | source)
XLA Modules:
  0.0 1667.0 jit_solution(13122066171834117596)
XLA Ops:
  10.0 82.4 %all_to_all.42 = bf16[1,16,64,1024]{3,2,0,1:T(8,128)(2,1)S(1)} all-to-all(bf16[1,16,64,1024]{3,2,0,1:T(8,128)(2,1)} %bitcast.101), channel_id=1, replica_groups=mesh['fsdp'=16,'rep'=2] {'fsdp'}, dimensions={1} | all-to-all | bytes 4194304 | tf_op jit(solution)/shard_map/all_to_all | solution.py:60
  92.5 4.6 all-to-all-start.2
  103.6 89.8 %all-reduce.7 = (bf16[1024]{0:T(1024)(128)(2,1)S(1)}, bf16[1024]{0:T(1024)(128)(2,1)S(1)}, bf16[1024]{0:T(1024)(128)(2,1)S(1)}) all-reduce(bf16[1024]{0:T(1024)(128)(2,1)S(1)} %dynamic-update-slice.1, bf16[1024]{0:T(1024)(128)(2,1)S(1)} %dynamic-update-slice.2, ...), channel_id=1, replica_groups=mesh['fsdp'=16,'rep'=2] {'fsdp'}, use_global_device_ids=true, to_apply=%add.1 | all-reduce | flops 3072 | bytes 12288
  195.1 2.9 fusion.30
  197.9 3.8 fusion.1
  204.6 22.3 %all-gather.7.cloned.1.call-done = bf16[1024,1024]{1,0:T(8,128)(2,1)} async-done(((bf16[64,1024]{1,0:T(8,128)(2,1)}), bf16[1024,1024]{1,0:T(8,128)(2,1)}) %all-gather.7.cloned.1.call-update) | async-done | bytes 2097168 | tf_op jit(solution)/shard_map/all_gather | solution.py:80
  226.9 2.9 multiply_reduce_fusion.6
  229.8 111.0 %all-gather.9.cloned.1.call-done = bf16[1024,4096]{1,0:T(8,128)(2,1)} async-done(((bf16[64,4096]{1,0:T(8,128)(2,1)}), bf16[1024,4096]{1,0:T(8,128)(2,1)}) %all-gather.9.cloned.1.call-update) | async-done | bytes 8388624 | tf_op jit(solution)/shard_map/all_gather | solution.py:81
  340.8 4.7 fusion.67
  345.5 108.4 %all-gather.11.cloned.1.call-done = bf16[4096,1024]{1,0:T(8,128)(2,1)} async-done(((bf16[256,1024]{1,0:T(8,128)(2,1)}), bf16[4096,1024]{1,0:T(8,128)(2,1)}) %all-gather.11.cloned.1.call-update) | async-done | bytes 8388624 | tf_op jit(solution)/shard_map/all_gather | solution.py:82
  454.0 7.4 fusion.8
  461.4 3.0 multiply_reduce_fusion.1
  465.5 2.5 multiply_reduce_fusion.5
  468.7 2.9 fusion.71
  472.5 3.1 convolution_convert_fusion.2
  475.7 1.8 copy.72
  477.5 2.6 convolution_convert_fusion.1
  480.1 1.8 multiply_reduce_fusion
  484.3 6.4 fusion.35
  490.7 9.4 fusion.66
  500.6 9.2 fusion.64
  510.9 5.2 multiply_reduce_fusion.2
  516.1 4.3 fusion.9
  520.4 5.2 copy.85
  526.1 13.0 reduce.24
  539.1 2.8 reshape.639
  541.9 4.0 all-to-all-start.3
  545.9 2.5 select_bitcast_fusion
  548.4 5.2 copy.86
  553.5 14.1 reduce.23
  567.6 4.5 reshape.637
  572.1 22.4 %all-to-all-done.3 = bf16[16,2,32768]{2,1,0:T(2,128)(2,1)S(1)} async-done(((bf16[16,2,32768]{2,1,0:T(2,128)(2,1)}), bf16[16,2,32768]{2,1,0:T(2,128)(2,1)S(1)}, u32[]{:S(2)}, u32[]{:S(2)}) %all-to-all-start.3) | async-done | bytes 2097184 | tf_op jit(solution)/shard_map/all_to_all | solution.py:236
  594.5 11.2 all-to-all-start.1
  605.8 1.6 convert_element_type.155
  607.4 232.0 %reduce-scatter.5.cloned.1.call-done = f32[64,3072]{1,0:T(8,128)} async-done(((f32[1024,3072]{1,0:T(8,128)}), f32[64,3072]{1,0:T(8,128)}) %reduce-scatter.5.cloned.1.call-update) | async-done | bytes 786448 | tf_op jit(solution)/shard_map/reduce_scatter | solution.py:217
  839.3 1.9 convert_element_type.153
  841.3 346.3 %reduce-scatter.9.cloned.1.call-done = f32[64,4096]{1,0:T(8,128)} async-done(((f32[1024,4096]{1,0:T(8,128)}), f32[64,4096]{1,0:T(8,128)}) %reduce-scatter.9.cloned.1.call-update) | async-done | bytes 1048592 | tf_op jit(solution)/shard_map/reduce_scatter | solution.py:219
  1187.6 2.1 convert_element_type.157
  1189.6 352.3 %reduce-scatter.11.cloned.1.call-done = f32[256,1024]{1,0:T(8,128)} async-done(((f32[4096,1024]{1,0:T(8,128)}), f32[256,1024]{1,0:T(8,128)}) %reduce-scatter.11.cloned.1.call-update) | async-done | bytes 1048592 | tf_op jit(solution)/shard_map/reduce_scatter | solution.py:220
  1541.9 2.1 convert_element_type.159
  1545.1 79.3 %all-reduce.6 = (bf16[1024]{0:T(1024)(128)(2,1)S(1)}, bf16[1024]{0:T(1024)(128)(2,1)S(1)}, bf16[1024]{0:T(1024)(128)(2,1)S(1)}) all-reduce(f32[1024]{0:T(1024)S(1)} %bitcast.123, f32[1024]{0:T(1024)S(1)} %get-tuple-element.11, f32[1024]{0:T(1024)S(1)} %get-tuple-element.9), channel_id=6, replica_groups=mesh['fsdp'=16,'rep'=2] {'fsdp'}, use_global_device_ids=true, to_apply=%region_19.20.clone | all-reduce | flops 3072 | bytes 18432
  1624.6 2.4 all-reduce.8
  1628.6 6.7 reshape.640
  1635.3 4.3 copy.82
  1639.6 10.4 reshape.638
  1650.0 4.3 copy.81
  1654.3 2.1 convert_element_type.158
  1656.5 2.1 convert_element_type.160
  (133 shorter events, 21.5 us)
Async XLA Ops:
  7.2 89.9 %copy-start = (s32[1,16]{1,0:T(1,128)S(1)}, s32[1,16]{1,0:T(1,128)}, u32[]{:S(2)}) copy-start(s32[1,16]{1,0:T(1,128)} %param.23) | copy-start | bytes 196
  7.2 190.8 %all-gather.5.cloned.1.call-start = ((), (), s32[]{:S(2)}) async-start(), calls=%async_computation.8 | async-start | bytes 6684672 | tf_op jit(solution)/shard_map/all_gather | solution.py:79
  7.9 219.0 %all-gather.7.cloned.1.call-start = ((), (), s32[]{:S(2)}) async-start(), calls=%async_computation.9 | async-start | bytes 2228224 | tf_op jit(solution)/shard_map/all_gather | solution.py:80
  8.7 332.1 %all-gather.9.cloned.1.call-start = ((), (), s32[]{:S(2)}) async-start(), calls=%async_computation.10 | async-start | bytes 8912896 | tf_op jit(solution)/shard_map/all_gather | solution.py:81
  9.4 444.5 %all-gather.11.cloned.1.call-start = ((), (), s32[]{:S(2)}) async-start(), calls=%async_computation.11 | async-start | bytes 8912896 | tf_op jit(solution)/shard_map/all_gather | solution.py:82
  92.4 101.9 %copy-start.3 = (bf16[1,16,64,1024]{3,2,0,1:T(8,128)(2,1)}, bf16[1,16,64,1024]{3,2,0,1:T(8,128)(2,1)S(1)}, u32[]{:S(2)}) copy-start(bf16[1,16,64,1024]{3,2,0,1:T(8,128)(2,1)S(1)} %all_to_all.42) | copy-start | bytes 6291460
  92.4 5.3 copy-start.28
  92.4 9.2 copy-start.26
  92.4 10.5 copy-start.29
  92.4 10.7 copy-start.30
  92.4 10.9 copy-start.31
  92.4 101.6 %copy-start.25 = (s32[1,16,128]{2,1,0:T(8,128)S(1)}, s32[1,16,128]{2,1,0:T(8,128)}, u32[]{:S(2)}) copy-start(s32[1,16,128]{2,1,0:T(8,128)} %param.22) | copy-start | bytes 24580
  92.5 102.6 %all-to-all-start.2 = ((bf16[1,16,64,1024]{3,2,0,1:T(8,128)(2,1)}), bf16[1,16,64,1024]{3,2,0,1:T(8,128)(2,1)}, u32[]{:S(2)}, u32[]{:S(2)}) async-start(bf16[1,16,64,1024]{3,2,0,1:T(8,128)(2,1)} %bitcast.102), calls=%async_computation.2 | async-start | bytes 4194304 | tf_op jit(solution)/shard_map/all_to_all | solution.py:61
  97.1 508.7 %reduce-scatter.7.cloned.1.call-start = ((), (), s32[]{:S(2)}) async-start(), calls=%async_computation.13 | async-start | bytes 4456448 | tf_op jit(solution)/shard_map/reduce_scatter | solution.py:218
  202.0 2.6 copy-start.12
  202.2 2.4 copy-start.14
  202.4 2.2 copy-start.22
  454.0 7.4 copy-start.2
  461.3 3.0 copy-start.4
  461.4 3.0 copy-start.5
  461.4 3.0 copy-start.18
  461.4 4.1 copy-start.27
  464.4 3.6 copy-start.16
  468.0 0.7 copy-start.7
  471.6 0.9 copy-start.8
  471.6 367.7 %reduce-scatter.5.cloned.1.call-start = ((), (), s32[]{:S(2)}) async-start(), calls=%async_computation.12 | async-start | bytes 13369344 | tf_op jit(solution)/shard_map/reduce_scatter | solution.py:217
  477.5 2.6 copy-start.23
  480.1 1.8 copy-start.9
  481.9 1.0 copy-start.15
  481.9 1.2 copy-start.13
  481.9 2.4 copy-start.20
  483.6 0.7 copy-start.10
  490.7 696.9 %reduce-scatter.9.cloned.1.call-start = ((), (), s32[]{:S(2)}) async-start(), calls=%async_computation.14 | async-start | bytes 17825792 | tf_op jit(solution)/shard_map/reduce_scatter | solution.py:219
  500.2 1041.8 %reduce-scatter.11.cloned.1.call-start = ((), (), s32[]{:S(2)}) async-start(), calls=%async_computation.15 | async-start | bytes 17825792 | tf_op jit(solution)/shard_map/reduce_scatter | solution.py:220
  509.8 0.9 copy-start.11
  509.8 1.0 copy-start.21
  510.9 5.3 copy-start.6
  510.9 5.3 copy-start.17
  541.9 4.0 copy-start.32
  541.9 52.6 %all-to-all-start.3 = ((bf16[16,2,32768]{2,1,0:T(2,128)(2,1)}), bf16[16,2,32768]{2,1,0:T(2,128)(2,1)S(1)}, u32[]{:S(2)}, u32[]{:S(2)}) async-start(bf16[16,2,32768]{2,1,0:T(2,128)(2,1)} %reshape.639), calls=%async_computation.3 | async-start | bytes 4194304 | tf_op jit(solution)/shard_map/all_to_all | solution.py:236
  594.5 1045.1 %all-to-all-start.1 = ((bf16[16,2,32768]{2,1,0:T(2,128)(2,1)}), bf16[16,2,32768]{2,1,0:T(2,128)(2,1)}, u32[]{:S(2)}, u32[]{:S(2)}) async-start(bf16[16,2,32768]{2,1,0:T(2,128)(2,1)} %reshape.637), calls=%async_computation.1 | async-start | bytes 4194304 | tf_op jit(solution)/shard_map/all_to_all | solution.py:235
  605.7 1048.6 %all-reduce.12.cloned.1.call-start = ((), (), s32[]{:S(2)}) async-start(), calls=%async_computation.16 | async-start | bytes 3145728 | tf_op jit(solution)/shard_map/psum | solution.py:226
  1654.3 4.3 copy-start.19
  1654.3 5.9 copy-start.1
  1654.3 5.2 copy-start.24
Sparse Core Ops, SparseCore 0:
  10.8 154.0 all-gather.4
  167.6 59.2 all-gather.6
  229.7 111.0 all-gather.8
  343.4 110.4 all-gather.10
  471.7 109.1 reduce-scatter.6
  586.4 252.8 reduce-scatter.4
  841.6 345.8 reduce-scatter.8
  1189.9 352.0 reduce-scatter.10
  1545.1 26.1 all-reduce.11
where the time goes:
time: 1680 us; the launch traced here: 1670 us
  waiting for transfers between devices  1200 us (71%)
  blocking collectives  254 us (15%)
  matrix products  78.5 us (5%)
  local copies, waits for them, and re-layouts  52.7 us (3%)
  other arithmetic  45.4 us (3%)
  starting transfers between devices  20.5 us (1%)
  between operations  18.5 us (1%)
    reduce_scatter x1, waiting for transfers between devices, body(): lax.psum_scatter(grad_downw, 'fsdp', scatter_dimension=0, tiled=True)  352 us
    reduce_scatter x1, waiting for transfers between devices, body(): lax.psum_scatter(grad_upw, 'fsdp', scatter_dimension=0, tiled=True)  346 us
    reduce_scatter x1, waiting for transfers between devices, body(): lax.psum_scatter(grad_qkvw, 'fsdp', scatter_dimension=0, tiled=True)  232 us
    unnamed x2, blocking collectives  169 us
    all_gather x1, waiting for transfers between devices, body(): lax.all_gather(w_up, 'fsdp', axis=0, tiled=True)  111 us
    all_gather x1, waiting for transfers between devices, body(): lax.all_gather(w_down, 'fsdp', axis=0, tiled=True)  108 us
    all_to_all x1, blocking collectives, body(): lax.all_to_all(tokens, 'fsdp', split_axis=1, concat_axis=2, tiled=True)  82.4 us
    unnamed x84, local copies, waits for them, and re-layouts  39.4 us
  transfers between devices with their start and end apart: 12, of which 7 were waited for; matrix products, arithmetic and copies ran while one was open for 9% of the time, Pallas kernels for 0%

commit v1 on v0

--- a/solution.py
+++ b/solution.py
@@ -1,8 +1,530 @@
-import math
+import functools
 
 import jax
 import jax.numpy as jnp
 from jax import lax
+from jax.experimental import pallas as pl
+from jax.experimental.pallas import tpu as pltpu
+
+MESH = pl.DeviceIdType.MESH
+ANY = pl.ANY
+
+
+def grid_axes(mesh):
+    devices = mesh.devices[:, 0]
+    count = len(devices)
+    axes = []
+    spots = [getattr(d, "coords", None) for d in devices]
+    if all(s is not None for s in spots) and len(set(map(tuple, spots))) == count:
+        low = [min(s[k] for s in spots) for k in range(3)]
+        at = {tuple(s[k] - low[k] for k in range(3)): f for f, s in enumerate(spots)}
+        for k in range(3):
+            size = max(s[k] for s in spots) - low[k] + 1
+            one = tuple(int(j == k) for j in range(3))
+            axes.append((at[one] if size > 1 else 1, size, k))
+        ok = all(
+            f == sum(stride * spot[k] for stride, _, k in axes) for spot, f in at.items()
+        )
+        axes = [a[:2] for a in axes] if ok else []
+    if not axes:
+        axes, left = [], count
+        for size in (2, 2):
+            size = size if left % size == 0 and left > 1 else 1
+            axes.append((count // left, size))
+            left //= size
+        axes.append((count // left, left))
+    return sorted(axes, key=lambda a: -a[1])
+
+
+def xor(a, b, size):
+    out, bit = 0, 1
+    while bit < size:
+        out = out + ((a // bit + b // bit) % 2) * bit
+        bit *= 2
+    return out
+
+
+class Piece:
+    def __init__(self, array, half, offset, width):
+        self.array, self.half, self.offset, self.width = array, half, offset, width
+
+    def cols(self, core):
+        start = self.offset
+        if self.half:
+            start = core * self.half + start
+            start = pl.multiple_of(start, 128)
+        return pl.ds(start, self.width)
+
+
+def colours(axes, widths):
+    qkv, out, up, down = (w // 2 for w in widths[:4])
+    a, b, c = axes
+    third = qkv // 3
+    return [
+        ((b, c, a), [Piece(1, out, 0, out), Piece(4, 0, 0, widths[4])]),
+        ((c, b, a), [Piece(0, qkv, 0, third)]),
+        ((a, b, c), [Piece(2, up, 0, up), Piece(0, qkv, third, third)]),
+        ((a, c, b), [Piece(3, down, 0, down), Piece(0, qkv, 2 * third, third)]),
+    ]
+
+
+def neighbours(axes, me):
+    found = []
+    for stride, size in axes:
+        at = (me // stride) % size
+        if size == 2:
+            found.append((None, (1 - 2 * at) * stride))
+        elif size > 2:
+            found.append((at < size - 1, stride))
+            found.append((at > 0, -stride))
+    return found
+
+
+def guarded(cond, fn):
+    if cond is None:
+        fn()
+    else:
+        pl.when(cond)(fn)
+
+
+def enter(axes, me, core):
+    barrier = pltpu.get_barrier_semaphore()
+    total = 1
+    for cond, step in neighbours(axes, me):
+        def hello(step=step):
+            pl.semaphore_signal(barrier, inc=1, device_id=(me + step, core), device_id_type=MESH)
+        guarded(cond, hello)
+        total = total + (1 if cond is None else cond.astype(jnp.int32))
+    pl.semaphore_signal(barrier, inc=1, device_id=(me, 1 - core), device_id_type=MESH)
+    pl.semaphore_wait(barrier, total)
+
+
+def gather_kernel(axes, plan, n, *refs):
+    k = 5
+    ins, outs = refs[:k], refs[k : 2 * k]
+    stages = refs[2 * k : 3 * k]
+    send_sem, recv_sem, pair_send, pair_recv, local_sem = refs[3 * k :]
+    me, core = lax.axis_index("fsdp"), lax.axis_index("rep")
+    enter(axes, me, core)
+    numbered, number = [], 0
+    for order, pieces in plan:
+        numbered.append((order, [(number + i, p) for i, p in enumerate(pieces)]))
+        number += len(pieces)
+
+    def spot(axis):
+        return (me // axis[0]) % axis[1]
+
+    def dst(piece, block):
+        return outs[piece.array].at[block, :, piece.cols(core)]
+
+    def put(pieces, block, own, phase, way, device, pair=False):
+        for i, piece in pieces:
+            if pair and not piece.half:
+                continue
+            src = ins[piece.array].at[:, piece.cols(core)] if own else dst(piece, block)
+            pltpu.make_async_remote_copy(
+                src_ref=src,
+                dst_ref=dst(piece, block),
+                send_sem=pair_send.at[i] if pair else send_sem.at[i, phase, way],
+                recv_sem=pair_recv.at[i] if pair else recv_sem.at[i, block],
+                device_id=device,
+                device_id_type=MESH,
+            ).start()
+
+    def along(pieces, order, block, own, phase, ways):
+        stride, size = order[phase]
+        at = spot(order[phase])
+        if size == 1:
+            return
+        if size == 2:
+            put(pieces, block, own, phase, 0, (me + (1 - 2 * at) * stride, core))
+            return
+        for way in ways:
+            step = 1 - 2 * way
+            pl.when(at < size - 1 if way == 0 else at > 0)(
+                functools.partial(put, pieces, block, own, phase, way, (me + step * stride, core))
+            )
+
+    def arrived(pieces, order, block, phase, way):
+        for i, piece in pieces:
+            pltpu.make_async_remote_copy(
+                src_ref=dst(piece, block),
+                dst_ref=dst(piece, block),
+                send_sem=send_sem.at[i, phase, way],
+                recv_sem=recv_sem.at[i, block],
+                device_id=(me, 1 - core),
+                device_id_type=MESH,
+            ).wait_recv()
+        if order[phase][1] > 2:
+            along(pieces, order, block, False, phase, (way,))
+        for later in range(phase + 1, 3):
+            along(pieces, order, block, False, later, (0, 1))
+        put(pieces, block, False, 0, 0, (me, 1 - core), pair=True)
+
+    for order, pieces in numbered:
+        for phase in range(3):
+            along(pieces, order, me, True, phase, (0, 1))
+    local = []
+    for j in range(k):
+        local.append(pltpu.make_async_copy(ins[j], stages[j], local_sem.at[j]))
+        local[-1].start()
+    events = []
+    for number, (order, pieces) in enumerate(numbered):
+        heavy = number >= 2
+        sizes = [a[1] for a in order]
+        for phase in range(3):
+            size = sizes[phase]
+            rest = 1
+            for s in sizes[:phase]:
+                rest *= s
+            for t in range(1, size):
+                ways = (0,) if size == 2 else (0, 1)
+                for way in ways:
+                    for j in range(rest):
+                        if heavy:
+                            key = 20 * t if phase == 0 else 20 * phase + 20 * (j + (t - 1) * rest + 1)
+                        else:
+                            key = 5 if phase == 0 else 10 + 5 * j if phase == 1 else 15 + 40 * t + 5 * j
+                        events.append((key, len(events), order, pieces, phase, t, way, j))
+    events.sort(key=lambda e: e[:2])
+
+    def run(order, pieces, phase, t, way, j):
+        stride, size = order[phase]
+        at = spot(order[phase])
+        origin = 1 - at if size == 2 else at - (1 - 2 * way) * t
+        block = me + (origin - at) * stride
+        for s, z in order[:phase]:
+            here = (me // s) % z
+            block = block + (xor(here, j % z, z) - here) * s
+            j = j // z
+        if size == 2:
+            arrived(pieces, order, block, phase, 0)
+        else:
+            pl.when((origin >= 0) & (origin < size))(
+                functools.partial(arrived, pieces, order, block, phase, way)
+            )
+
+    def settle():
+        for j in range(k):
+            local[j].wait()
+            local[j] = pltpu.make_async_copy(stages[j], outs[j].at[me], local_sem.at[j])
+            local[j].start()
+
+    for number, (_, _, order, pieces, phase, t, way, j) in enumerate(events):
+        run(order, pieces, phase, t, way, j)
+        if number == 3:
+            settle()
+    for copy in local:
+        copy.wait()
+
+    def drain(i, piece, count, send, recv, which):
+        many = outs[piece.array].at[pl.ds(0, count), :, piece.cols(core)]
+        copy = pltpu.make_async_remote_copy(
+            src_ref=many, dst_ref=many, send_sem=send, recv_sem=recv,
+            device_id=(me, 1 - core), device_id_type=MESH,
+        )
+        if which == "send":
+            copy.wait_send()
+        else:
+            copy.wait_recv()
+
+    for order, pieces in numbered:
+        rest = 1
+        for phase in range(3):
+            stride, size = order[phase]
+            at = spot(order[phase])
+            for i, piece in pieces:
+                if size == 2:
+                    drain(i, piece, rest, send_sem.at[i, phase, 0], recv_sem.at[i, 0], "send")
+                elif size > 2:
+                    for here in range(size):
+                        def both(here=here, i=i, piece=piece, phase=phase, rest=rest, size=size):
+                            if here < size - 1:
+                                drain(i, piece, (here + 1) * rest, send_sem.at[i, phase, 0], recv_sem.at[i, 0], "send")
+                            if here > 0:
+                                drain(i, piece, (size - here) * rest, send_sem.at[i, phase, 1], recv_sem.at[i, 0], "send")
+                        pl.when(at == here)(both)
+            rest *= size
+        for i, piece in pieces:
+            if piece.half:
+                drain(i, piece, n - 1, pair_send.at[i], pair_recv.at[i], "send")
+                drain(i, piece, n - 1, pair_send.at[i], pair_recv.at[i], "recv")
+
+
+def gather_all(axes, n, arrays, collective_id):
+    plan = colours(axes, [a.shape[1] for a in arrays])
+    pieces = sum(len(p) for _, p in plan)
+    return pl.pallas_call(
+        functools.partial(gather_kernel, axes, plan, n),
+        out_shape=[jax.ShapeDtypeStruct((n,) + a.shape, a.dtype) for a in arrays],
+        in_specs=[pl.BlockSpec(memory_space=ANY)] * len(arrays),
+        out_specs=[pl.BlockSpec(memory_space=ANY)] * len(arrays),
+        scratch_shapes=[pltpu.VMEM(a.shape, a.dtype) for a in arrays]
+        + [
+            pltpu.SemaphoreType.DMA((pieces, 3, 2)),
+            pltpu.SemaphoreType.DMA((pieces, n)),
+            pltpu.SemaphoreType.DMA((pieces,)),
+            pltpu.SemaphoreType.DMA((pieces,)),
+            pltpu.SemaphoreType.DMA((len(arrays),)),
+        ],
+        compiler_params=pltpu.CompilerParams(collective_id=collective_id, has_side_effects=True),
+        name="gather_all",
+    )(*arrays)
+def add_into(acc, a, got, g, rows):
+    step = min(rows, 16)
+
+    def go(i, _):
+        at = pl.ds(pl.multiple_of(i * step, step), step)
+        acc[a, at, :] = (acc[a, at, :].astype(jnp.float32) + got[g, at, :].astype(jnp.float32)).astype(acc.dtype)
+        return 0
+
+    lax.fori_loop(0, rows // step, go, 0)
+
+
+def slots(size):
+    return 1 if size <= 2 else size + 1
+
+
+def scatter_kernel(axes, plan, n, *refs):
+    k = 5
+    ins, outs = refs[:k], refs[k : 2 * k]
+    total = sum(len(p) for _, p in plan)
+    buffers = refs[2 * k : 2 * k + 5 * total]
+    own_sem, pair_send, pair_recv, send_sem, recv_sems, last_send, last_recv = (
+        refs[-9], refs[-8], refs[-7], refs[-6], refs[-5:-2], refs[-2], refs[-1]
+    )
+    me, core = lax.axis_index("fsdp"), lax.axis_index("rep")
+    enter(axes, me, core)
+    numbered, number = [], 0
+    for order, pieces in plan:
+        numbered.append((order, [(number + i, p) for i, p in enumerate(pieces)]))
+        number += len(pieces)
+    acc = [buffers[5 * i] for i in range(total)]
+    pair = [buffers[5 * i + 1] for i in range(total)]
+    got = [buffers[5 * i + 2 : 5 * i + 5] for i in range(total)]
+
+    def spot(axis):
+        return (me // axis[0]) % axis[1]
+
+    def pair_copy(i, piece, block):
+        return pltpu.make_async_remote_copy(
+            src_ref=ins[piece.array].at[block, :, piece.cols(1 - core)],
+            dst_ref=pair[i].at[block],
+            send_sem=pair_send.at[i],
+            recv_sem=pair_recv.at[i, block],
+            device_id=(me, 1 - core),
+            device_id_type=MESH,
+        )
+
+    def own_copy(i, piece, block):
+        return pltpu.make_async_copy(
+            ins[piece.array].at[block, :, piece.cols(core)], acc[i].at[block], own_sem.at[i, block]
+        )
+
+    def block_at(order, phase, origin, rest):
+        stride = order[phase][0]
+        block = me + (origin - spot(order[phase])) * stride
+        for s, z in order[:phase]:
+            here = (me // s) % z
+            block = block + (xor(here, z - 1 - rest % z, z) - here) * s
+            rest = rest // z
+        return block
+
+    def rests(order, phase):
+        count = 1
+        for _, z in order[:phase]:
+            count *= z
+        return count
+
+    def ready(pieces, block):
+        for i, piece in pieces:
+            own_copy(i, piece, block).wait()
+            pair_copy(i, piece, block).wait_recv()
+            add_into(acc[i], block, pair[i], block, acc[i].shape[1])
+
+    def hop(i, phase, block, rest, slot, send, device):
+        return pltpu.make_async_remote_copy(
+            src_ref=acc[i].at[block],
+            dst_ref=got[i][phase].at[rest, slot],
+            send_sem=send,
+            recv_sem=recv_sems[phase].at[i, rest * got[i][phase].shape[1] + slot],
+            device_id=device,
+            device_id_type=MESH,
+        )
+
+    def take(pieces, phase, block, rest, slot):
+        for i, piece in pieces:
+            hop(i, phase, block, rest, slot, send_sem.at[i, phase], (me, 1 - core)).wait_recv()
+            add_into(acc[i], block, got[i][phase].at[rest], slot, acc[i].shape[1])
+
+    def give(pieces, phase, block, rest, slot, device):
+        for i, piece in pieces:
+            hop(i, phase, block, rest, slot, send_sem.at[i, phase], device).start()
+
+    def event(order, pieces, phase, e, first):
+        stride, size = order[phase]
+        rest_count = rests(order, phase)
+        at = spot(order[phase])
+        far, rest = size - 1 - e // rest_count, e % rest_count
+        origin = xor(at, far, size)
+        block = block_at(order, phase, origin, rest)
+        if first:
+            ready(pieces, block)
+        if size == 1:
+            return
+        if size == 2:
+            pl.when(far == 1)(
+                lambda: give(pieces, phase, block, rest, 0, (me + (1 - 2 * at) * stride, core))
+            )
+            pl.when(far == 0)(lambda: take(pieces, phase, block, rest, 0))
+            return
+
+        @pl.when(far > 0)
+        def _():
+            up = (origin > at).astype(jnp.int32)
+            behind = jnp.where(up == 1, at > 0, at < size - 1)
+            pl.when(behind)(lambda: take(pieces, phase, block, rest, origin))
+            step = 2 * up - 1
+            landing = jnp.where((up == 0) & (origin == at - 1), size, origin)
+            give(pieces, phase, block, rest, landing, (me + step * stride, core))
+
+        @pl.when(far == 0)
+        def _():
+            pl.when(at > 0)(lambda: take(pieces, phase, block, rest, at))
+            pl.when(at < size - 1)(lambda: take(pieces, phase, block, rest, size))
+
+    for stage in range(2):
+        for order, pieces in numbered:
+            last = order[2]
+            count = rests(order, 2)
+
+            def begin(e, _, order=order, pieces=pieces):
+                far, rest = order[2][1] - 1 - e // rests(order, 2), e % rests(order, 2)
+                block = block_at(order, 2, xor(spot(order[2]), far, order[2][1]), rest)
+                for i, piece in pieces:
+                    pair_copy(i, piece, block).start()
+                    own_copy(i, piece, block).start()
+                return 0
+
+            lead = (last[1] - 1) * count
+            lax.fori_loop(0 if stage == 0 else lead, lead if stage == 0 else n, begin, 0)
+
+    tasks = []
+    for number, (order, pieces) in enumerate(numbered):
+        lead = (order[2][1] - 1) * rests(order, 2)
+        later = rests(order, 2)
+        inner = rests(order, 1)
+        tasks.append((number, order, pieces, lead, later, inner))
+
+    def lead_event(order, pieces, e):
+        event(order, pieces, 2, e, True)
+
+    def later_event(order, pieces, e, lead, later, inner):
+        event(order, pieces, 2, lead + e, True)
+        event(order, pieces, 1, e, False)
+        pl.when(e >= later - inner)(lambda: event(order, pieces, 0, e - (later - inner), False))
+
+    def loop(count, fns):
+        def go(e, _):
+            for size, fn in fns:
+                if size == count:
+                    fn(e)
+                else:
+                    pl.when(e < size)(lambda fn=fn: fn(e))
+            return 0
+
+        lax.fori_loop(0, count, go, 0)
+
+    light, heavy = tasks[:2], tasks[2:]
+    loop(max(t[3] for t in heavy), [(t[3], functools.partial(lead_event, t[1], t[2])) for t in heavy])
+    both = [(t[3], functools.partial(lead_event, t[1], t[2])) for t in light] + [
+        (t[4], functools.partial(lambda e, t: later_event(t[1], t[2], e, *t[3:]), t=t)) for t in heavy
+    ]
+    loop(max(b[0] for b in both), both)
+    loop(
+        max(t[4] for t in light),
+        [(t[4], functools.partial(lambda e, t: later_event(t[1], t[2], e, *t[3:]), t=t)) for t in light],
+    )
+
+    final = []
+    for order, pieces in numbered:
+        for i, piece in pieces:
+            outs[piece.array][:, piece.cols(core)] = acc[i][me]
+            if piece.half:
+                final.append(
+                    pltpu.make_async_remote_copy(
+                        src_ref=acc[i].at[me],
+                        dst_ref=outs[piece.array].at[:, piece.cols(core)],
+                        send_sem=last_send.at[i],
+                        recv_sem=last_recv.at[i],
+                        device_id=(me, 1 - core),
+                        device_id_type=MESH,
+                    )
+                )
+                final[-1].start()
+    for copy in final:
+        copy.wait()
+
+    def drain(i, phase, count):
+        many = acc[i].at[pl.ds(0, count)]
+        pltpu.make_async_remote_copy(
+            src_ref=many, dst_ref=many, send_sem=send_sem.at[i, phase], recv_sem=last_recv.at[i],
+            device_id=(me, 1 - core), device_id_type=MESH,
+        ).wait_send()
+
+    for order, pieces in numbered:
+        for i, piece in pieces:
+            for phase in range(3):
+                if order[phase][1] > 1:
+                    drain(i, phase, (order[phase][1] - 1) * rests(order, phase))
+            many = acc[i].at[pl.ds(0, n)]
+            pltpu.make_async_remote_copy(
+                src_ref=many, dst_ref=many, send_sem=pair_send.at[i], recv_sem=last_recv.at[i],
+                device_id=(me, 1 - core), device_id_type=MESH,
+            ).wait_send()
+
+
+def scatter_all(axes, n, arrays, collective_id):
+    plan = colours(axes, [a.shape[2] for a in arrays])
+    pieces = [(order, p) for order, ps in plan for p in ps]
+    scratch = []
+    for order, p in pieces:
+        rows, dtype = arrays[p.array].shape[1], arrays[p.array].dtype
+        scratch += [pltpu.VMEM((n, rows, p.width), dtype)] * 2
+        count = 1
+        for phase in range(3):
+            size = order[phase][1]
+            scratch.append(pltpu.VMEM((count, slots(size), rows, p.width), dtype))
+            count *= size
+    total = len(pieces)
+    shapes = []
+    for phase in range(3):
+        most = 1
+        for order, _ in plan:
+            count = slots(order[phase][1])
+            for a in order[:phase]:
+                count *= a[1]
+            most = max(most, count)
+        shapes.append((total, most))
+    dma = pltpu.SemaphoreType.DMA
+    return pl.pallas_call(
+        functools.partial(scatter_kernel, axes, plan, n),
+        out_shape=[jax.ShapeDtypeStruct(a.shape[1:], a.dtype) for a in arrays],
+        in_specs=[pl.BlockSpec(memory_space=ANY)] * len(arrays),
+        out_specs=[pl.BlockSpec(memory_space=pltpu.VMEM)] * len(arrays),
+        scratch_shapes=scratch
+        + [dma((total, n)), dma((total,)), dma((total, n)), dma((total, 3))]
+        + [dma(s) for s in shapes]
+        + [dma((total,)), dma((total,))],
+        compiler_params=pltpu.CompilerParams(
+            collective_id=collective_id, has_side_effects=True, vmem_limit_bytes=60 * 1024 * 1024
+        ),
+        name="scatter_all",
+    )(*arrays)
+
+
+import math
+
 from jax.sharding import PartitionSpec as P
 
 D = 1024
@@ -35,6 +557,7 @@
 
 
 def body(
+    axes,
     tokens,
     cotangent,
     w_qkv,
@@ -75,15 +598,12 @@
     row_gradient = jnp.einsum(
         "puf,pfy->puy", one_hot_matrix, sequence_cotangent, preferred_element_type=jnp.float32
     )
-    gathered = (
-        lax.all_gather(w_qkv, "fsdp", axis=0, tiled=True),
-        lax.all_gather(w_out, "fsdp", axis=0, tiled=True),
-        lax.all_gather(w_up, "fsdp", axis=0, tiled=True),
-        lax.all_gather(w_down, "fsdp", axis=0, tiled=True),
-        lax.all_gather(w_router, "fsdp", axis=0, tiled=True),
-        lax.all_gather(gain_attn, "fsdp", axis=0, tiled=True),
-        lax.all_gather(gain_mlp, "fsdp", axis=0, tiled=True),
-    )
+    shards = lax.axis_size("fsdp")
+    part = w_router.shape[0]
+    vectors = jnp.pad(jnp.stack([w_router, gain_attn, gain_mlp]), ((0, 13), (0, 128 - part)))
+    blocks = gather_all(axes, shards, [w_qkv, w_out, w_up, w_down, vectors], 0)
+    small = blocks[4][:, :3, :part].transpose(1, 0, 2).reshape(3, D)
+    gathered = tuple(b.reshape(-1, b.shape[2]) for b in blocks[:4]) + (small[0], small[1], small[2])
     rows_low = incoming_rows.astype(jnp.bfloat16)
     router_val = jnp.einsum("scd,d->sc", rows_low, gathered[4], preferred_element_type=jnp.float32)
     normed_attn, inverse_attn = normalize(incoming_rows, gathered[5].astype(jnp.float32))
@@ -126,15 +646,7 @@
     ).astype(jnp.bfloat16)
     output_seq = jnp.where(touched[..., None], scattered, sequence_tokens)
     output_seq = jnp.where(living[..., None], output_seq, jnp.zeros_like(output_seq))
-    back_weights = (
-        lax.all_gather(w_qkv, "fsdp", axis=0, tiled=True),
-        lax.all_gather(w_out, "fsdp", axis=0, tiled=True),
-        lax.all_gather(w_up, "fsdp", axis=0, tiled=True),
-        lax.all_gather(w_down, "fsdp", axis=0, tiled=True),
-        lax.all_gather(w_router, "fsdp", axis=0, tiled=True),
-        lax.all_gather(gain_attn, "fsdp", axis=0, tiled=True),
-        lax.all_gather(gain_mlp, "fsdp", axis=0, tiled=True),
-    )
+    back_weights = gathered
     grad_comb = router_val[..., None] * row_gradient
     grad_router_val = jnp.sum(row_gradient * combined, axis=-1)
     total_gradient = row_gradient + grad_router_val[..., None] * back_weights[4].astype(jnp.float32)
@@ -213,24 +725,15 @@
     )
     grad_seq = jnp.where(touched[..., None], spread_back, sequence_cotangent.astype(jnp.float32))
     grad_seq = jnp.where(living[..., None], grad_seq, jnp.zeros_like(grad_seq)).astype(jnp.bfloat16)
-    shares = (
-        lax.psum_scatter(grad_qkvw, "fsdp", scatter_dimension=0, tiled=True),
-        lax.psum_scatter(grad_outw, "fsdp", scatter_dimension=0, tiled=True),
-        lax.psum_scatter(grad_upw, "fsdp", scatter_dimension=0, tiled=True),
-        lax.psum_scatter(grad_downw, "fsdp", scatter_dimension=0, tiled=True),
-        lax.psum_scatter(grad_routerw, "fsdp", scatter_dimension=0, tiled=True),
-        lax.psum_scatter(grad_gain_first, "fsdp", scatter_dimension=0, tiled=True),
-        lax.psum_scatter(grad_gain_second, "fsdp", scatter_dimension=0, tiled=True),
-    )
-    totals = (
-        lax.psum(shares[0].astype(jnp.bfloat16), "rep").astype(jnp.float32),
-        lax.psum(shares[1].astype(jnp.bfloat16), "rep").astype(jnp.float32),
-        lax.psum(shares[2].astype(jnp.bfloat16), "rep").astype(jnp.float32),
-        lax.psum(shares[3].astype(jnp.bfloat16), "rep").astype(jnp.float32),
-        lax.psum(shares[4].astype(jnp.bfloat16), "rep").astype(jnp.float32),
-        lax.psum(shares[5].astype(jnp.bfloat16), "rep").astype(jnp.float32),
-        lax.psum(shares[6].astype(jnp.bfloat16), "rep").astype(jnp.float32),
-    )
+    small_grads = jnp.stack([grad_routerw, grad_gain_first, grad_gain_second])
+    small_grads = small_grads.reshape(3, shards, part).transpose(1, 0, 2)
+    small_grads = jnp.pad(small_grads, ((0, 0), (0, 5), (0, 128 - part)))
+    partial = [
+        g.astype(jnp.bfloat16).reshape(shards, -1, g.shape[1])
+        for g in (grad_qkvw, grad_outw, grad_upw, grad_downw)
+    ]
+    shares = scatter_all(axes, shards, partial + [small_grads], 1)
+    totals = tuple(t.astype(jnp.float32) for t in shares[:4]) + tuple(shares[4][j, :part] for j in range(3))
     back_out, back_grad = (
         lax.all_to_all(output_seq[None], "fsdp", split_axis=2, concat_axis=1, tiled=True),
         lax.all_to_all(grad_seq[None], "fsdp", split_axis=2, concat_axis=1, tiled=True),
@@ -264,7 +767,7 @@
         P("rep", None),
     )
     return jax.shard_map(
-        body,
+        functools.partial(body, grid_axes(mesh)),
         mesh=mesh,
         in_specs=placed,
         out_specs=(

time: 1680 us -> 598 us (0.36)
  waiting for transfers between devices: 1200 us -> 16.9 us
  Pallas kernels: 0 us -> 327 us
  blocking collectives: 254 us -> 57.1 us
    reduce_scatter x4 -> x0, waiting for transfers between devices: 931 us -> none  [the longest x1 352 us: body(): lax.psum_scatter(grad_downw, 'fsdp', scatter_dimension=0, tiled=True)]
    pallas_call x0 -> x2, Pallas kernels: none -> 327 us  [the longest x1 201 us: scatter_all(): pl.pallas_call(functools.partial(scatter_kernel, axes, plan, n), out_shap...]
    all_gather x4 -> x0, waiting for transfers between devices: 242 us -> none  [the longest x1 111 us: body(): lax.all_gather(w_up, 'fsdp', axis=0, tiled=True)]
    unnamed x2 -> x0, blocking collectives: 169 us -> none
    all_to_all x1, blocking collectives: 82.4 us -> 57.1 us  [body(): lax.all_to_all(tokens, 'fsdp', split_axis=1, concat_axis=2, tiled=True)]
    unnamed x84 -> x73, local copies, waits for them, and re-layouts: 39.4 us -> 40.6 us
  transfers between devices with their start and end apart: 12 -> 3, of which waited for: 7 -> 1; matrix products, arithmetic and copies ran while one was open for 9% -> 15% of each run, Pallas kernels for 0% -> 55%
where the time goes in v1:
time: 598 us; the launch traced here: 594 us
  Pallas kernels  327 us (55%)
  matrix products  70.8 us (12%)
  local copies, waits for them, and re-layouts  58.7 us (10%)
  blocking collectives  57.1 us (10%)
  other arithmetic  38.4 us (6%)
  starting transfers between devices  20.8 us (3%)
  waiting for transfers between devices  16.9 us (3%)
    pallas_call x1, Pallas kernels, scatter_all(): pl.pallas_call(functools.partial(scatter_kernel, axes, plan, n), out_shap...  201 us
    pallas_call x1, Pallas kernels, gather_all(): pl.pallas_call(functools.partial(gather_kernel, axes, plan, n), out_shape...  126 us
    all_to_all x1, blocking collectives, body(): lax.all_to_all(tokens, 'fsdp', split_axis=1, concat_axis=2, tiled=True)  57.1 us
    unnamed x73, local copies, waits for them, and re-layouts  40.6 us
    unnamed x4, other arithmetic  28.6 us
    all_to_all x1, waiting for transfers between devices, body(): lax.all_to_all(grad_seq[None], 'fsdp', split_axis=2, concat_axis=1, tiled...  16.9 us
  transfers between devices with their start and end apart: 3, of which 1 were waited for; matrix products, arithmetic and copies ran while one was open for 15% of the time, Pallas kernels for 55%

profile of v1, /device:TPU:0, one launch (start us, length us, event | category | flops | bytes accessed | tf_op | source)
XLA Modules:
  0.0 593.9 jit_solution(3250701948069868013)
XLA Ops:
  0.7 57.1 %all_to_all.42 = bf16[1,16,64,1024]{3,2,0,1:T(8,128)(2,1)S(1)} all-to-all(bf16[1,16,64,1024]{3,2,0,1:T(8,128)(2,1)} %bitcast.136), channel_id=1, replica_groups=mesh['fsdp'=16,'rep'=2] {'fsdp'}, dimensions={1} | all-to-all | bytes 4194304 | tf_op jit(solution)/shard_map/all_to_all | solution.py:583
  57.8 4.6 all-to-all-start.2
  63.0 1.3 fusion.66
  66.2 126.3 %gather_all.1 = (bf16[16,64,3072]{2,1,0:T(8,128)(2,1)}, bf16[16,64,1024]{2,1,0:T(8,128)(2,1)}, bf16[16,64,4096]{2,1,0:T(8,128)(2,1)}, bf16[16,256,1024]{2,1,0:T(8,128)(2,1)}, bf16[16,16,128]{2,1,0:T(8,128)(2,1)}) custom-call(bf16[64,3072]{1,0:T(8,128)(2,1)} %refs_0_.1, bf16[64,1024]{1,0:T(8,128)(2,1)} %refs_1_.1, bf16[64,4096]{1,0:T(8,128)(2,1)} %refs_2_.1, ...), custom_call_target="tpu_custom_call" | custom-call | tf_op jit(solution)/shard_map/gather_all/pallas_call | solution.py:257
  192.5 0.8 slice_bitcast_fusion
  197.3 3.8 fusion.1
  201.6 0.8 copy.69
  202.6 1.5 fusion.77
  204.1 1.8 convolution_convert_fusion.7
  205.9 1.3 multiply_reduce_fusion.6
  207.2 2.1 fusion.30
  209.3 4.9 fusion.75
  214.2 7.2 %fusion.8 = bf16[128,4096]{1,0:T(8,128)(2,1)S(1)} fusion(f32[128,4096]{1,0:T(8,128)S(1)} %fusion.75, bf16[4096,1024]{1,0:T(8,128)(2,1)} %bitcast.162, f32[128,1024]{1,0:T(8,128)S(1)} %fusion.30, f32[128]{0:T(128)S(1)} %convolution_bitcast_fusion), kind=kOutput, calls=%fused_computation.15 | convolution fusion | flops 1084489728 | bytes 12059136 | tf_op jit(solution)/shard_map/scd,fd->scf/dot_general | solution.py:654
  221.5 3.0 multiply_reduce_fusion.1
  224.6 2.7 multiply_reduce_fusion.5
  228.0 1.5 convolution_convert_fusion.6
  229.6 1.8 copy.75
  231.4 1.8 multiply_reduce_fusion
  234.2 1.0 fusion.13
  235.1 1.2 fusion.14
  236.3 2.6 convolution_convert_fusion.5
  238.9 5.4 multiply_reduce_fusion.2
  244.4 4.3 fusion.9
  248.6 5.2 copy.90
  254.3 14.5 %reduce.35 = bf16[1024,1024]{1,0:T(8,128)(2,1)} reduce(bf16[1024,1,1,1024]{3,2,1,0:T(2,128)(2,1)} %bitcast.123, bf16[]{:T(256)} %broadcast.353), dimensions={1,2}, to_apply=%bitcast.113.reduce_sub_computation | reduce | bytes 4194306
  268.8 4.5 reshape.707
  273.3 5.4 all-to-all-start.3
  278.7 2.7 select_bitcast_fusion
  281.3 5.2 copy.91
  286.5 14.1 %reduce.34 = bf16[1024,1024]{1,0:T(8,128)(2,1)} reduce(bf16[1024,1,1,1024]{3,2,1,0:T(2,128)(2,1)} %bitcast.124, bf16[]{:T(256)} %broadcast.353), dimensions={1,2}, to_apply=%bitcast.114.reduce_sub_computation | reduce | bytes 4194306
  300.6 4.5 reshape.705
  305.1 16.9 %all-to-all-done.3 = bf16[16,2,32768]{2,1,0:T(2,128)(2,1)} async-done(((bf16[16,2,32768]{2,1,0:T(2,128)(2,1)}), bf16[16,2,32768]{2,1,0:T(2,128)(2,1)}, u32[]{:S(2)}, u32[]{:S(2)}) %all-to-all-start.3) | async-done | bytes 2097184 | tf_op jit(solution)/shard_map/all_to_all | solution.py:739
  321.9 10.9 %all-to-all-start.1 = ((bf16[16,2,32768]{2,1,0:T(2,128)(2,1)}), bf16[16,2,32768]{2,1,0:T(2,128)(2,1)}, u32[]{:S(2)}, u32[]{:S(2)}) async-start(bf16[16,2,32768]{2,1,0:T(2,128)(2,1)} %reshape.705), calls=%async_computation.1 | async-start | bytes 4194304 | tf_op jit(solution)/shard_map/all_to_all | solution.py:738
  332.9 1.0 copy.80
  334.0 2.4 fusion.67
  337.1 3.0 convolution_convert_fusion.4
  340.1 4.6 convolution_convert_fusion.2
  344.7 5.7 convolution_convert_fusion.1
  350.3 5.6 convolution_convert_fusion
  356.0 200.9 %scatter_all.1 = (bf16[64,3072]{1,0:T(8,128)(2,1)}, bf16[64,1024]{1,0:T(8,128)(2,1)}, bf16[64,4096]{1,0:T(8,128)(2,1)}, bf16[256,1024]{1,0:T(8,128)(2,1)}, f32[8,128]{1,0:T(8,128)}) custom-call(bf16[16,64,3072]{2,1,0:T(8,128)(2,1)} %bitcast.121, bf16[16,64,1024]{2,1,0:T(8,128)(2,1)} %bitcast.127, bf16[16,64,4096]{2,1,0:T(8,128)(2,1)} %bitcast.120, ...), custom_call_target="tpu_custom_call" | custom-call | tf_op jit(solution)/shard_map/scatter_all/pallas_call | solution.py:510
  556.8 2.1 convert_element_type.165
  559.0 2.1 convert_element_type.166
  561.1 0.9 convert_element_type.163
  562.8 1.3 slice_bitcast_fusion.1
  564.1 10.4 %reshape.708 = bf16[1024,1,1,1024]{3,2,1,0:T(2,128)(2,1)} reshape(bf16[16,2,32768]{2,1,0:T(2,128)(2,1)} %all-to-all-done.3) | data formatting | bytes 4194304
  574.5 4.3 copy.87
  578.9 10.4 %reshape.706 = bf16[1024,1,1,1024]{3,2,1,0:T(2,128)(2,1)} reshape(bf16[16,2,32768]{2,1,0:T(2,128)(2,1)} %all-to-all-done.1) | data formatting | bytes 4194304
  589.3 4.3 copy.86
  (101 shorter events, 8.2 us)
Async XLA Ops:
  0.6 61.8 %copy-start = (s32[1,16]{1,0:T(1,128)S(1)}, s32[1,16]{1,0:T(1,128)}, u32[]{:S(2)}) copy-start(s32[1,16]{1,0:T(1,128)} %param.23) | copy-start | bytes 196
  57.8 138.9 %copy-start.4 = (bf16[1,16,64,1024]{3,2,0,1:T(8,128)(2,1)}, bf16[1,16,64,1024]{3,2,0,1:T(8,128)(2,1)S(1)}, u32[]{:S(2)}) copy-start(bf16[1,16,64,1024]{3,2,0,1:T(8,128)(2,1)S(1)} %all_to_all.42) | copy-start | bytes 6291460
  57.8 5.2 copy-start.28
  57.8 7.8 %copy-start.25 = (bf16[64]{0:T(256)(128)(2,1)S(1)}, bf16[64]{0:T(256)(128)(2,1)}, u32[]{:S(2)}) copy-start(bf16[64]{0:T(256)(128)(2,1)} %param.20) | copy-start | bytes 388
  57.8 7.8 %copy-start.26 = (bf16[64]{0:T(256)(128)(2,1)S(1)}, bf16[64]{0:T(256)(128)(2,1)}, u32[]{:S(2)}) copy-start(bf16[64]{0:T(256)(128)(2,1)} %param.19) | copy-start | bytes 388
  57.8 7.8 %copy-start.27 = (bf16[64]{0:T(256)(128)(2,1)S(1)}, bf16[64]{0:T(256)(128)(2,1)}, u32[]{:S(2)}) copy-start(bf16[64]{0:T(256)(128)(2,1)} %param.18) | copy-start | bytes 388
  57.8 138.5 %copy-start.24 = (s32[1,16,128]{2,1,0:T(8,128)S(1)}, s32[1,16,128]{2,1,0:T(8,128)}, u32[]{:S(2)}) copy-start(s32[1,16,128]{2,1,0:T(8,128)} %param.22) | copy-start | bytes 24580
  57.8 149.4 %all-to-all-start.2 = ((bf16[1,16,64,1024]{3,2,0,1:T(8,128)(2,1)}), bf16[1,16,64,1024]{3,2,0,1:T(8,128)(2,1)}, u32[]{:S(2)}, u32[]{:S(2)}) async-start(bf16[1,16,64,1024]{3,2,0,1:T(8,128)(2,1)} %bitcast.137), calls=%async_computation.2 | async-start | bytes 4194304 | tf_op jit(solution)/shard_map/all_to_all | solution.py:584
  201.4 4.5 copy-start.14
  201.6 4.3 copy-start.16
  204.1 1.8 copy-start.2
  209.3 15.3 %copy-start.7 = (f32[128,1024]{1,0:T(8,128)}, f32[128,1024]{1,0:T(8,128)S(1)}, u32[]{:S(2)}) copy-start(f32[128,1024]{1,0:T(8,128)S(1)} %fusion.30) | copy-start | bytes 1572868
  209.3 12.2 %slice-start = ((s8[8388608]{0:T(1024)(128)(4,1)}), s8[4194304]{0:T(1024)(128)(4,1)S(1)}, s32[]{:S(2)}) async-start(s8[8388608]{0:T(1024)(128)(4,1)} %bitcast.117), calls=%async_computation.4 | async-start | bytes 8388608
  209.3 15.3 %slice-start.2 = ((s8[8388608]{0:T(1024)(128)(4,1)}), s8[4194304]{0:T(1024)(128)(4,1)S(1)}, s32[]{:S(2)}) async-start(s8[8388608]{0:T(1024)(128)(4,1)} %bitcast.163), calls=%async_computation.6 | async-start | bytes 8388608
  214.2 7.3 %slice-start.1 = ((s8[8388608]{0:T(1024)(128)(4,1)}), s8[4194304]{0:T(1024)(128)(4,1)S(1)}, s32[]{:S(2)}) async-start(s8[8388608]{0:T(1024)(128)(4,1)} %bitcast.117), calls=%async_computation.5 | async-start | bytes 8388608
  214.2 10.3 %slice-start.3 = ((s8[8388608]{0:T(1024)(128)(4,1)}), s8[4194304]{0:T(1024)(128)(4,1)S(1)}, s32[]{:S(2)}) async-start(s8[8388608]{0:T(1024)(128)(4,1)} %bitcast.163), calls=%async_computation.7 | async-start | bytes 8388608
  221.5 3.0 copy-start.5
  221.5 3.1 copy-start.20
  224.5 2.8 copy-start.18
  224.6 3.5 copy-start.3
  227.3 0.7 copy-start.10
  231.4 1.9 copy-start.11
  233.2 1.0 copy-start.17
  233.2 1.9 copy-start.15
  238.9 5.4 copy-start.8
  238.9 5.5 copy-start.19
  273.3 48.6 %all-to-all-start.3 = ((bf16[16,2,32768]{2,1,0:T(2,128)(2,1)}), bf16[16,2,32768]{2,1,0:T(2,128)(2,1)}, u32[]{:S(2)}, u32[]{:S(2)}) async-start(bf16[16,2,32768]{2,1,0:T(2,128)(2,1)} %reshape.707), calls=%async_computation.3 | async-start | bytes 4194304 | tf_op jit(solution)/shard_map/all_to_all | solution.py:739
  321.9 256.9 %all-to-all-start.1 = ((bf16[16,2,32768]{2,1,0:T(2,128)(2,1)}), bf16[16,2,32768]{2,1,0:T(2,128)(2,1)}, u32[]{:S(2)}, u32[]{:S(2)}) async-start(bf16[16,2,32768]{2,1,0:T(2,128)(2,1)} %reshape.705), calls=%async_computation.1 | async-start | bytes 4194304 | tf_op jit(solution)/shard_map/all_to_all | solution.py:738
  333.9 6.1 %copy-start.12 = (bf16[16,64,128]{2,1,0:T(8,128)(2,1)S(1)}, bf16[16,64,128]{2,1,0:T(8,128)(2,1)}, u32[]{:S(2)}) copy-start(bf16[16,64,128]{2,1,0:T(8,128)(2,1)} %fusion.13) | copy-start | bytes 786436
  333.9 6.1 %copy-start.13 = (bf16[16,64,128]{2,1,0:T(8,128)(2,1)S(1)}, bf16[16,64,128]{2,1,0:T(8,128)(2,1)}, u32[]{:S(2)}) copy-start(bf16[16,64,128]{2,1,0:T(8,128)(2,1)} %fusion.14) | copy-start | bytes 786436
  334.0 6.1 %copy-start.22 = (bf16[16,64,128]{2,1,0:T(8,128)(2,1)S(1)}, bf16[16,64,128]{2,1,0:T(8,128)(2,1)}, u32[]{:S(2)}) copy-start(bf16[16,64,128]{2,1,0:T(8,128)(2,1)} %convolution_convert_fusion.5) | copy-start | bytes 786436
  340.1 4.6 copy-start.6
  344.7 5.7 copy-start.9
  556.8 4.3 copy-start.21
  556.8 5.2 copy-start.23
  589.3 4.3 copy-start.1

commit v2 on v1

--- a/solution.py
+++ b/solution.py
@@ -68,44 +68,57 @@
     ]
 
 
-def neighbours(axes, me):
-    found = []
-    for stride, size in axes:
-        at = (me // stride) % size
-        if size == 2:
-            found.append((None, (1 - 2 * at) * stride))
-        elif size > 2:
-            found.append((at < size - 1, stride))
-            found.append((at > 0, -stride))
-    return found
-
-
-def guarded(cond, fn):
-    if cond is None:
-        fn()
-    else:
-        pl.when(cond)(fn)
-
-
-def enter(axes, me, core):
+def enter(n, me, core):
     barrier = pltpu.get_barrier_semaphore()
-    total = 1
-    for cond, step in neighbours(axes, me):
-        def hello(step=step):
-            pl.semaphore_signal(barrier, inc=1, device_id=(me + step, core), device_id_type=MESH)
-        guarded(cond, hello)
-        total = total + (1 if cond is None else cond.astype(jnp.int32))
+
+    def hello(i, _):
+        pl.semaphore_signal(barrier, inc=1, device_id=((me + i) % n, core), device_id_type=MESH)
+        return 0
+
+    lax.fori_loop(1, n, hello, 0)
     pl.semaphore_signal(barrier, inc=1, device_id=(me, 1 - core), device_id_type=MESH)
-    pl.semaphore_wait(barrier, total)
+    pl.semaphore_wait(barrier, n)
+
+
+def rows_out(n, me, core, rows, landing, send_sem, recv_sem, own_sem):
+    own = pltpu.make_async_copy(rows.at[me], landing.at[me], own_sem)
+    own.start()
+
+    def go(i, _):
+        to = (me + i) % n
+        pltpu.make_async_remote_copy(
+            src_ref=rows.at[to], dst_ref=landing.at[me], send_sem=send_sem, recv_sem=recv_sem,
+            device_id=(to, core), device_id_type=MESH,
+        ).start()
+        return 0
+
+    lax.fori_loop(1, n, go, 0)
+    return own
+
+
+def rows_wait(n, me, core, rows, landing, send_sem, recv_sem, own):
+    own.wait()
+    for which in range(2):
+        copy = pltpu.make_async_remote_copy(
+            src_ref=rows.at[pl.ds(0, n - 1)], dst_ref=landing.at[pl.ds(0, n - 1)],
+            send_sem=send_sem, recv_sem=recv_sem, device_id=(me, 1 - core), device_id_type=MESH,
+        )
+        copy.wait_recv() if which else copy.wait_send()
 
 
 def gather_kernel(axes, plan, n, *refs):
     k = 5
-    ins, outs = refs[:k], refs[k : 2 * k]
-    stages = refs[2 * k : 3 * k]
-    send_sem, recv_sem, pair_send, pair_recv, local_sem = refs[3 * k :]
+    ins, rows, flag = refs[:k], refs[k], refs[k + 1]
+    outs, landing, other = refs[k + 2 : 2 * k + 2], refs[2 * k + 2], refs[2 * k + 3]
+    stages = refs[2 * k + 4 : 3 * k + 4]
+    send_sem, recv_sem, pair_send, pair_recv, local_sem, row_sems = refs[3 * k + 4 :]
     me, core = lax.axis_index("fsdp"), lax.axis_index("rep")
-    enter(axes, me, core)
+    enter(n, me, core)
+    told = pltpu.make_async_remote_copy(
+        src_ref=flag, dst_ref=other, send_sem=row_sems.at[3], recv_sem=row_sems.at[4],
+        device_id=(me, 1 - core), device_id_type=MESH,
+    )
+    told.start()
     numbered, number = [], 0
     for order, pieces in plan:
         numbered.append((order, [(number + i, p) for i, p in enumerate(pieces)]))
@@ -164,6 +177,7 @@
     for order, pieces in numbered:
         for phase in range(3):
             along(pieces, order, me, True, phase, (0, 1))
+    own = rows_out(n, me, core, rows, landing, row_sems.at[0], row_sems.at[1], row_sems.at[2])
     local = []
     for j in range(k):
         local.append(pltpu.make_async_copy(ins[j], stages[j], local_sem.at[j]))
@@ -216,6 +230,8 @@
             settle()
     for copy in local:
         copy.wait()
+    told.wait()
+    rows_wait(n, me, core, rows, landing, row_sems.at[0], row_sems.at[1], own)
 
     def drain(i, piece, count, send, recv, which):
         many = outs[piece.array].at[pl.ds(0, count), :, piece.cols(core)]
@@ -251,25 +267,23 @@
                 drain(i, piece, n - 1, pair_send.at[i], pair_recv.at[i], "recv")
 
 
-def gather_all(axes, n, arrays, collective_id):
+def gather_all(axes, n, arrays, rows, flag, collective_id):
     plan = colours(axes, [a.shape[1] for a in arrays])
     pieces = sum(len(p) for _, p in plan)
+    vmem = pl.BlockSpec(memory_space=pltpu.VMEM)
+    anywhere = pl.BlockSpec(memory_space=ANY)
+    dma = pltpu.SemaphoreType.DMA
     return pl.pallas_call(
         functools.partial(gather_kernel, axes, plan, n),
-        out_shape=[jax.ShapeDtypeStruct((n,) + a.shape, a.dtype) for a in arrays],
-        in_specs=[pl.BlockSpec(memory_space=ANY)] * len(arrays),
-        out_specs=[pl.BlockSpec(memory_space=ANY)] * len(arrays),
+        out_shape=[jax.ShapeDtypeStruct((n,) + a.shape, a.dtype) for a in arrays]
+        + [jax.ShapeDtypeStruct(a.shape, a.dtype) for a in (rows, flag)],
+        in_specs=[anywhere] * len(arrays) + [vmem, vmem],
+        out_specs=[anywhere] * (len(arrays) + 1) + [vmem],
         scratch_shapes=[pltpu.VMEM(a.shape, a.dtype) for a in arrays]
-        + [
-            pltpu.SemaphoreType.DMA((pieces, 3, 2)),
-            pltpu.SemaphoreType.DMA((pieces, n)),
-            pltpu.SemaphoreType.DMA((pieces,)),
-            pltpu.SemaphoreType.DMA((pieces,)),
-            pltpu.SemaphoreType.DMA((len(arrays),)),
-        ],
+        + [dma((pieces, 3, 2)), dma((pieces, n)), dma((pieces,)), dma((pieces,)), dma((len(arrays),)), dma((5,))],
         compiler_params=pltpu.CompilerParams(collective_id=collective_id, has_side_effects=True),
         name="gather_all",
-    )(*arrays)
+    )(*arrays, rows, flag)
 def add_into(acc, a, got, g, rows):
     step = min(rows, 16)
 
@@ -281,20 +295,28 @@
     lax.fori_loop(0, rows // step, go, 0)
 
 
+def turn(at, t, size):
+    if size == 2:
+        return at + (1 - 2 * at) * (1 - t)
+    up = size - 1 - at
+    first_up = jnp.where(t < up, size - 1 - t, t - up)
+    first_down = jnp.where(t < at, t, size - 1 - (t - at))
+    return jnp.where(t == size - 1, at, jnp.where(2 * at < size, first_up, first_down))
+
+
 def slots(size):
     return 1 if size <= 2 else size + 1
 
 
 def scatter_kernel(axes, plan, n, *refs):
     k = 5
-    ins, outs = refs[:k], refs[k : 2 * k]
+    ins, rows, outs, landing = refs[:k], refs[k], refs[k + 1 : 2 * k + 1], refs[2 * k + 1]
     total = sum(len(p) for _, p in plan)
-    buffers = refs[2 * k : 2 * k + 5 * total]
-    own_sem, pair_send, pair_recv, send_sem, recv_sems, last_send, last_recv = (
-        refs[-9], refs[-8], refs[-7], refs[-6], refs[-5:-2], refs[-2], refs[-1]
-    )
+    buffers = refs[2 * k + 2 : 2 * k + 2 + 5 * total]
+    own_sem, pair_send, pair_recv, send_sem = refs[-10:-6]
+    recv_sems, last_send, last_recv, row_sems = refs[-6:-3], refs[-3], refs[-2], refs[-1]
     me, core = lax.axis_index("fsdp"), lax.axis_index("rep")
-    enter(axes, me, core)
+    enter(n, me, core)
     numbered, number = [], 0
     for order, pieces in plan:
         numbered.append((order, [(number + i, p) for i, p in enumerate(pieces)]))
@@ -321,20 +343,11 @@
             ins[piece.array].at[block, :, piece.cols(core)], acc[i].at[block], own_sem.at[i, block]
         )
 
-    def block_at(order, phase, origin, rest):
-        stride = order[phase][0]
-        block = me + (origin - spot(order[phase])) * stride
-        for s, z in order[:phase]:
-            here = (me // s) % z
-            block = block + (xor(here, z - 1 - rest % z, z) - here) * s
-            rest = rest // z
+    def block_at(order, phase, origin, turns):
+        block = me + (origin - spot(order[phase])) * order[phase][0]
+        for axis, t in zip(order[:phase], turns):
+            block = block + (turn(spot(axis), t, axis[1]) - spot(axis)) * axis[0]
         return block
-
-    def rests(order, phase):
-        count = 1
-        for _, z in order[:phase]:
-            count *= z
-        return count
 
     def ready(pieces, block):
         for i, piece in pieces:
@@ -361,25 +374,27 @@
         for i, piece in pieces:
             hop(i, phase, block, rest, slot, send_sem.at[i, phase], device).start()
 
-    def event(order, pieces, phase, e, first):
+    def event(order, pieces, phase, t, turns, first):
         stride, size = order[phase]
-        rest_count = rests(order, phase)
         at = spot(order[phase])
-        far, rest = size - 1 - e // rest_count, e % rest_count
-        origin = xor(at, far, size)
-        block = block_at(order, phase, origin, rest)
+        origin = turn(at, t, size)
+        mine = t == size - 1
+        block = block_at(order, phase, origin, turns)
+        rest = 0
+        for axis, away in zip(order[:phase], turns):
+            rest = rest * axis[1] + away
         if first:
             ready(pieces, block)
         if size == 1:
             return
         if size == 2:
-            pl.when(far == 1)(
+            pl.when(jnp.logical_not(mine))(
                 lambda: give(pieces, phase, block, rest, 0, (me + (1 - 2 * at) * stride, core))
             )
-            pl.when(far == 0)(lambda: take(pieces, phase, block, rest, 0))
+            pl.when(mine)(lambda: take(pieces, phase, block, rest, 0))
             return
 
-        @pl.when(far > 0)
+        @pl.when(jnp.logical_not(mine))
         def _():
             up = (origin > at).astype(jnp.int32)
             behind = jnp.where(up == 1, at > 0, at < size - 1)
@@ -388,63 +403,76 @@
             landing = jnp.where((up == 0) & (origin == at - 1), size, origin)
             give(pieces, phase, block, rest, landing, (me + step * stride, core))
 
-        @pl.when(far == 0)
+        @pl.when(mine)
         def _():
             pl.when(at > 0)(lambda: take(pieces, phase, block, rest, at))
             pl.when(at < size - 1)(lambda: take(pieces, phase, block, rest, size))
 
-    for stage in range(2):
-        for order, pieces in numbered:
-            last = order[2]
-            count = rests(order, 2)
-
-            def begin(e, _, order=order, pieces=pieces):
-                far, rest = order[2][1] - 1 - e // rests(order, 2), e % rests(order, 2)
-                block = block_at(order, 2, xor(spot(order[2]), far, order[2][1]), rest)
-                for i, piece in pieces:
-                    pair_copy(i, piece, block).start()
-                    own_copy(i, piece, block).start()
-                return 0
-
-            lead = (last[1] - 1) * count
-            lax.fori_loop(0 if stage == 0 else lead, lead if stage == 0 else n, begin, 0)
-
-    tasks = []
-    for number, (order, pieces) in enumerate(numbered):
-        lead = (order[2][1] - 1) * rests(order, 2)
-        later = rests(order, 2)
-        inner = rests(order, 1)
-        tasks.append((number, order, pieces, lead, later, inner))
-
-    def lead_event(order, pieces, e):
-        event(order, pieces, 2, e, True)
-
-    def later_event(order, pieces, e, lead, later, inner):
-        event(order, pieces, 2, lead + e, True)
-        event(order, pieces, 1, e, False)
-        pl.when(e >= later - inner)(lambda: event(order, pieces, 0, e - (later - inner), False))
-
-    def loop(count, fns):
-        def go(e, _):
-            for size, fn in fns:
-                if size == count:
-                    fn(e)
-                else:
-                    pl.when(e < size)(lambda fn=fn: fn(e))
-            return 0
-
-        lax.fori_loop(0, count, go, 0)
-
-    light, heavy = tasks[:2], tasks[2:]
-    loop(max(t[3] for t in heavy), [(t[3], functools.partial(lead_event, t[1], t[2])) for t in heavy])
-    both = [(t[3], functools.partial(lead_event, t[1], t[2])) for t in light] + [
-        (t[4], functools.partial(lambda e, t: later_event(t[1], t[2], e, *t[3:]), t=t)) for t in heavy
-    ]
-    loop(max(b[0] for b in both), both)
-    loop(
-        max(t[4] for t in light),
-        [(t[4], functools.partial(lambda e, t: later_event(t[1], t[2], e, *t[3:]), t=t)) for t in light],
-    )
+    def each(count, fn):
+        lax.fori_loop(0, count, lambda e, _: (fn(e), 0)[1], 0)
+
+    def begin(order, pieces, s):
+        _, (_, nq), (_, nr) = order
+
+        def go(e):
+            block = block_at(order, 2, turn(spot(order[2]), e // nq, nr), (s, e % nq))
+            for i, piece in pieces:
+                pair_copy(i, piece, block).start()
+                own_copy(i, piece, block).start()
+
+        each(nr * nq, go)
+
+    def lead(order, pieces, s):
+        _, (_, nq), (_, nr) = order
+        each((nr - 1) * nq, lambda e: event(order, pieces, 2, e // nq, (s, e % nq), True))
+
+    def later(order, pieces, s, low, high):
+        def go(e):
+            event(order, pieces, 2, order[2][1] - 1, (s, low + e), True)
+            event(order, pieces, 1, low + e, (s,), False)
+
+        each(high - low, go)
+
+    def finish(order, pieces, s):
+        event(order, pieces, 0, s, (), False)
+
+    light, heavy = numbered[:2], numbered[2:]
+    steps, few = heavy[0][0][0][1], max(c[0][0][1] for c in light)
+
+    def begin_all(s):
+        for colour in heavy:
+            pl.when(s < steps)(lambda colour=colour: begin(*colour, s))
+        for colour in light:
+            pl.when(s < colour[0][0][1])(lambda colour=colour: begin(*colour, s))
+
+    each(max(steps, few), begin_all)
+    own = rows_out(n, me, core, rows, landing, row_sems.at[0], row_sems.at[1], row_sems.at[2])
+    for colour in heavy + light:
+        lead(*colour, 0)
+
+    def step(s):
+        for colour in heavy:
+            pl.when(s < steps)(lambda colour=colour: later(*colour, s, 0, 1))
+        for colour in heavy:
+            pl.when(s + 1 < steps)(lambda colour=colour: lead(*colour, s + 1))
+        for colour in heavy:
+            pl.when((s >= 1) & (s < steps))(lambda colour=colour: finish(*colour, s - 1))
+        for colour in light:
+            size = colour[0][0][1]
+            pl.when(s + 1 < size)(lambda colour=colour: lead(*colour, s + 1))
+        for colour in heavy:
+            pl.when(s < steps)(lambda colour=colour: later(*colour, s, 1, colour[0][1][1]))
+        for colour in light:
+            size = colour[0][0][1]
+
+            @pl.when((s >= 1) & (s <= size))
+            def _(colour=colour):
+                later(*colour, s - 1, 0, colour[0][1][1])
+                finish(*colour, s - 1)
+        for colour in heavy:
+            pl.when(s == steps - 1)(lambda colour=colour: finish(*colour, s))
+
+    each(max(steps, few + 1), step)
 
     final = []
     for order, pieces in numbered:
@@ -464,6 +492,7 @@
                 final[-1].start()
     for copy in final:
         copy.wait()
+    rows_wait(n, me, core, rows, landing, row_sems.at[0], row_sems.at[1], own)
 
     def drain(i, phase, count):
         many = acc[i].at[pl.ds(0, count)]
@@ -476,7 +505,10 @@
         for i, piece in pieces:
             for phase in range(3):
                 if order[phase][1] > 1:
-                    drain(i, phase, (order[phase][1] - 1) * rests(order, phase))
+                    count = order[phase][1] - 1
+                    for axis in order[:phase]:
+                        count *= axis[1]
+                    drain(i, phase, count)
             many = acc[i].at[pl.ds(0, n)]
             pltpu.make_async_remote_copy(
                 src_ref=many, dst_ref=many, send_sem=pair_send.at[i], recv_sem=last_recv.at[i],
@@ -484,17 +516,17 @@
             ).wait_send()
 
 
-def scatter_all(axes, n, arrays, collective_id):
+def scatter_all(axes, n, arrays, rows, collective_id):
     plan = colours(axes, [a.shape[2] for a in arrays])
     pieces = [(order, p) for order, ps in plan for p in ps]
     scratch = []
     for order, p in pieces:
-        rows, dtype = arrays[p.array].shape[1], arrays[p.array].dtype
-        scratch += [pltpu.VMEM((n, rows, p.width), dtype)] * 2
+        deep, dtype = arrays[p.array].shape[1], arrays[p.array].dtype
+        scratch += [pltpu.VMEM((n, deep, p.width), dtype)] * 2
         count = 1
         for phase in range(3):
             size = order[phase][1]
-            scratch.append(pltpu.VMEM((count, slots(size), rows, p.width), dtype))
+            scratch.append(pltpu.VMEM((count, slots(size), deep, p.width), dtype))
             count *= size
     total = len(pieces)
     shapes = []
@@ -509,18 +541,19 @@
     dma = pltpu.SemaphoreType.DMA
     return pl.pallas_call(
         functools.partial(scatter_kernel, axes, plan, n),
-        out_shape=[jax.ShapeDtypeStruct(a.shape[1:], a.dtype) for a in arrays],
-        in_specs=[pl.BlockSpec(memory_space=ANY)] * len(arrays),
-        out_specs=[pl.BlockSpec(memory_space=pltpu.VMEM)] * len(arrays),
+        out_shape=[jax.ShapeDtypeStruct(a.shape[1:], a.dtype) for a in arrays]
+        + [jax.ShapeDtypeStruct(rows.shape, rows.dtype)],
+        in_specs=[pl.BlockSpec(memory_space=ANY)] * len(arrays) + [pl.BlockSpec(memory_space=pltpu.VMEM)],
+        out_specs=[pl.BlockSpec(memory_space=pltpu.VMEM)] * len(arrays) + [pl.BlockSpec(memory_space=ANY)],
         scratch_shapes=scratch
         + [dma((total, n)), dma((total,)), dma((total, n)), dma((total, 3))]
         + [dma(s) for s in shapes]
-        + [dma((total,)), dma((total,))],
+        + [dma((total,)), dma((total,)), dma((3,))],
         compiler_params=pltpu.CompilerParams(
             collective_id=collective_id, has_side_effects=True, vmem_limit_bytes=60 * 1024 * 1024
         ),
         name="scatter_all",
-    )(*arrays)
+    )(*arrays, rows)
 
 
 import math
@@ -532,6 +565,7 @@
 HEAD_DIM = 64
 SEQ_MAX = 1024
 CAP = 128
+PAST = 1 << 24
 
 
 EPSILON = 1e-06
@@ -572,39 +606,72 @@
     dealing,
 ):
     factor = 1.0 / math.sqrt(HEAD_DIM)
-    group_seqs = tokens.shape[1]
-    per_device = group_seqs // lax.axis_size("fsdp")
-    first_seq = lax.axis_index("fsdp") * per_device
-    my_ids = lax.dynamic_slice_in_dim(dealing[0], first_seq, per_device)
-    picker = my_ids[:, None] == jnp.arange(group_seqs, dtype=jnp.int32)[None, :]
-    seq_lengths = jnp.sum(jnp.where(picker, lengths[0][None, :], 0), axis=1)
-    seq_routes = jnp.sum(jnp.where(picker[:, :, None], routed[0][None, :, :], 0), axis=1)
-    whole_tokens, whole_cot = (
-        lax.all_to_all(tokens, "fsdp", split_axis=1, concat_axis=2, tiled=True),
-        lax.all_to_all(cotangent, "fsdp", split_axis=1, concat_axis=2, tiled=True),
-    )
-    sequence_tokens = whole_tokens[0]
-    sequence_cotangent = whole_cot[0]
-    positions = jnp.arange(SEQ_MAX, dtype=jnp.int32)
+    shards, place = lax.axis_size("fsdp"), lax.axis_index("fsdp")
+    group_seqs, width = tokens.shape[1], tokens.shape[2]
+    cap = min(24, width)
     slot_ids = jnp.arange(CAP, dtype=jnp.int32)
+    picker = dealing[0][:, None] == jnp.arange(group_seqs, dtype=jnp.int32)[None, :]
+    row_lengths = jnp.sum(jnp.where(picker, lengths[0][None, :], 0), axis=1)
+    row_routes = jnp.sum(jnp.where(picker[:, :, None], routed[0][None, :, :], 0), axis=1)
+    row_routes = jnp.where(slot_ids[None, :] < (row_lengths // 8)[:, None], row_routes, PAST)
+    here = place * width + jnp.arange(width, dtype=jnp.int32)
+    below = jnp.sum((row_routes[:, :, None] < here[None, None, :]).astype(jnp.int32), axis=1)
+    upto = jnp.sum((row_routes[:, :, None] <= here[None, None, :]).astype(jnp.int32), axis=1)
+    touched = upto > below
+    living = here[None, :] < row_lengths[:, None]
+    rank = jnp.where(touched, below - below[:, :1], -1)
+    select = (rank[:, None, :] == jnp.arange(cap, dtype=jnp.int32)[None, :, None]).astype(jnp.bfloat16)
+    shard_of = row_routes // width
+    crowd = jnp.sum(
+        (shard_of[:, :, None] == jnp.arange(shards, dtype=jnp.int32)[None, None, :]).astype(jnp.int32), axis=1
+    )
+    flag = jnp.broadcast_to((jnp.max(crowd) > cap).astype(jnp.float32), (8, 128))
+    packed_rows = jnp.concatenate(
+        [
+            jnp.einsum("jip,jpd->jid", select, t[0], preferred_element_type=jnp.float32).astype(jnp.bfloat16)
+            for t in (tokens, cotangent)
+        ],
+        axis=1,
+    )
+    seq_lengths = lax.dynamic_slice_in_dim(row_lengths, place, 1)
+    routes = lax.dynamic_slice_in_dim(row_routes, place, 1)[0]
     valid_slot = slot_ids[None, :] < (seq_lengths // 8)[:, None]
-    selected_slots = (seq_routes[:, :, None] == positions[None, None, :]) & valid_slot[:, :, None]
-    one_hot_matrix = selected_slots.astype(jnp.bfloat16)
-    touched = jnp.any(selected_slots, axis=1)
-    living = positions[None, :] < seq_lengths[:, None]
-    incoming_rows = jnp.einsum(
-        "puf,pfy->puy", one_hot_matrix, sequence_tokens, preferred_element_type=jnp.float32
-    )
-    row_gradient = jnp.einsum(
-        "puf,pfy->puy", one_hot_matrix, sequence_cotangent, preferred_element_type=jnp.float32
-    )
-    shards = lax.axis_size("fsdp")
+    seq_shard = routes // width
+    seq_rank = slot_ids - jnp.sum((routes[None, :] < (seq_shard * width)[:, None]).astype(jnp.int32), axis=1)
+    fits = valid_slot[0] & (seq_rank < cap)
+    landing = jnp.where(fits, seq_shard * (2 * cap) + seq_rank, -1)
+    cells = jnp.arange(shards * 2 * cap, dtype=jnp.int32)
+    pick = jnp.concatenate([landing[:, None] == cells[None, :], (landing[:, None] == (cells - cap)[None, :]) & fits[:, None]])
+    pick = pick.astype(jnp.bfloat16)
     part = w_router.shape[0]
     vectors = jnp.pad(jnp.stack([w_router, gain_attn, gain_mlp]), ((0, 13), (0, 128 - part)))
-    blocks = gather_all(axes, shards, [w_qkv, w_out, w_up, w_down, vectors], 0)
+    blocks = gather_all(axes, shards, [w_qkv, w_out, w_up, w_down, vectors], packed_rows, flag, 0)
+    crowded = jnp.maximum(flag, blocks[6])[0, 0] > 0
+    got_rows = jnp.einsum(
+        "cs,sd->cd", pick, blocks[5].reshape(-1, D), preferred_element_type=jnp.float32
+    ).astype(jnp.bfloat16)
+
+    def all_rows(got):
+        positions = jnp.arange(SEQ_MAX, dtype=jnp.int32)
+        onehot = (routes[:, None] == positions[None, :]).astype(jnp.bfloat16)
+        return jnp.concatenate(
+            [
+                jnp.dot(
+                    onehot,
+                    lax.all_to_all(t, "fsdp", split_axis=1, concat_axis=2, tiled=True)[0, 0],
+                    preferred_element_type=jnp.float32,
+                ).astype(jnp.bfloat16)
+                for t in (tokens, cotangent)
+            ]
+        )
+
+    if cap < width:
+        got_rows = lax.cond(crowded, all_rows, lambda got: got, got_rows)
+    rows_low = got_rows[None, :CAP]
+    incoming_rows = rows_low.astype(jnp.float32)
+    row_gradient = got_rows[None, CAP:].astype(jnp.float32)
     small = blocks[4][:, :3, :part].transpose(1, 0, 2).reshape(3, D)
     gathered = tuple(b.reshape(-1, b.shape[2]) for b in blocks[:4]) + (small[0], small[1], small[2])
-    rows_low = incoming_rows.astype(jnp.bfloat16)
     router_val = jnp.einsum("scd,d->sc", rows_low, gathered[4], preferred_element_type=jnp.float32)
     normed_attn, inverse_attn = normalize(incoming_rows, gathered[5].astype(jnp.float32))
     normed_low = normed_attn.astype(jnp.bfloat16)
@@ -641,11 +708,6 @@
     )
     combined = branch_attn + branch_mlp
     refreshed_rows = (incoming_rows + router_val[..., None] * combined).astype(jnp.bfloat16)
-    scattered = jnp.einsum(
-        "jyv,jyi->jvi", one_hot_matrix, refreshed_rows, preferred_element_type=jnp.float32
-    ).astype(jnp.bfloat16)
-    output_seq = jnp.where(touched[..., None], scattered, sequence_tokens)
-    output_seq = jnp.where(living[..., None], output_seq, jnp.zeros_like(output_seq))
     back_weights = gathered
     grad_comb = router_val[..., None] * row_gradient
     grad_router_val = jnp.sum(row_gradient * combined, axis=-1)
@@ -717,14 +779,12 @@
     grad_routerw = jnp.einsum(
         "scd,sc->d", incoming_rows, grad_router_val, precision=EXACT_PRECISION
     )
-    spread_back = jnp.einsum(
-        "jyv,jyi->jvi",
-        selected_slots.astype(jnp.float32),
-        total_gradient,
-        precision=EXACT_PRECISION,
-    )
-    grad_seq = jnp.where(touched[..., None], spread_back, sequence_cotangent.astype(jnp.float32))
-    grad_seq = jnp.where(living[..., None], grad_seq, jnp.zeros_like(grad_seq)).astype(jnp.bfloat16)
+    new_rows = jnp.concatenate([refreshed_rows[0], total_gradient[0].astype(jnp.bfloat16)])
+    sent_rows = (
+        jnp.einsum("cs,cd->sd", pick, new_rows, preferred_element_type=jnp.float32)
+        .astype(jnp.bfloat16)
+        .reshape(shards, 2 * cap, D)
+    )
     small_grads = jnp.stack([grad_routerw, grad_gain_first, grad_gain_second])
     small_grads = small_grads.reshape(3, shards, part).transpose(1, 0, 2)
     small_grads = jnp.pad(small_grads, ((0, 0), (0, 5), (0, 128 - part)))
@@ -732,12 +792,33 @@
         g.astype(jnp.bfloat16).reshape(shards, -1, g.shape[1])
         for g in (grad_qkvw, grad_outw, grad_upw, grad_downw)
     ]
-    shares = scatter_all(axes, shards, partial + [small_grads], 1)
+    shares = scatter_all(axes, shards, partial + [small_grads], sent_rows, 1)
     totals = tuple(t.astype(jnp.float32) for t in shares[:4]) + tuple(shares[4][j, :part] for j in range(3))
-    back_out, back_grad = (
-        lax.all_to_all(output_seq[None], "fsdp", split_axis=2, concat_axis=1, tiled=True),
-        lax.all_to_all(grad_seq[None], "fsdp", split_axis=2, concat_axis=1, tiled=True),
-    )
+    def place_rows(rows, held):
+        spread = jnp.einsum("jip,jid->jpd", select, rows, preferred_element_type=jnp.float32).astype(jnp.bfloat16)
+        kept = jnp.where(touched[..., None], spread, held[0])
+        return jnp.where(living[..., None], kept, jnp.zeros_like(kept))[None]
+
+    def compact(landed, rows):
+        return place_rows(landed[:, :cap], tokens), place_rows(landed[:, cap:], cotangent)
+
+    def entire(landed, rows):
+        positions = jnp.arange(SEQ_MAX, dtype=jnp.int32)
+        onehot = (routes[:, None] == positions[None, :]).astype(jnp.bfloat16)
+        placed = []
+        for r, held in ((rows[:CAP], tokens), (rows[CAP:], cotangent)):
+            spread = jnp.einsum("cp,cd->pd", onehot, r, preferred_element_type=jnp.float32)
+            spread = lax.all_to_all(
+                spread.astype(jnp.bfloat16)[None, None], "fsdp", split_axis=2, concat_axis=1, tiled=True
+            )
+            kept = jnp.where(touched[..., None], spread[0], held[0])
+            placed.append(jnp.where(living[..., None], kept, jnp.zeros_like(kept))[None])
+        return tuple(placed)
+
+    if cap < width:
+        back_out, back_grad = lax.cond(crowded, entire, compact, shares[5], new_rows)
+    else:
+        back_out, back_grad = compact(shares[5], new_rows)
     return (
         back_out,
         back_grad,

time: 598 us -> 402 us (0.67)
  blocking collectives: 57.1 us -> 0 us
  Pallas kernels: 327 us -> 279 us
  local copies, waits for them, and re-layouts: 58.7 us -> 14.6 us
  other arithmetic: 38.4 us -> 15 us
  starting transfers between devices: 20.8 us -> 0 us
  waiting for transfers between devices: 16.9 us -> 0 us
  matrix products: 70.8 us -> 82.6 us
    all_to_all x1 -> x0, blocking collectives: 57.1 us -> none  [body(): lax.all_to_all(tokens, 'fsdp', split_axis=1, concat_axis=2, tiled=True)]
    pallas_call x1, Pallas kernels: 201 us -> 149 us  [scatter_all(): pl.pallas_call(functools.partial(scatter_kernel, axes, plan, n), out_shap...]
    unnamed x73 -> x56, local copies, waits for them, and re-layouts: 40.6 us -> 2.23 us
    unnamed x4 -> x0, other arithmetic: 28.6 us -> none
    all_to_all x3 -> x0, starting transfers between devices: 20.8 us -> none  [the longest x1 10.9 us: body(): lax.all_to_all(output_seq[None], 'fsdp', split_axis=2, concat_axis=1, til...]
    all_to_all x3 -> x0, waiting for transfers between devices: 16.9 us -> none  [the longest x1 16.9 us: body(): lax.all_to_all(grad_seq[None], 'fsdp', split_axis=2, concat_axis=1, tiled...]
    broadcast_in_dim x2 -> x1, local copies, waits for them, and re-layouts: 10.3 us -> 0.6 us  [body(): jnp.broadcast_to((jnp.max(crowd) > cap).astype(jnp.float32), (8, 128))]
  transfers between devices with their start and end apart: 3 -> 0, of which waited for: 1 -> 0; matrix products, arithmetic and copies ran while one was open for 15% -> 0% of each run, Pallas kernels for 55% -> 0%
where the time goes in v2:
time: 402 us; the launch traced here: 397 us
  Pallas kernels  279 us (69%)
  matrix products  82.6 us (21%)
  other arithmetic  15 us (4%)
  local copies, waits for them, and re-layouts  14.6 us (4%)
  between operations  5.25 us (1%)
    pallas_call x1, Pallas kernels, scatter_all(): pl.pallas_call(functools.partial(scatter_kernel, axes, plan, n), out_shap...  149 us
    pallas_call x1, Pallas kernels, gather_all(): pl.pallas_call(functools.partial(gather_kernel, axes, plan, n), out_shape...  130 us

profile of v2, /device:TPU:0, one launch (start us, length us, event | category | flops | bytes accessed | tf_op | source)
XLA Modules:
  0.0 396.6 jit_solution(5920956309130828302)
XLA Ops:
  0.7 1.0 select_reduce_fusion.1
  4.9 0.7 iota_compare_fusion.14
  5.6 0.8 select_reduce_fusion
  7.0 0.7 convert_reduce_fusion
  7.8 2.0 fusion.24
  10.3 1.3 pad_maximum_fusion.1.refs_5_
  11.9 0.6 reduce_max.18
  14.4 129.6 %gather_all.1 = (bf16[16,64,3072]{2,1,0:T(8,128)(2,1)}, bf16[16,64,1024]{2,1,0:T(8,128)(2,1)}, bf16[16,64,4096]{2,1,0:T(8,128)(2,1)}, bf16[16,256,1024]{2,1,0:T(...) custom-call(bf16[64,3072]{1,0:T(8,128)(2,1)} %refs_0_.1, ...), custom_call_target="tpu_custom_call" | custom-call | tf_op jit(solution)/shard_map/gather_all/pallas_call | solution.py:276
  144.1 2.0 convolution_convert_fusion.8
  147.6 0.8 slice_bitcast_fusion
  148.5 3.8 fusion.11
  152.3 0.8 fusion.96
  153.3 1.2 copy.73
  154.6 1.5 fusion.97
  156.1 0.8 copy.74
  156.9 1.6 convolution_convert_fusion.11
  158.6 3.0 multiply_reduce_fusion.3
  161.6 4.8 %fusion.94 = f32[128,4096]{1,0:T(8,128)S(1)} fusion(bf16[1024,4096]{1,0:T(8,128)(2,1)} %bitcast.151, f32[128,1024]{1,0:T(8,128)S(1)} %get-tuple-element.110, f32[1024]{0:T(1024)S(1)} %reshape.671, f32[128]{0:T(128)S(1)} %get-tuple-element.130), kind=kOutput, calls=%fused_computation.189 | convolution fusion | flops 1074135040 | bytes 11014656 | tf_op jit(solution)/shard_map/scd,df->scf/dot_general | solution.py:702
  166.4 6.5 %convolution_add_fusion = f32[128,1024]{1,0:T(8,128)} fusion(f32[128,1024]{1,0:T(8,128)S(1)} %copy-done.20, bf16[4096,1024]{1,0:T(8,128)(2,1)} %bitcast.202, f32[128,4096]{1,0:T(8,128)S(1)} %fusion.94), kind=kOutput, calls=%fused_computation.60 | convolution fusion | flops 1078591488 | bytes 11534336 | tf_op jit(solution)/shard_map/scf,fd->scd/dot_general | solution.py:706
  173.2 7.6 %fusion.18 = bf16[128,4096]{1,0:T(8,128)(2,1)S(1)} fusion(f32[128,4096]{1,0:T(8,128)} %copy-done.3, bf16[4096,1024]{1,0:T(8,128)(2,1)} %bitcast.203, f32[128]{0:T(128)S(1)} %convolution_bitcast_fusion, bf16[256,1024]{1,0:T(8,128)(2,1)S(1)} %get-tuple-element.146), kind=kOutput, calls=%fused_computation.35 | convolution fusion | flops 1084620800 | bytes 11796992 | tf_op jit(solution)/shard_map/scd,fd->scf/dot_general | solution.py:716
  180.8 6.8 %multiply_reduce_fusion.1 = (f32[1024]{0:T(1024)S(1)}, f32[128]{0:T(128)S(1)}, f32[128,1024]{1,0:T(8,128)S(1)}) fusion(f32[128,1024]{1,0:T(8,128)S(1)} %get-tuple-element.110, f32[128]{0:T(128)S(1)} %get-tuple-element.130, f32[1024]{0:T(1024)S(1)} %reshape.671, bf16[128,4096]{1,0:T(8,128)(2,1)S(1)} %fusion.18, bf16[1024,4096]{1,0:T(8,128)(2,1)} %bitcast.152), kind=kOutput, calls=%fused_computation.93 | convolution fusion | flops 1074527104 | bytes 10494976 | tf_op jit(solution)/shard_map/scf,df->scd/dot_general | solution.py:724
  187.7 0.8 copy-done.6
  188.7 1.5 convolution_convert_fusion.10
  190.2 1.8 copy.76
  192.0 2.2 multiply_reduce_fusion
  194.5 0.7 copy-done.13
  195.2 1.0 fusion.32
  196.2 1.2 fusion.33
  197.4 2.6 convolution_convert_fusion.9
  199.9 6.2 %fusion.49 = (f32[128]{0:T(128)S(1)}, f32[1024]{0:T(1024)S(1)}, f32[128]{0:T(128)S(1)}, bf16[128,1024]{1,0:T(8,128)(2,1)}, f32[128,1024]{1,0:T(8,128)}) fusion(f32[1024]{0:T(1024)S(1)} %reshape.670, bf16[256,1024]{1,0:T(8,128)(2,1)S(1)} %get-tuple-element.146, f32[128]{0:T(128)S(1)} %get-tuple-element.128, f32[128,1024]{1,0:T(8,128)} %convolution_add_fusion, ...), kind=kOutput, calls=%fused_computation.89 | convolution fusion | flops 809368320 | bytes 8923136 | tf_op jit(solution)/shard_map/sce,de->scd/dot_general | solution.py:772
  206.2 1.6 fusion.40
  208.5 2.7 convolution_convert_fusion.7
  211.2 0.7 slice_bitcast_fusion.4
  211.9 1.8 copy.80
  213.7 1.6 fusion.81
  216.2 7.3 %convolution_convert_fusion.2 = bf16[4096,1024]{1,0:T(8,128)(2,1)} fusion(f32[128]{0:T(128)S(1)} %convolution_bitcast_fusion, bf16[256,1024]{1,0:T(8,128)(2,1)S(1)} %get-tuple-element.146, f32[128,4096]{1,0:T(8,128)} %copy-done.3), kind=kOutput, calls=%fused_computation.22 | convolution fusion | flops 1083047936 | bytes 10748416 | tf_op jit(solution)/shard_map/scf,scd->fd/dot_general | solution.py:719
  223.5 5.7 %convolution_convert_fusion.3 = bf16[1024,4096]{1,0:T(8,128)(2,1)} fusion(bf16[128,4096]{1,0:T(8,128)(2,1)S(1)} %copy-done.8, f32[128,1024]{1,0:T(8,128)S(1)} %get-tuple-element.110, f32[1024]{0:T(1024)S(1)} %reshape.671, f32[128]{0:T(128)S(1)} %get-tuple-element.130), kind=kOutput, calls=%fused_computation.23 | convolution fusion | flops 1078329344 | bytes 9966080 | tf_op jit(solution)/shard_map/scd,scf->df/dot_general | solution.py:727
  229.2 2.0 convolution_convert_fusion.6
  231.2 4.6 %convolution_convert_fusion.4 = bf16[1024,3072]{1,0:T(8,128)(2,1)} fusion(bf16[128,1024]{0,1:T(8,128)(2,1)S(1)} %bitcast.186, bf16[128,1024]{0,1:T(8,128)(2,1)S(1)} %bitcast.173, bf16[128,1024]{0,1:T(8,128)(2,1)S(1)} %bitcast.171, f32[1024]{0:T(1024)S(1)} %reshape.670, f32[128]{0:T(128)S(1)} %get-tuple-element.128, bf16[256,1024]{1,0:T(8,128)(2,1)S(1)} %get-tuple-element.146), kind=kOutput, calls=%fused_computation.24 | convolution fusion | flops 811335680 | bytes 7344640 | tf_op jit(solution)/shard_map/scd,sce->de/dot_general | solution.py:769
  235.8 149.3 %scatter_all.1 = (bf16[64,3072]{1,0:T(8,128)(2,1)}, bf16[64,1024]{1,0:T(8,128)(2,1)}, bf16[64,4096]{1,0:T(8,128)(2,1)}, bf16[256,1024]{1,0:T(8,128)(2,1)}, f32[8...) custom-call(bf16[16,64,3072]{2,1,0:T(8,128)(2,1)} %bitcast.154, bf16[16,64,1024]{2,1,0:T(8,128)(2,1)} %bitcast.163, ...), custom_call_target="tpu_custom_call" | custom-call | tf_op jit(solution)/shard_map/scatter_all/pallas_call | solution.py:542
  385.2 4.0 %conditional.3 = (bf16[1,16,64,1024]{3,2,1,0:T(8,128)(2,1)}, bf16[1,16,64,1024]{3,2,1,0:T(8,128)(2,1)}) conditional(s32[]{:T(128)} %bitcast.20, (pred[16,64]{1,0:T(8,128)(4,1)S(1)}, pred[16,64]{1,0:T(8,128)(4,1)S(1)}, bf16[16,48,1024]{2,1,0:T(8,128)(2,1)S(1)}, bf16[16,24,64]{2,1,0:T(8,128)(2,1)S(1)}, bf16[1,16,64,1024]{3,2,1,0:T(8,128)(2,1)}, ...), branch_computations={%region_19.20_spmd, %region_20.21_spmd} | conditional | flops 543424512 | bytes 88607880 | solution.py:819
  385.2 2.0 fusion.3
  387.2 2.0 fusion.5
  389.2 2.1 convert_element_type.230
  391.3 2.1 convert_element_type.231
  393.4 0.9 convert_element_type.228
  394.4 0.7 convert_element_type.229
  395.1 1.3 slice_bitcast_fusion.1
  (98 shorter events, 7.0 us)
Async XLA Ops:
  0.6 9.2 %copy-start = (bf16[1,16,64,1024]{3,2,1,0:T(8,128)(2,1)S(1)}, bf16[1,16,64,1024]{3,2,1,0:T(8,128)(2,1)}, u32[]{:S(2)}) copy-start(bf16[1,16,64,1024]{3,2,1,0:T(8,128)(2,1)} %param.17) | copy-start | bytes 6291460
  6.9 137.1 %copy-start.25 = (pred[128,768]{1,0:T(32,128)(4,1)}, pred[128,768]{1,0:T(32,128)(4,1)S(1)}, u32[]{:S(2)}) copy-start(pred[128,768]{1,0:T(32,128)(4,1)S(1)} %get-tuple-element.131) | copy-start | bytes 294916
  6.9 137.1 %copy-start.26 = (pred[128,768]{1,0:T(32,128)(4,1)}, pred[128,768]{1,0:T(32,128)(4,1)S(1)}, u32[]{:S(2)}) copy-start(pred[128,768]{1,0:T(32,128)(4,1)S(1)} %get-tuple-element.132) | copy-start | bytes 294916
  10.3 3.5 copy-start.28
  10.3 3.5 copy-start.29
  10.3 3.5 copy-start.30
  144.0 2.0 copy-start.27
  153.3 5.3 %copy-start.12 = (bf16[1,128,1024]{1,2,0:T(8,128)(2,1)}, bf16[1,128,1024]{1,2,0:T(8,128)(2,1)S(1)}, u32[]{:S(2)}) copy-start(bf16[1,128,1024]{1,2,0:T(8,128)(2,1)S(1)} %copy.72) | copy-start | bytes 786436
  154.5 4.1 %copy-start.14 = (bf16[1,128,1024]{1,2,0:T(8,128)(2,1)}, bf16[1,128,1024]{1,2,0:T(8,128)(2,1)S(1)}, u32[]{:S(2)}) copy-start(bf16[1,128,1024]{1,2,0:T(8,128)(2,1)S(1)} %copy.73) | copy-start | bytes 786436
  158.6 7.8 %copy-start.18 = (bf16[16,64,128]{2,1,0:T(8,128)(2,1)}, bf16[16,64,128]{2,1,0:T(8,128)(2,1)S(1)}, u32[]{:S(2)}) copy-start(bf16[16,64,128]{2,1,0:T(8,128)(2,1)S(1)} %convolution_convert_fusion.11) | copy-start | bytes 786436
  161.6 4.8 %copy-start.20 = (f32[128,1024]{1,0:T(8,128)S(1)}, f32[128,1024]{1,0:T(8,128)}, u32[]{:S(2)}) copy-start(f32[128,1024]{1,0:T(8,128)} %get-tuple-element.135) | copy-start | bytes 1572868
  166.4 6.6 %copy-start.3 = (f32[128,4096]{1,0:T(8,128)}, f32[128,4096]{1,0:T(8,128)S(1)}, u32[]{:S(2)}) copy-start(f32[128,4096]{1,0:T(8,128)S(1)} %fusion.94) | copy-start | bytes 6291460
  180.8 6.8 %copy-start.7 = (bf16[128,4096]{1,0:T(8,128)(2,1)}, bf16[128,4096]{1,0:T(8,128)(2,1)S(1)}, u32[]{:S(2)}) copy-start(bf16[128,4096]{1,0:T(8,128)(2,1)S(1)} %fusion.18) | copy-start | bytes 3145732
  180.8 7.8 %copy-start.4 = (bf16[16,64,1024]{2,1,0:T(8,128)(2,1)S(1)}, bf16[16,64,1024]{2,1,0:T(8,128)(2,1)}, u32[]{:S(2)}) copy-start(bf16[16,64,1024]{2,1,0:T(8,128)(2,1)} %get-tuple-element.80) | copy-start | bytes 6291460
  187.6 0.8 copy-start.6
  192.0 2.3 copy-start.9
  194.3 1.0 copy-start.13
  194.3 1.9 copy-start.15
  206.2 2.3 copy-start.22
  207.8 0.7 copy-start.16
  216.2 7.3 %copy-start.8 = (bf16[128,4096]{1,0:T(8,128)(2,1)S(1)}, bf16[128,4096]{1,0:T(8,128)(2,1)}, u32[]{:S(2)}) copy-start(bf16[128,4096]{1,0:T(8,128)(2,1)} %copy-done.7) | copy-start | bytes 3145732
  223.5 5.7 %copy-start.19 = (bf16[16,64,128]{2,1,0:T(8,128)(2,1)S(1)}, bf16[16,64,128]{2,1,0:T(8,128)(2,1)}, u32[]{:S(2)}) copy-start(bf16[16,64,128]{2,1,0:T(8,128)(2,1)} %copy-done.18) | copy-start | bytes 786436
  229.2 2.0 copy-start.10
  229.2 2.0 copy-start.11
  229.2 2.0 copy-start.23
  235.8 149.4 %copy-start.17 = (bf16[128,1024]{1,0:T(8,128)(2,1)S(1)}, bf16[128,1024]{1,0:T(8,128)(2,1)}, u32[]{:S(2)}) copy-start(bf16[128,1024]{1,0:T(8,128)(2,1)} %copy-done.16) | copy-start | bytes 786436
  385.2 2.0 copy-start.1
  389.2 4.3 %copy-start.21 = (bf16[64,3072]{1,0:T(8,128)(2,1)S(1)}, bf16[64,3072]{1,0:T(8,128)(2,1)}, u32[]{:S(2)}) copy-start(bf16[64,3072]{1,0:T(8,128)(2,1)} %get-tuple-element.86) | copy-start | bytes 1179652
  389.2 5.2 %copy-start.24 = (bf16[64,1024]{1,0:T(8,128)(2,1)S(1)}, bf16[64,1024]{1,0:T(8,128)(2,1)}, u32[]{:S(2)}) copy-start(bf16[64,1024]{1,0:T(8,128)(2,1)} %get-tuple-element.87) | copy-start | bytes 393220

commit v3 on v2

--- a/solution.py
+++ b/solution.py
@@ -1,3 +1,4 @@
+import math
 import functools
 
 import jax
@@ -5,6 +6,18 @@
 from jax import lax
 from jax.experimental import pallas as pl
 from jax.experimental.pallas import tpu as pltpu
+from jax.sharding import PartitionSpec as P
+
+D = 1024
+HEADS = 16
+HEAD_DIM = 64
+SEQ_MAX = 1024
+CAP = 128
+PAST = 1 << 24
+
+
+EPSILON = 1e-06
+EXACT_PRECISION = lax.Precision.HIGHEST
 
 MESH = pl.DeviceIdType.MESH
 ANY = pl.ANY
@@ -556,20 +569,749 @@
     )(*arrays, rows)
 
 
-import math
-
-from jax.sharding import PartitionSpec as P
-
-D = 1024
-HEADS = 16
-HEAD_DIM = 64
-SEQ_MAX = 1024
-CAP = 128
-PAST = 1 << 24
-
-
-EPSILON = 1e-06
-EXACT_PRECISION = lax.Precision.HIGHEST
+SQRT_2_PI = math.sqrt(2.0 / math.pi)
+NN = (((1,), (0,)), ((), ()))
+NT = (((1,), (1,)), ((), ()))
+TN = (((0,), (0,)), ((), ()))
+
+
+def mm(a, b, dims=NN):
+    return lax.dot_general(a, b, dims, preferred_element_type=jnp.float32)
+
+
+def each(count, fn):
+    lax.fori_loop(0, count, lambda e, _: (fn(e), 0)[1], 0)
+
+
+class Part:
+    def __init__(self, array, offset, width):
+        self.array, self.offset, self.width = array, offset, width
+
+    def of(self, ref, block):
+        return ref.at[block, :, pl.ds(self.offset, self.width)]
+
+
+EARLY, AT0, AT1, CUT, SPLIT = 60, 4, 85, 70, False
+
+
+def first_shares(axes, vectors):
+    a, b, c = axes
+    half = D // 2
+    return [
+        ((b, c, a), [Part(1, 0, D // 8), Part(4, 0, vectors)]),
+        ((c, b, a), [Part(0, 0, D // 8)]),
+        ((a, b, c), [Part(0, D // 8, half + 3 * D // 8)]),
+        ((a, c, b), [Part(0, D, half), Part(1, D // 8, 3 * D // 8)]),
+    ]
+
+
+def second_shares(axes):
+    a, b, c = axes
+    return [
+        ((b, c, a), [Part(2, 0, 3 * D // 8)]),
+        ((c, b, a), [Part(3, 0, D // 4)]),
+        ((a, b, c), [Part(2, 3 * D // 8, 13 * D // 8)]),
+        ((a, c, b), [Part(3, D // 4, 3 * D // 4)]),
+    ]
+
+
+def number_parts(plan):
+    numbered, number = [], 0
+    for order, parts in plan:
+        numbered.append((order, [(number + i, p) for i, p in enumerate(parts)]))
+        number += len(parts)
+    return numbered
+
+
+def send(src, dst, send_sem, recv_sem, device):
+    return pltpu.make_async_remote_copy(
+        src_ref=src, dst_ref=dst, send_sem=send_sem, recv_sem=recv_sem, device_id=device, device_id_type=MESH
+    )
+
+
+class Gather:
+    def __init__(self, n, me, core, numbered, whole, sems):
+        self.n, self.me, self.core, self.numbered, self.whole = n, me, core, numbered, whole
+        self.send_sem, self.recv_sem = sems
+
+    def spot(self, axis):
+        return (self.me // axis[0]) % axis[1]
+
+    def put(self, parts, block, phase, way, step):
+        for i, part in parts:
+            dst = part.of(self.whole[part.array], block)
+            send(
+                dst, dst, self.send_sem.at[i, phase, way], self.recv_sem.at[i, block], (self.me + step, self.core)
+            ).start()
+
+    def along(self, parts, order, block, phase, ways):
+        stride, size = order[phase]
+        at = self.spot(order[phase])
+        if size == 2:
+            self.put(parts, block, phase, 0, (1 - 2 * at) * stride)
+        elif size > 2:
+            for way in ways:
+                step = (1 - 2 * way) * stride
+                pl.when(at < size - 1 if way == 0 else at > 0)(
+                    functools.partial(self.put, parts, block, phase, way, step)
+                )
+
+    def arrived(self, parts, order, block, phase, way):
+        for i, part in parts:
+            dst = part.of(self.whole[part.array], block)
+            send(
+                dst, dst, self.send_sem.at[i, phase, way], self.recv_sem.at[i, block], (self.me, 1 - self.core)
+            ).wait_recv()
+        if order[phase][1] > 2:
+            self.along(parts, order, block, phase, (way,))
+        for later in range(phase + 1, 3):
+            self.along(parts, order, block, later, (0, 1))
+
+    def start(self):
+        for order, parts in self.numbered:
+            for phase in range(3):
+                self.along(parts, order, self.me, phase, (0, 1))
+
+    def events(self):
+        found = []
+        for number, (order, parts) in enumerate(self.numbered):
+            heavy = number >= 2
+            sizes = [a[1] for a in order]
+            for phase in range(3):
+                size, rest = sizes[phase], math.prod(sizes[:phase])
+                for t in range(1, size):
+                    for way in (0,) if size == 2 else (0, 1):
+                        for j in range(rest):
+                            if heavy:
+                                key = 20 * t if phase == 0 else 20 * phase + 20 * (j + (t - 1) * rest + 1)
+                            else:
+                                key = 5 if phase == 0 else 10 + 5 * j if phase == 1 else 15 + 40 * t + 5 * j
+                            found.append((key, len(found), order, parts, phase, t, way, j))
+        found.sort(key=lambda e: e[:2])
+        return [functools.partial(self.run, *e[2:]) for e in found]
+
+    def run(self, order, parts, phase, t, way, j):
+        stride, size = order[phase]
+        at = self.spot(order[phase])
+        origin = 1 - at if size == 2 else at - (1 - 2 * way) * t
+        block = self.me + (origin - at) * stride
+        for s, z in order[:phase]:
+            here = (self.me // s) % z
+            block = block + (xor(here, j % z, z) - here) * s
+            j = j // z
+        if size == 2:
+            self.arrived(parts, order, block, phase, 0)
+        else:
+            pl.when((origin >= 0) & (origin < size))(
+                functools.partial(self.arrived, parts, order, block, phase, way)
+            )
+
+    def drain(self):
+        for order, parts in self.numbered:
+            rest = 1
+            for phase in range(3):
+                size = order[phase][1]
+                at = self.spot(order[phase])
+                for i, part in parts:
+                    def gone(count, way, i=i, part=part, phase=phase):
+                        many = part.of(self.whole[part.array], pl.ds(0, count))
+                        send(
+                            many, many, self.send_sem.at[i, phase, way], self.recv_sem.at[i, 0], (self.me, 1 - self.core)
+                        ).wait_send()
+
+                    if size == 2:
+                        gone(rest, 0)
+                    elif size > 2:
+                        for here in range(size):
+                            def both(here=here, gone=gone, rest=rest, size=size):
+                                if here < size - 1:
+                                    gone((here + 1) * rest, 0)
+                                if here > 0:
+                                    gone((size - here) * rest, 1)
+                            pl.when(at == here)(both)
+                rest *= size
+
+
+class Scatter:
+    def __init__(self, me, core, numbered, acc, got, sems):
+        self.me, self.core, self.numbered, self.acc, self.got = me, core, numbered, acc, got
+        self.send_sem, self.recv_sems, self.drain_sem = sems
+
+    def spot(self, axis):
+        return (self.me // axis[0]) % axis[1]
+
+    def block_at(self, order, phase, origin, turns):
+        block = self.me + (origin - self.spot(order[phase])) * order[phase][0]
+        for axis, t in zip(order[:phase], turns):
+            block = block + (turn(self.spot(axis), t, axis[1]) - self.spot(axis)) * axis[0]
+        return block
+
+    def hop(self, i, part, phase, block, rest, slot, device):
+        return send(
+            part.of(self.acc[part.array], block),
+            self.got[i][phase].at[rest, slot],
+            self.send_sem.at[i, phase],
+            self.recv_sems[phase].at[i, rest * self.got[i][phase].shape[1] + slot],
+            device,
+        )
+
+    def take(self, parts, phase, block, rest, slot):
+        for i, part in parts:
+            self.hop(i, part, phase, block, rest, slot, (self.me, 1 - self.core)).wait_recv()
+            acc, got = self.acc[part.array], self.got[i][phase]
+            rows = acc.shape[1]
+            step = min(rows, 16)
+            cols = pl.ds(part.offset, part.width)
+
+            def go(e, acc=acc, got=got, step=step, cols=cols):
+                at = pl.ds(pl.multiple_of(e * step, step), step)
+                acc[block, at, cols] = acc[block, at, cols] + got[rest, slot, at, :]
+
+            each(rows // step, go)
+
+    def give(self, parts, phase, block, rest, slot, step):
+        for i, part in parts:
+            self.hop(i, part, phase, block, rest, slot, (self.me + step, self.core)).start()
+
+    def event(self, order, parts, phase, t, turns):
+        stride, size = order[phase]
+        at = self.spot(order[phase])
+        origin = turn(at, t, size)
+        mine = t == size - 1
+        block = self.block_at(order, phase, origin, turns)
+        rest = 0
+        for axis, away in zip(order[:phase], turns):
+            rest = rest * axis[1] + away
+        if size == 1:
+            return
+        if size == 2:
+            pl.when(jnp.logical_not(mine))(
+                lambda: self.give(parts, phase, block, rest, 0, (1 - 2 * at) * stride)
+            )
+            pl.when(mine)(lambda: self.take(parts, phase, block, rest, 0))
+            return
+
+        @pl.when(jnp.logical_not(mine))
+        def _():
+            up = (origin > at).astype(jnp.int32)
+            behind = jnp.where(up == 1, at > 0, at < size - 1)
+            pl.when(behind)(lambda: self.take(parts, phase, block, rest, origin))
+            landing = jnp.where((up == 0) & (origin == at - 1), size, origin)
+            self.give(parts, phase, block, rest, landing, (2 * up - 1) * stride)
+
+        @pl.when(mine)
+        def _():
+            pl.when(at > 0)(lambda: self.take(parts, phase, block, rest, at))
+            pl.when(at < size - 1)(lambda: self.take(parts, phase, block, rest, size))
+
+    def lead(self, order, parts, s):
+        _, (_, nq), (_, nr) = order
+        each((nr - 1) * nq, lambda e: self.event(order, parts, 2, e // nq, (s, e % nq)))
+
+    def later(self, order, parts, s, low, high):
+        def go(e):
+            self.event(order, parts, 2, order[2][1] - 1, (s, low + e))
+            self.event(order, parts, 1, low + e, (s,))
+
+        each(high - low, go)
+
+    def finish(self, order, parts, s):
+        self.event(order, parts, 0, s, ())
+
+    def stages(self):
+        light, heavy = self.numbered[:2], self.numbered[2:]
+        steps, few = heavy[0][0][0][1], max(c[0][0][1] for c in light)
+        found = [functools.partial(self.lead, *colour, 0) for colour in heavy + light]
+        for s in range(max(steps, few + 1)):
+            if s < steps:
+                found += [functools.partial(self.later, *colour, s, 0, 1) for colour in heavy]
+            if s + 1 < steps:
+                found += [functools.partial(self.lead, *colour, s + 1) for colour in heavy]
+            if 1 <= s < steps:
+                found += [functools.partial(self.finish, *colour, s - 1) for colour in heavy]
+            found += [functools.partial(self.lead, *c, s + 1) for c in light if s + 1 < c[0][0][1]]
+            if s < steps:
+                found += [functools.partial(self.later, *c, s, 1, c[0][1][1]) for c in heavy]
+            for c in light:
+                if 1 <= s <= c[0][0][1]:
+                    found += [
+                        functools.partial(self.later, *c, s - 1, e, e + 1) for e in range(c[0][1][1])
+                    ]
+                    found.append(functools.partial(self.finish, *c, s - 1))
+            if s == steps - 1:
+                found += [functools.partial(self.finish, *colour, s) for colour in heavy]
+        return found
+
+    def drain(self):
+        for order, parts in self.numbered:
+            for i, part in parts:
+                for phase in range(3):
+                    if order[phase][1] > 1:
+                        count = (order[phase][1] - 1) * math.prod([a[1] for a in order[:phase]])
+                        many = part.of(self.acc[part.array], pl.ds(0, count))
+                        send(
+                            many, many, self.send_sem.at[i, phase], self.drain_sem, (self.me, 1 - self.core)
+                        ).wait_send()
+
+
+class Refs:
+    pass
+
+
+def block_kernel(axes, n, cap, *refs):
+    names = (
+        "wq", "wo", "wu", "wd", "vec", "rows_in", "pick", "extra", "notes", "gq", "go", "gu", "gd", "gs",
+        "landed", "new", "Wq", "Wo", "Wu", "Wd", "V", "Wo2", "Aq", "Ao", "Au", "Ad", "As", "As2", "land",
+        "rows_out", "X", "DY", "N1", "QKV", "PROBS", "ATT", "PART", "SENT", "GOT1", "GOT2", "GOT3", "GOT4",
+        "BA", "N2", "ACT", "GM", "GU", "M1", "GA", "GATT", "GQKV", "GR", "NOTE", "FQ", "FO", "FU", "FD",
+    )
+    r = Refs()
+    for name, ref in zip(names, refs):
+        setattr(r, name, ref)
+    got_refs, sems = refs[len(names) : -8], refs[-8:]
+    g_send, g_recv, g_local, s_send, s_recv0, s_recv1, s_recv2, misc = sems
+    R = D // n
+    me, core = lax.axis_index("fsdp"), lax.axis_index("rep")
+    half = D // 2
+    pair = (me, 1 - core)
+    units = r.wd.shape[0] // 2
+    blocks = [r.Wq, r.Wo, r.Wu, r.Wd, r.V]
+
+    def stage(src, dst, k):
+        pltpu.make_async_copy(src, dst, g_local.at[k]).start()
+
+    def column(f, size, start):
+        return pl.ds(pl.multiple_of(f * size + start, 128), size)
+
+    for k in range(3):
+        stage(r.wq.at[:, pl.ds(pl.multiple_of(k * D + core * half, 128), half)], r.Wq.at[me, :, pl.ds(k * half, half)], 0)
+    stage(r.wo.at[:, column(core, half, 0)], r.Wo.at[me], 1)
+    each(
+        n, lambda f: stage(r.wu.at[:, column(2 * f + core, units, 0)], r.Wu.at[me, :, column(f, units, 0)], 2)
+    )
+    stage(r.wd.at[pl.ds(pl.multiple_of(core * units, 16), units)], r.Wd.at[me], 3)
+    stage(r.vec, r.V.at[me], 4)
+    enter(n, me, core)
+    for k, whole in enumerate(blocks):
+        pltpu.make_async_copy(whole.at[me], whole.at[me], g_local.at[k]).wait()
+    counter = [0]
+
+    def to_pair(src, dst):
+        k = counter[0]
+        counter[0] += 2
+        copy = send(src, dst, misc.at[k], misc.at[k + 1], pair)
+        copy.start()
+        return copy
+
+    numbered = number_parts(first_shares(axes, 128) + second_shares(axes))
+    g_sems = (g_send, g_recv)
+    gathers = [Gather(n, me, core, part, blocks, g_sems) for part in (numbered[:4], numbered[4:])]
+    gathers[0].start()
+    row_sems = [misc.at[40 + k] for k in range(6)]
+    own_rows = rows_out(n, me, core, r.rows_in, r.land, *row_sems[:3])
+    note = to_pair(r.notes, r.NOTE)
+    events = gathers[0].events()
+    early = len(events) * EARLY // 100
+    for event in events[:early]:
+        event()
+    gathers[1].start()
+    for event in events[early:]:
+        event()
+    mine, theirs = pl.ds(0, CAP), pl.ds(CAP, CAP)
+    STEP = 64
+    TILE = 256
+    flying = Refs()
+
+    def cols(e, size=TILE):
+        return pl.ds(pl.multiple_of(e * size, size), size)
+
+    def flat(ref, at):
+        return ref[:, :, at].reshape(-1, at.size)
+
+    def vector(v):
+        per = 128 // R
+        tiles = []
+        for t in range(D // 128):
+            total = r.V[t * per].astype(jnp.float32)[v : v + 1, :]
+            for j in range(1, per):
+                total = total + r.V[t * per + j].astype(jnp.float32)[v : v + 1, :]
+            tiles.append(total)
+        return jnp.concatenate(tiles, axis=1)
+
+    w_router, gain1, gain2 = vector(0), vector(1), vector(2)
+
+    def inverse(v):
+        return lax.rsqrt(jnp.mean(v * v, axis=1, keepdims=True) + EPSILON)
+
+    def rows_here():
+        rows_wait(n, me, core, r.rows_in, r.land, row_sems[0], row_sems[1], own_rows)
+        flying.out_half = to_pair(r.Wo.at[pl.ds((1 - core) * (n // 2), n // 2)], r.Wo2)
+
+    def extract(k, ref):
+        def go(e):
+            at = pl.ds(k * CAP, CAP)
+            ref[:CAP, cols(e)] = (
+                mm(r.pick[at, :], r.land[:, :, cols(e)].reshape(-1, TILE)) + r.extra[at, cols(e)].astype(jnp.float32)
+            ).astype(jnp.bfloat16)
+
+        each(D // TILE, go)
+
+    def swap_rows():
+        flying.both = [to_pair(ref.at[mine], ref.at[theirs]) for ref in (r.X, r.DY)] + [note]
+
+    def first(e):
+        at = pl.ds(pl.multiple_of(e * STEP, STEP), STEP)
+        x = r.X[at, :].astype(jnp.float32)
+        r.N1[at, :] = (x * inverse(x) * gain1).astype(jnp.bfloat16)
+        router = jnp.sum(x * w_router, axis=1, keepdims=True)
+        r.GM[at, :] = (router * r.DY[at, :].astype(jnp.float32)).astype(jnp.bfloat16)
+
+    def first_rows():
+        for copy in flying.both:
+            copy.wait()
+        each(2 * CAP // STEP, first)
+
+    def project(e):
+        r.QKV[:, cols(e)] = mm(r.N1[...], flat(r.Wq, cols(e))).astype(jnp.bfloat16)
+
+    factor = 1.0 / math.sqrt(HEAD_DIM)
+    pairs = half // 128
+    lane = lax.broadcasted_iota(jnp.int32, (CAP, 128), 1) // HEAD_DIM
+    zero = jnp.zeros((CAP, 128), jnp.bfloat16)
+    causal = lax.broadcasted_iota(jnp.int32, (CAP, CAP), 1) <= lax.broadcasted_iota(jnp.int32, (CAP, CAP), 0)
+
+    def heads(e):
+        s, p = e // pairs, e % pairs
+        rows = pl.ds(pl.multiple_of(s * CAP, CAP), CAP)
+        q, k, v = (r.QKV[rows, cols(p + j * pairs, 128)] for j in range(3))
+        return s, p, rows, q, k, v
+
+    def attend(e):
+        s, p, rows, q, k, v = heads(e)
+        valid = jnp.where(s == 0, r.notes[0:1, :], r.NOTE[0:1, :]) > 0
+        parts = []
+        for h in range(2):
+            score = mm(jnp.where(lane == h, q, zero), k, NT) * factor
+            score = jnp.where(causal & valid, score, -1e30)
+            top = jnp.exp(score - jnp.max(score, axis=1, keepdims=True))
+            probs = top / jnp.sum(top, axis=1, keepdims=True)
+            r.PROBS[2 * e + h] = probs
+            parts.append(mm(probs.astype(jnp.bfloat16), v))
+        r.ATT[rows, cols(p, 128)] = jnp.where(lane == 0, parts[0], parts[1]).astype(jnp.bfloat16)
+
+    near = pl.ds(pl.multiple_of(core * half, half), half)
+    away = pl.ds(pl.multiple_of((1 - core) * half, half), half)
+    own_heads = pl.ds(core * (n // 2), n // 2)
+
+    def wo_near():
+        return r.Wo[own_heads].reshape(half, half)
+
+    def wo_away():
+        return r.Wo2[...].reshape(half, half)
+
+    def project_out(where):
+        if where == 0:
+            r.BA[:, near] = mm(r.ATT[...], wo_near())
+        else:
+            flying.out_half.wait()
+            r.BA[:, away] = mm(r.ATT[...], wo_away())
+
+    def pass_on(part, got):
+        for a, b in ((mine, theirs), (theirs, mine)):
+            r.SENT[a, :] = part[b, :].astype(jnp.bfloat16)
+        flying.gone = to_pair(r.SENT, got)
+
+    def second(e):
+        at = pl.ds(pl.multiple_of(e * STEP, STEP), STEP)
+        branch = r.BA[at, :] + r.GOT1[at, :].astype(jnp.float32)
+        r.BA[at, :] = branch
+        middle = r.X[at, :].astype(jnp.float32) + branch
+        r.N2[at, :] = (middle * inverse(middle) * gain2).astype(jnp.bfloat16)
+
+    def second_rows():
+        flying.gone.wait()
+        each(2 * CAP // STEP, second)
+
+    def some(fn, low, high):
+        return lambda: lax.fori_loop(low, high, lambda e, _: (fn(e), 0)[1], 0)
+
+    def spread(items, chunks, low, high):
+        done = 0
+        for number, item in enumerate(items):
+            item()
+            want = len(chunks) * (number + 1 - low) // max(high - low, 1)
+            while done < min(max(want, 0), len(chunks)):
+                chunks[done]()
+                done += 1
+        for chunk in chunks[done:]:
+            chunk()
+
+    forward = [rows_here, functools.partial(extract, 0, r.X), functools.partial(extract, 1, r.DY), swap_rows, first_rows]
+    forward += [some(project, e, e + 1) for e in range(3 * half // TILE)]
+    forward += [some(attend, e, e + 2) for e in range(0, 2 * pairs, 2)]
+    forward += [
+        functools.partial(project_out, 0), functools.partial(project_out, 1),
+        lambda: pass_on(r.BA, r.GOT1), second_rows,
+    ]
+    events = gathers[1].events()
+    spread(events, forward, len(events) * AT0 // 100, len(events) * AT1 // 100)
+    hidden = r.Wd.shape[1]
+    per = TILE // hidden if hidden < TILE else 1
+
+    def down_rows(e):
+        return pl.ds(e * per, per)
+
+    def hidden_units(e):
+        up = mm(r.N2[...], flat(r.Wu, cols(e)))
+        inner = jnp.tanh(SQRT_2_PI * (up + 0.044715 * up * up * up))
+        act = (0.5 * up * (1.0 + inner)).astype(jnp.bfloat16)
+        slope = 0.5 * (1.0 + inner) + 0.5 * up * (1.0 - inner * inner) * (
+            SQRT_2_PI * (1.0 + 3 * 0.044715 * up * up)
+        )
+        r.ACT[:, cols(e)] = act
+        down = r.Wd[down_rows(e)].reshape(TILE, D)
+        grad_act = mm(r.GM[...], down, NT)
+        r.GU[:, cols(e)] = (slope * grad_act).astype(jnp.bfloat16)
+        r.Ad[down_rows(e)] = mm(act, r.GM[...], TN).astype(jnp.bfloat16).reshape(per, hidden, D)
+
+    tiles = 2 * D // TILE
+    each(tiles, hidden_units)
+
+    def up_grads(e):
+        r.Au[:, :, cols(e)] = mm(r.N2[...], r.GU[:, cols(e)], TN).astype(jnp.bfloat16).reshape(n, R, TILE)
+
+    total = sum(len(p) for _, p in numbered)
+    got = [got_refs[3 * i : 3 * i + 3] for i in range(total)]
+    s_sems = (s_send, (s_recv0, s_recv1, s_recv2), misc.at[46])
+    acc = [r.Aq, r.Ao, r.Au, r.Ad, r.As]
+    late, soon = (Scatter(me, core, part, acc, got, s_sems) for part in (numbered[:4], numbered[4:]))
+    many = TILE // R
+
+    def back_up(e):
+        block = r.Wu[pl.ds(e * many, many)].reshape(TILE, 2 * D)
+        r.PART[:, cols(e)] = mm(r.GU[...], block, NT)
+
+    def mlp(e):
+        r.M1[:, cols(e)] = mm(r.ACT[...], r.Wd[:, :, cols(e)].reshape(2 * D, TILE))
+
+    def mlp_out():
+        flying.gone.wait()
+        r.SENT[mine, :] = r.M1[theirs, :].astype(jnp.bfloat16)
+        flying.gone = to_pair(r.SENT.at[mine], r.GOT3)
+
+    zeros = jnp.zeros((1, D), jnp.float32)
+
+    def third(e, total):
+        at = pl.ds(pl.multiple_of(e * STEP, STEP), STEP)
+        x = r.X[at, :].astype(jnp.float32)
+        dy = r.DY[at, :].astype(jnp.float32)
+        middle = x + r.BA[at, :]
+        inv = inverse(middle)
+        grad = r.PART[at, :] + r.GOT2[at, :].astype(jnp.float32)
+        scaled = gain2 * grad
+        grad_middle = inv * scaled - middle * inv**3 * jnp.mean(scaled * middle, axis=1, keepdims=True)
+        router = jnp.sum(x * w_router, axis=1, keepdims=True)
+        r.GA[at, :] = (router * dy + grad_middle).astype(jnp.bfloat16)
+        r.PART[at, :] = grad_middle
+        counted = jnp.where(e < CAP // STEP, 1.0, 0.0)
+        return total + counted * jnp.sum(grad * middle * inv, axis=0, keepdims=True)
+
+    def third_rows():
+        flying.gain2 = lax.fori_loop(0, 2 * CAP // STEP, third, zeros)
+
+    def out_grads():
+        r.Ao[own_heads] = mm(r.ATT[...], r.GA[:, near], TN).astype(jnp.bfloat16).reshape(n // 2, R, half)
+
+    def attended_grads():
+        r.GATT[...] = (mm(r.GA[:, near], wo_near(), NT) + mm(r.GA[:, away], wo_away(), NT)).astype(jnp.bfloat16)
+
+    def other_out_grads():
+        flying.gone.wait()
+        r.Wo2[...] = mm(r.ATT[...], r.GA[:, away], TN).astype(jnp.bfloat16).reshape(n // 2, R, half)
+        flying.out = to_pair(r.Wo2, r.Ao.at[own_heads])
+
+    def attend_back(e):
+        s, p, rows, q, k, v = heads(e)
+        grad = r.GATT[rows, cols(p, 128)]
+        gq, gk, gv = [], [], []
+        for h in range(2):
+            grad_h, q_h = jnp.where(lane == h, grad, zero), jnp.where(lane == h, q, zero)
+            probs = r.PROBS[2 * e + h]
+            grad_probs = mm(grad_h, v, NT)
+            gv.append(mm(probs.astype(jnp.bfloat16), grad_h, TN))
+            grad_scores = probs * (grad_probs - jnp.sum(probs * grad_probs, axis=1, keepdims=True))
+            grad_scores = grad_scores.astype(jnp.bfloat16)
+            gq.append(mm(grad_scores, k))
+            gk.append(mm(grad_scores, q_h, TN))
+        r.GQKV[rows, cols(p, 128)] = (jnp.where(lane == 0, gq[0], gq[1]) * factor).astype(jnp.bfloat16)
+        r.GQKV[rows, cols(p + pairs, 128)] = ((gk[0] + gk[1]) * factor).astype(jnp.bfloat16)
+        r.GQKV[rows, cols(p + 2 * pairs, 128)] = (gv[0] + gv[1]).astype(jnp.bfloat16)
+
+    def qkv_grads(e):
+        r.Aq[:, :, cols(e)] = mm(r.N1[...], r.GQKV[:, cols(e)], TN).astype(jnp.bfloat16).reshape(n, R, TILE)
+
+    def back_qkv(e):
+        block = r.Wq[pl.ds(e * many, many)].reshape(TILE, 3 * half)
+        r.M1[:, cols(e)] = mm(r.GQKV[...], block, NT)
+
+    def fourth(e, total):
+        at = pl.ds(pl.multiple_of(e * STEP, STEP), STEP)
+        x = r.X[at, :].astype(jnp.float32)
+        dy = r.DY[at, :].astype(jnp.float32)
+        combined = r.BA[at, :] + r.M1[at, :] + r.GOT3[at, :].astype(jnp.float32)
+        router = jnp.sum(x * w_router, axis=1, keepdims=True)
+        r.new[at, :] = (x + router * combined).astype(jnp.bfloat16)
+        grad_router = jnp.sum(dy * combined, axis=1, keepdims=True)
+        r.GR[at, :] = dy + grad_router * w_router + r.PART[at, :]
+        return total + jnp.sum(grad_router * x, axis=0, keepdims=True)
+
+    def fourth_rows():
+        flying.router = lax.fori_loop(0, CAP // STEP, fourth, zeros)
+
+    def last_out():
+        r.SENT[theirs, :] = r.M1[theirs, :].astype(jnp.bfloat16)
+        flying.gone = to_pair(r.SENT.at[theirs], r.GOT4)
+
+    def fifth(e, total):
+        at = pl.ds(pl.multiple_of(e * STEP, STEP), STEP)
+        x = r.X[at, :].astype(jnp.float32)
+        grad = r.M1[at, :] + r.GOT4[at, :].astype(jnp.float32)
+        inv = inverse(x)
+        scaled = gain1 * grad
+        grad_x = inv * scaled - x * inv**3 * jnp.mean(scaled * x, axis=1, keepdims=True)
+        below = pl.ds(pl.multiple_of(CAP + e * STEP, STEP), STEP)
+        r.new[below, :] = (r.GR[at, :] + grad_x).astype(jnp.bfloat16)
+        return total + jnp.sum(grad * x * inv, axis=0, keepdims=True)
+
+    def fifth_rows():
+        flying.gone.wait()
+        gain1_grad = lax.fori_loop(0, CAP // STEP, fifth, zeros)
+        small = jnp.concatenate([flying.router, gain1_grad, flying.gain2, jnp.zeros((5, D), jnp.float32)], axis=0)
+        for block in range(n):
+            tile = block * R // 128
+            r.As[block] = small[:, tile * 128 : tile * 128 + 128]
+        flying.small = to_pair(r.As, r.As2)
+
+    def place(e):
+        sent = mm(r.pick[...], r.new[:, cols(e)], TN).astype(jnp.bfloat16)
+        r.rows_out[:, :, cols(e)] = sent.reshape(n, -1, TILE)
+
+    def send_late():
+        flying.rows = rows_out(n, me, core, r.rows_out, r.landed, *row_sems[3:])
+        flying.small.wait()
+        flying.out.wait()
+        r.As[...] = r.As[...] + r.As2[...]
+
+    backward = [some(up_grads, e, e + 2) for e in range(0, tiles, 2)] if SPLIT else []
+    backward += [some(back_up, e, e + 1) for e in range(D // TILE)]
+    backward += [lambda: pass_on(r.PART, r.GOT2)]
+    backward += [some(mlp, e, e + 1) for e in range(D // TILE)]
+    backward += [mlp_out, third_rows, out_grads, attended_grads, other_out_grads]
+    backward += [some(attend_back, e, e + 1) for e in range(2 * pairs)]
+    backward += [fourth_rows]
+    backward += [some(back_qkv, e, e + 1) for e in range(D // TILE)]
+    backward += [last_out]
+    backward += [some(qkv_grads, e, e + 1) for e in range(3 * half // TILE)]
+    backward += [fifth_rows, some(place, 0, D // TILE), send_late]
+    each(tiles, up_grads)
+    stages = soon.stages()
+    cut = len(stages) * CUT // 100
+    spread(stages[:cut], backward, 1, cut)
+    rest, more = stages[cut:], late.stages()
+    while rest or more:
+        if more:
+            more.pop(0)()
+        if rest:
+            rest.pop(0)()
+    for gather in gathers:
+        gather.drain()
+    final = [to_pair(acc[k].at[me], ref) for k, ref in enumerate((r.FQ, r.FO, r.FU, r.FD))]
+
+    def give(k, side, ref):
+        value = ref[...].astype(jnp.float32)
+        if k == 0:
+            for j in range(3):
+                r.gq[:, pl.ds(pl.multiple_of(j * D + side * half, 128), half)] = value[:, j * half : (j + 1) * half]
+        elif k == 1:
+            r.go[:, column(side, half, 0)] = value
+        elif k == 2:
+            for f in range(n):
+                r.gu[:, column(2 * f + side, units, 0)] = value[:, f * units : (f + 1) * units]
+        else:
+            r.gd[pl.ds(pl.multiple_of(side * units, 8), units), :] = value
+
+    for k in range(4):
+        give(k, core, acc[k].at[me])
+    r.gs[...] = r.As[me]
+    for k, ref in enumerate((r.FQ, r.FO, r.FU, r.FD)):
+        final[k].wait()
+        give(k, 1 - core, ref)
+    rows_wait(n, me, core, r.rows_out, r.landed, row_sems[3], row_sems[4], flying.rows)
+    late.drain()
+    soon.drain()
+
+
+def whole_block(axes, n, cap, weights, vec, rows_in, pick, extra, notes):
+    plan = first_shares(axes, 128) + second_shares(axes)
+    bf, f32 = jnp.bfloat16, jnp.float32
+    shards = weights
+    weights = [
+        jax.ShapeDtypeStruct((w.shape[0] // (2 if k == 3 else 1), w.shape[1] // (1 if k == 3 else 2)), bf)
+        for k, w in enumerate(shards)
+    ]
+    R, F = weights[0].shape[0], weights[3].shape[0]
+    vmem = pl.BlockSpec(memory_space=pltpu.VMEM)
+    anywhere = pl.BlockSpec(memory_space=ANY)
+    out = [jax.ShapeDtypeStruct(w.shape, f32) for w in shards]
+    out += [
+        jax.ShapeDtypeStruct((8, 128), f32),
+        jax.ShapeDtypeStruct(rows_in.shape, bf),
+        jax.ShapeDtypeStruct((2 * CAP, D), bf),
+    ]
+    rows = 2 * CAP
+    half = D // 2
+    V = pltpu.VMEM
+    scratch = [V((n,) + w.shape, bf) for w in weights]
+    scratch += [V((n,) + vec.shape, bf), V((n // 2, R, half), bf)]
+    scratch += [V((n,) + w.shape, bf) for w in weights]
+    scratch += [V((n, 8, 128), f32)] * 2
+    scratch += [V((n, 2 * cap, D), bf), V((n, 2 * cap, D), bf)]
+    scratch += [V((rows, D), bf)] * 3
+    scratch += [V((rows, 3 * half), bf), V((HEADS, CAP, CAP), f32), V((rows, half), bf)]
+    scratch += [V((rows, D), f32), V((rows, D), bf), V((rows, D), bf), V((rows, D), bf), V((CAP, D), bf), V((CAP, D), bf)]
+    scratch += [V((rows, D), f32), V((rows, D), bf)]
+    scratch += [V((rows, 2 * D), bf), V((rows, D), bf), V((rows, 2 * D), bf)]
+    scratch += [V((rows, D), f32), V((rows, D), bf), V((rows, half), bf), V((rows, 3 * half), bf)]
+    scratch += [V((CAP, D), f32), V((8, 128), f32)]
+    scratch += [V(w.shape, bf) for w in weights]
+    most = [1, 1, 1]
+    total = 0
+    deep = [R, R, R, F, 8]
+    for order, parts in plan:
+        total += len(parts)
+        for p in parts:
+            count = 1
+            for phase in range(3):
+                size = order[phase][1]
+                kind = f32 if p.array == 4 else bf
+                scratch.append(V((count, slots(size), deep[p.array], p.width), kind))
+                most[phase] = max(most[phase], count * slots(size))
+                count *= size
+    dma = pltpu.SemaphoreType.DMA
+    scratch += [dma((total, 3, 2)), dma((total, n)), dma((5,)), dma((total, 3))]
+    scratch += [dma((total, m)) for m in most]
+    scratch += [dma((48,))]
+    return pl.pallas_call(
+        functools.partial(block_kernel, axes, n, cap),
+        out_shape=out,
+        in_specs=[anywhere] * 6 + [vmem] * 3,
+        out_specs=[vmem] * 5 + [anywhere, vmem],
+        scratch_shapes=scratch,
+        compiler_params=pltpu.CompilerParams(
+            collective_id=2, has_side_effects=True, vmem_limit_bytes=67043328
+        ),
+        name="whole_block",
+    )(*shards, vec, rows_in, pick, extra, notes)
 
 
 def normalize(values, gain):
@@ -590,7 +1332,7 @@
     return packed[..., offset : offset + D].reshape(packed.shape[:2] + (HEADS, HEAD_DIM))
 
 
-def body(
+def narrow_body(
     axes,
     tokens,
     cotangent,
@@ -832,6 +1574,136 @@
     )
 
 
+def wide_body(
+    axes,
+    tokens,
+    cotangent,
+    w_qkv,
+    w_out,
+    w_up,
+    w_down,
+    w_router,
+    gain_attn,
+    gain_mlp,
+    lengths,
+    routed,
+    dealing,
+):
+    factor = 1.0 / math.sqrt(HEAD_DIM)
+    shards, place = lax.axis_size("fsdp"), lax.axis_index("fsdp")
+    group_seqs, width = tokens.shape[1], tokens.shape[2]
+    cap = min(24, width)
+    slot_ids = jnp.arange(CAP, dtype=jnp.int32)
+    picker = dealing[0][:, None] == jnp.arange(group_seqs, dtype=jnp.int32)[None, :]
+    row_lengths = jnp.sum(jnp.where(picker, lengths[0][None, :], 0), axis=1)
+    row_routes = jnp.sum(jnp.where(picker[:, :, None], routed[0][None, :, :], 0), axis=1)
+    row_routes = jnp.where(slot_ids[None, :] < (row_lengths // 8)[:, None], row_routes, PAST)
+    here = place * width + jnp.arange(width, dtype=jnp.int32)
+    below = jnp.sum((row_routes[:, :, None] < here[None, None, :]).astype(jnp.int32), axis=1)
+    upto = jnp.sum((row_routes[:, :, None] <= here[None, None, :]).astype(jnp.int32), axis=1)
+    touched = upto > below
+    living = here[None, :] < row_lengths[:, None]
+    rank = jnp.where(touched, below - below[:, :1], -1)
+    select = (rank[:, None, :] == jnp.arange(cap, dtype=jnp.int32)[None, :, None]).astype(jnp.bfloat16)
+    shard_of = row_routes // width
+    crowd = jnp.sum(
+        (shard_of[:, :, None] == jnp.arange(shards, dtype=jnp.int32)[None, None, :]).astype(jnp.int32), axis=1
+    )
+    flag = jnp.broadcast_to((jnp.max(crowd) > cap).astype(jnp.float32), (8, 128))
+    packed_rows = jnp.concatenate(
+        [
+            jnp.einsum("jip,jpd->jid", select, t[0], preferred_element_type=jnp.float32).astype(jnp.bfloat16)
+            for t in (tokens, cotangent)
+        ],
+        axis=1,
+    )
+    seq_lengths = lax.dynamic_slice_in_dim(row_lengths, place, 1)
+    routes = lax.dynamic_slice_in_dim(row_routes, place, 1)[0]
+    valid_slot = slot_ids[None, :] < (seq_lengths // 8)[:, None]
+    seq_shard = routes // width
+    seq_rank = slot_ids - jnp.sum((routes[None, :] < (seq_shard * width)[:, None]).astype(jnp.int32), axis=1)
+    fits = valid_slot[0] & (seq_rank < cap)
+    landing = jnp.where(fits, seq_shard * (2 * cap) + seq_rank, -1)
+    cells = jnp.arange(shards * 2 * cap, dtype=jnp.int32)
+    pick = jnp.concatenate([landing[:, None] == cells[None, :], (landing[:, None] == (cells - cap)[None, :]) & fits[:, None]])
+    pick = pick.astype(jnp.bfloat16)
+    part = w_router.shape[0]
+    mine = jnp.max(flag)
+    other = lax.ppermute(flag, "rep", [(0, 1), (1, 0)])
+    crowded = jnp.maximum(mine, jnp.max(other)) > 0
+    positions = jnp.arange(SEQ_MAX, dtype=jnp.int32)
+
+    def all_rows():
+        onehot = (routes[:, None] == positions[None, :]).astype(jnp.bfloat16)
+        return jnp.concatenate(
+            [
+                jnp.dot(
+                    onehot,
+                    lax.all_to_all(t, "fsdp", split_axis=1, concat_axis=2, tiled=True)[0, 0],
+                    preferred_element_type=jnp.float32,
+                ).astype(jnp.bfloat16)
+                for t in (tokens, cotangent)
+            ]
+        )
+
+    extra = jnp.zeros((2 * CAP, D), jnp.bfloat16)
+    if cap < width:
+        extra = lax.cond(crowded, all_rows, lambda: jnp.zeros((2 * CAP, D), jnp.bfloat16))
+        pick = jnp.where(crowded, jnp.zeros_like(pick), pick)
+    weights = [w_qkv, w_out, w_up, w_down]
+    lanes = (place * part) % 128
+    vectors = jnp.pad(jnp.stack([w_router, gain_attn, gain_mlp]), ((0, 13), (0, 0)))
+    vectors = lax.dynamic_update_slice(jnp.zeros((16, 128), jnp.bfloat16), vectors, (0, lanes))
+    notes = jnp.broadcast_to(valid_slot.astype(jnp.float32), (8, CAP))
+    gq, go, gu, gd, gs, landed, new_rows = whole_block(
+        axes, shards, cap, weights, vectors, packed_rows, pick, extra, notes
+    )
+    small = lax.dynamic_slice(gs, (0, lanes), (8, part))
+    totals = (gq, go, gu, gd, small[0], small[1], small[2])
+
+    def place_rows(rows, held):
+        spread = jnp.einsum("jip,jid->jpd", select, rows, preferred_element_type=jnp.float32).astype(jnp.bfloat16)
+        kept = jnp.where(touched[..., None], spread, held[0])
+        return jnp.where(living[..., None], kept, jnp.zeros_like(kept))[None]
+
+    def compact(landed, rows):
+        return place_rows(landed[:, :cap], tokens), place_rows(landed[:, cap:], cotangent)
+
+    def entire(landed, rows):
+        positions = jnp.arange(SEQ_MAX, dtype=jnp.int32)
+        onehot = (routes[:, None] == positions[None, :]).astype(jnp.bfloat16)
+        placed = []
+        for r, held in ((rows[:CAP], tokens), (rows[CAP:], cotangent)):
+            spread = jnp.einsum("cp,cd->pd", onehot, r, preferred_element_type=jnp.float32)
+            spread = lax.all_to_all(
+                spread.astype(jnp.bfloat16)[None, None], "fsdp", split_axis=2, concat_axis=1, tiled=True
+            )
+            kept = jnp.where(touched[..., None], spread[0], held[0])
+            placed.append(jnp.where(living[..., None], kept, jnp.zeros_like(kept))[None])
+        return tuple(placed)
+
+    if cap < width:
+        back_out, back_grad = lax.cond(crowded, entire, compact, landed, new_rows)
+    else:
+        back_out, back_grad = compact(landed, new_rows)
+    return (
+        back_out,
+        back_grad,
+        totals[0],
+        totals[1],
+        totals[2],
+        totals[3],
+        totals[4],
+        totals[5],
+        totals[6],
+    )
+
+
+def body(axes, *arrays):
+    run = wide_body if arrays[2].shape[0] % 16 == 0 else narrow_body
+    return run(axes, *arrays)
+
+
 def solution(mesh):
     placed = (
         P("rep", None, "fsdp", None),

time: 402 us -> 351 us (0.87); the launches traced: 397 us -> 355 us
  matrix products: 82.6 us -> 9.7 us
  Pallas kernels: 279 us -> 322 us
  local copies, waits for them, and re-layouts: 14.6 us -> 8.17 us
  other arithmetic: 15 us -> 9.29 us
    dot_general x23 -> x2, matrix products: 77.2 us -> 2.39 us  [wide_body(): jnp.einsum('jip,jpd->jid', select, t[0], preferred_element_type=jnp.float32)]
    pallas_call x2 -> x1, Pallas kernels: 279 us -> 322 us  [whole_block(): pl.pallas_call(functools.partial(block_kernel, axes, n, cap), out_shape=o...]
    convert_element_type x10 -> x1, other arithmetic: 8.02 us -> 0.66 us  [wide_body(): (rank[:, None, :] == jnp.arange(cap, dtype=jnp.int32)[None, :, None]).ast...]
  transfers between devices with their start and end apart: 0 -> 1, of which waited for: 0 -> 0; matrix products, arithmetic and copies ran while one was open for 0% -> 2% of each run, Pallas kernels for 0% -> 0%
where the time goes in v3:
time: 351 us; the launch traced here: 355 us
  Pallas kernels  322 us (92%)
  matrix products  9.7 us (3%)
  other arithmetic  9.29 us (3%)
  local copies, waits for them, and re-layouts  8.17 us (2%)
  between operations  5 us (1%)
    pallas_call x1, Pallas kernels, whole_block(): pl.pallas_call(functools.partial(block_kernel, axes, n, cap), out_shape=o...  322 us
    dot_general x2, matrix products, place_rows(): jnp.einsum('jip,jid->jpd', select, rows, preferred_element_type=jnp.float32)  7.31 us
  transfers between devices with their start and end apart: 1, of which 0 were waited for; matrix products, arithmetic and copies ran while one was open for 2% of the time, Pallas kernels for 0%

profile of v3, /device:TPU:0, one launch (start us, length us, event | category | flops | bytes accessed | tf_op | source)
XLA Modules:
  0.0 354.8 jit_solution(16348062296689600893)
XLA Ops:
  0.6 0.0 copy-start
  0.7 0.9 iota_compare_fusion.9
  1.5 0.9 select_reduce_fusion.1
  2.4 0.8 select_reduce_fusion
  3.2 0.1 add_select_fusion
  3.3 0.3 convert_reduce_fusion.2
  3.6 0.6 reduce_max.16
  5.0 0.6 collective-permute-start
  5.5 0.6 dynamic_slice.9
  7.4 0.6 broadcast_compare_fusion
  8.1 0.7 convert_reduce_fusion
  10.1 0.2 convert_reduce_fusion.3
  10.3 0.1 slice_reduce_fusion
  10.4 0.6 subtract_select_fusion
  11.0 0.7 fusion.27
  11.6 2.0 fusion.23
  13.6 0.0 copy-done
  13.7 0.4 fusion.20
  14.1 0.0 copy-start.15
  14.1 0.0 copy-start.16
  14.1 0.0 copy-start.17
  14.1 1.3 pad_maximum_fusion.1.refs_5_
  15.4 0.2 iota_compare_fusion.3
  15.6 0.0 copy-done.15
  15.6 0.0 copy-done.16
  15.6 0.0 copy-done.17
  15.6 0.2 dynamic_update_slice.3.refs_4_
  15.8 0.0 copy-start.12
  15.8 0.0 collective-permute-done
  15.8 0.6 reduce_max.20
  17.1 0.8 fusion.26.refs_6_
  17.9 0.0 copy-done.13
  17.9 0.0 copy-done.12
  17.9 0.9 conditional.2
  17.9 0.9 broadcast.243
  18.8 0.6 broadcast_in_dim.153.refs_8_
  19.4 322.0 %whole_block.1 = (f32[64,3072]{1,0:T(8,128)}, f32[64,1024]{1,0:T(8,128)}, f32[64,4096]{1,0:T(8,128)}, f32[256,1024]{1,0:T(8,128)}, f32[8,128]{1,0:T(8,128)}, /*i...) custom-call(bf16[64,3072]{1,0:T(8,128)(2,1)} %refs_0_.1, bf16[64,1024]{1,0:T(8,128)(2,1)} %refs_1_.1, ...), custom_call_target="tpu_custom_call" | custom-call | tf_op jit(solution)/shard_map/whole_block/pallas_call | solution.py:1304
  341.4 0.8 constant_dynamic-slice_fusion.1
  342.1 0.5 slice_bitcast_fusion
  342.7 7.4 %conditional.3 = (bf16[1,16,64,1024]{3,2,1,0:T(8,128)(2,1)}, bf16[1,16,64,1024]{3,2,1,0:T(8,128)(2,1)}) conditional(s32[]{:T(128)} %convert_element_type.63, (pred[16,64]{1,0:T(8,128)(4,1)}, pred[16,64]{1,0:T(8,128)(4,1)}, bf16[16,48,1024]{2,1,0:T(8,128)(2,1)}, bf16[16,24,64]{2,1,0:T(8,128)(2,1)}, bf16[1,16,64,1024]{3,2,1,0:T(8,128)(2,1)}, ...), branch_computations={%region_10.11_spmd, %region_11.12_spmd} | conditional | flops 543424512 | bytes 82326760 | solution.py:1686
  342.7 0.0 copy-start.8
  342.7 4.1 %fusion.9 = bf16[1,16,64,1024]{3,2,1,0:T(8,128)(2,1)} fusion(bf16[1,16,64,1024]{3,2,1,0:T(8,128)(2,1)} %get-tuple-element.43, pred[16,64]{1,0:T(8,128)(4,1)} %get-tuple-element.40, pred[16,64]{1,0:T(8,128)(4,1)} %get-tuple-element.39, bf16[16,24,64]{2,1,0:T(8,128)(2,1)} %get-tuple-element.41, bf16[16,48,1024]{2,1,0:T(8,128)(2,1)} %get-tuple-element.42), kind=kOutput, calls=%fused_computation.14 | convolution fusion | flops 53477376 | bytes 5083136 | tf_op jit(solution)/shard_map/cond/branch_0_fun/jip,jid->jpd/dot_general | solution.py:1665
  346.8 0.0 copy-done.5
  346.8 3.2 fusion.7
  350.0 0.9 copy.50
  350.9 1.7 copy.51
  352.6 1.0 copy.52
  353.6 1.0 copy.53
  (23 shorter events, 0.1 us)
Async XLA Ops:
  0.6 13.0 %copy-start = (bf16[1,16,64,1024]{3,2,1,0:T(8,128)(2,1)S(1)}, bf16[1,16,64,1024]{3,2,1,0:T(8,128)(2,1)}, u32[]{:S(2)}) copy-start(bf16[1,16,64,1024]{3,2,1,0:T(8,128)(2,1)} %param.16) | copy-start | bytes 6291460
  5.0 10.9 %collective-permute-start = (f32[8,128]{1,0:T(8,128)S(1)}, f32[8,128]{1,0:T(8,128)S(1)}, u32[]{:S(2)}, u32[]{:S(2)}) collective-permute-start(f32[8,128]{1,0:T(8,128)S(1)} %broadcast_in_dim.149), channel_id=1, source_target_pairs={{0,1},{1,0},{2,3},{3,2},{4,5},{5,4},{6,7},{7,6},{8,9},{9,8},{10,11... | collective-permute-start | bytes 12296 | tf_op jit(solution)/shard_map/ppermute | solution.py:1632
  8.0 9.9 %copy-start.13 = (s32[1,128]{1,0:T(1,128)}, s32[1,128]{1,0:T(1,128)S(1)}, u32[]{:S(2)}) copy-start(s32[1,128]{1,0:T(1,128)S(1)} %get-tuple-element.94) | copy-start | bytes 1540
  14.1 1.5 copy-start.15
  14.1 1.5 copy-start.16
  14.1 1.5 copy-start.17
  15.8 2.1 copy-start.12
  342.7 7.4 %copy-start.6 = (f32[64,3072]{1,0:T(8,128)S(1)}, f32[64,3072]{1,0:T(8,128)}, u32[]{:S(2)}) copy-start(f32[64,3072]{1,0:T(8,128)} %get-tuple-element.123) | copy-start | bytes 2359300
  342.7 4.1 %copy-start.2 = (bf16[16,48,1024]{2,1,0:T(8,128)(2,1)S(1)}, bf16[16,48,1024]{2,1,0:T(8,128)(2,1)}, u32[]{:S(2)}) copy-start(bf16[16,48,1024]{2,1,0:T(8,128)(2,1)} %get-tuple-element.42) | copy-start | bytes 4718596 | tf_op jit(solution)/shard_map/cond
  342.7 4.1 %copy-start.5 = (bf16[16,24,64]{2,1,0:T(8,128)(2,1)S(1)}, bf16[16,24,64]{2,1,0:T(8,128)(2,1)}, u32[]{:S(2)}) copy-start(bf16[16,24,64]{2,1,0:T(8,128)(2,1)} %get-tuple-element.41) | copy-start | bytes 147460 | tf_op jit(solution)/shard_map/cond
  342.7 4.1 %copy-start.8 = (pred[16,64]{1,0:T(8,128)(4,1)S(1)}, pred[16,64]{1,0:T(8,128)(4,1)}, u32[]{:S(2)}) copy-start(pred[16,64]{1,0:T(8,128)(4,1)} %get-tuple-element.39) | copy-start | bytes 3076 | tf_op jit(solution)/shard_map/cond
  342.7 4.1 %copy-start.10 = (pred[16,64]{1,0:T(8,128)(4,1)S(1)}, pred[16,64]{1,0:T(8,128)(4,1)}, u32[]{:S(2)}) copy-start(pred[16,64]{1,0:T(8,128)(4,1)} %get-tuple-element.40) | copy-start | bytes 3076 | tf_op jit(solution)/shard_map/cond
  350.0 2.6 copy-start.4
  350.0 3.6 %copy-start.3 = (f32[256,1024]{1,0:T(8,128)S(1)}, f32[256,1024]{1,0:T(8,128)}, u32[]{:S(2)}) copy-start(f32[256,1024]{1,0:T(8,128)} %get-tuple-element.126) | copy-start | bytes 3145732

commit v4 on v3

--- a/solution.py
+++ b/solution.py
@@ -107,6 +107,20 @@
 
     lax.fori_loop(1, n, go, 0)
     return own
+
+
+def rows_each(n, me, core, rows, landing, send_sem, recv_sem, own_sem):
+    own = pltpu.make_async_copy(rows.at[me], landing.at[me], own_sem)
+    own.start()
+
+    def go(i):
+        to = (me + i) % n
+        pltpu.make_async_remote_copy(
+            src_ref=rows.at[to], dst_ref=landing.at[me], send_sem=send_sem, recv_sem=recv_sem,
+            device_id=(to, core), device_id_type=MESH,
+        ).start()
+
+    return own, [functools.partial(go, i) for i in (ORDER or range(1, n))]
 
 
 def rows_wait(n, me, core, rows, landing, send_sem, recv_sem, own):
@@ -591,7 +605,9 @@
         return ref.at[block, :, pl.ds(self.offset, self.width)]
 
 
-EARLY, AT0, AT1, CUT, SPLIT = 60, 4, 85, 70, False
+EARLY, AT0, AT1, CUT, SPLIT = 30, 4, 85, 50, False
+AHEAD = 2
+ROWS_IN, ROWS_OUT, ORDER = (0, 100), 4, ()
 
 
 def first_shares(axes, vectors):
@@ -821,12 +837,13 @@
     def stages(self):
         light, heavy = self.numbered[:2], self.numbered[2:]
         steps, few = heavy[0][0][0][1], max(c[0][0][1] for c in light)
-        found = [functools.partial(self.lead, *colour, 0) for colour in heavy + light]
+        found = [functools.partial(self.lead, *c, s) for c in heavy[::-1] for s in range(min(AHEAD, steps))]
+        found += [functools.partial(self.lead, *colour, 0) for colour in light]
         for s in range(max(steps, few + 1)):
             if s < steps:
                 found += [functools.partial(self.later, *colour, s, 0, 1) for colour in heavy]
-            if s + 1 < steps:
-                found += [functools.partial(self.lead, *colour, s + 1) for colour in heavy]
+            if s + AHEAD < steps:
+                found += [functools.partial(self.lead, *colour, s + AHEAD) for colour in heavy]
             if 1 <= s < steps:
                 found += [functools.partial(self.finish, *colour, s - 1) for colour in heavy]
             found += [functools.partial(self.lead, *c, s + 1) for c in light if s + 1 < c[0][0][1]]
@@ -908,15 +925,29 @@
     gathers = [Gather(n, me, core, part, blocks, g_sems) for part in (numbered[:4], numbered[4:])]
     gathers[0].start()
     row_sems = [misc.at[40 + k] for k in range(6)]
-    own_rows = rows_out(n, me, core, r.rows_in, r.land, *row_sems[:3])
+    def spread(items, chunks, low, high):
+        done = 0
+        for number, item in enumerate(items):
+            item()
+            want = len(chunks) * (number + 1 - low) // max(high - low, 1) if number + 1 >= low else 0
+            while done < min(max(want, 0), len(chunks)):
+                chunks[done]()
+                done += 1
+        for chunk in chunks[done:]:
+            chunk()
+
+    own_rows, row_sends = rows_each(n, me, core, r.rows_in, r.land, *row_sems[:3])
     note = to_pair(r.notes, r.NOTE)
     events = gathers[0].events()
-    early = len(events) * EARLY // 100
-    for event in events[:early]:
-        event()
-    gathers[1].start()
-    for event in events[early:]:
-        event()
+    events.insert(len(events) * EARLY // 100, gathers[1].start)
+    behind = gathers[1].events()
+    late_sends = []
+    if ROWS_IN[1] > 100:
+        late_sends = row_sends[(n - 1) * 100 // ROWS_IN[1]:]
+        row_sends = row_sends[: (n - 1) * 100 // ROWS_IN[1]]
+    spread(events, row_sends, len(events) * ROWS_IN[0] // 100, len(events) * min(ROWS_IN[1], 100) // 100)
+    for number, chunk in enumerate(late_sends):
+        behind.insert(2 * number, chunk)
     mine, theirs = pl.ds(0, CAP), pl.ds(CAP, CAP)
     STEP = 64
     TILE = 256
@@ -1035,17 +1066,6 @@
     def some(fn, low, high):
         return lambda: lax.fori_loop(low, high, lambda e, _: (fn(e), 0)[1], 0)
 
-    def spread(items, chunks, low, high):
-        done = 0
-        for number, item in enumerate(items):
-            item()
-            want = len(chunks) * (number + 1 - low) // max(high - low, 1)
-            while done < min(max(want, 0), len(chunks)):
-                chunks[done]()
-                done += 1
-        for chunk in chunks[done:]:
-            chunk()
-
     forward = [rows_here, functools.partial(extract, 0, r.X), functools.partial(extract, 1, r.DY), swap_rows, first_rows]
     forward += [some(project, e, e + 1) for e in range(3 * half // TILE)]
     forward += [some(attend, e, e + 2) for e in range(0, 2 * pairs, 2)]
@@ -1053,8 +1073,7 @@
         functools.partial(project_out, 0), functools.partial(project_out, 1),
         lambda: pass_on(r.BA, r.GOT1), second_rows,
     ]
-    events = gathers[1].events()
-    spread(events, forward, len(events) * AT0 // 100, len(events) * AT1 // 100)
+    spread(behind, forward, len(behind) * AT0 // 100, len(behind) * AT1 // 100)
     hidden = r.Wd.shape[1]
     per = TILE // hidden if hidden < TILE else 1
 
@@ -1197,7 +1216,7 @@
         r.rows_out[:, :, cols(e)] = sent.reshape(n, -1, TILE)
 
     def send_late():
-        flying.rows = rows_out(n, me, core, r.rows_out, r.landed, *row_sems[3:])
+        flying.rows, flying.sends = rows_each(n, me, core, r.rows_out, r.landed, *row_sems[3:])
         flying.small.wait()
         flying.out.wait()
         r.As[...] = r.As[...] + r.As2[...]
@@ -1213,11 +1232,16 @@
     backward += [last_out]
     backward += [some(qkv_grads, e, e + 1) for e in range(3 * half // TILE)]
     backward += [fifth_rows, some(place, 0, D // TILE), send_late]
+    stages = soon.stages()
+    for stage in stages[:AHEAD]:
+        stage()
     each(tiles, up_grads)
-    stages = soon.stages()
+    stages = stages[AHEAD:]
     cut = len(stages) * CUT // 100
     spread(stages[:cut], backward, 1, cut)
     rest, more = stages[cut:], late.stages()
+    for number, chunk in enumerate(flying.sends):
+        more.insert((number + 1) * ROWS_OUT - 1 if ROWS_OUT else 0, chunk)
     while rest or more:
         if more:
             more.pop(0)()
@@ -1228,7 +1252,7 @@
     final = [to_pair(acc[k].at[me], ref) for k, ref in enumerate((r.FQ, r.FO, r.FU, r.FD))]
 
     def give(k, side, ref):
-        value = ref[...].astype(jnp.float32)
+        value = ref[...]
         if k == 0:
             for j in range(3):
                 r.gq[:, pl.ds(pl.multiple_of(j * D + side * half, 128), half)] = value[:, j * half : (j + 1) * half]
@@ -1238,7 +1262,7 @@
             for f in range(n):
                 r.gu[:, column(2 * f + side, units, 0)] = value[:, f * units : (f + 1) * units]
         else:
-            r.gd[pl.ds(pl.multiple_of(side * units, 8), units), :] = value
+            r.gd[pl.ds(pl.multiple_of(side * units, 16), units), :] = value
 
     for k in range(4):
         give(k, core, acc[k].at[me])
@@ -1262,7 +1286,7 @@
     R, F = weights[0].shape[0], weights[3].shape[0]
     vmem = pl.BlockSpec(memory_space=pltpu.VMEM)
     anywhere = pl.BlockSpec(memory_space=ANY)
-    out = [jax.ShapeDtypeStruct(w.shape, f32) for w in shards]
+    out = [jax.ShapeDtypeStruct(w.shape, bf) for w in shards]
     out += [
         jax.ShapeDtypeStruct((8, 128), f32),
         jax.ShapeDtypeStruct(rows_in.shape, bf),
@@ -1631,20 +1655,21 @@
     mine = jnp.max(flag)
     other = lax.ppermute(flag, "rep", [(0, 1), (1, 0)])
     crowded = jnp.maximum(mine, jnp.max(other)) > 0
-    positions = jnp.arange(SEQ_MAX, dtype=jnp.int32)
+    ring = [(i, (i + 1) % shards) for i in range(shards)]
+
+    def chosen(j):
+        return (lax.dynamic_index_in_dim(row_routes, j, 0, keepdims=False)[:, None] == here[None, :]).astype(jnp.bfloat16)
 
     def all_rows():
-        onehot = (routes[:, None] == positions[None, :]).astype(jnp.bfloat16)
-        return jnp.concatenate(
-            [
-                jnp.dot(
-                    onehot,
-                    lax.all_to_all(t, "fsdp", split_axis=1, concat_axis=2, tiled=True)[0, 0],
-                    preferred_element_type=jnp.float32,
-                ).astype(jnp.bfloat16)
+        def go(i, rows):
+            j = (place - 1 - i) % shards
+            mine = [
+                jnp.dot(chosen(j), lax.dynamic_index_in_dim(t[0], j, 0, keepdims=False), preferred_element_type=jnp.float32)
                 for t in (tokens, cotangent)
             ]
-        )
+            return lax.ppermute(rows, "fsdp", ring) + jnp.concatenate(mine).astype(jnp.bfloat16)
+
+        return lax.fori_loop(0, shards, go, jnp.zeros((2 * CAP, D), jnp.bfloat16))
 
     extra = jnp.zeros((2 * CAP, D), jnp.bfloat16)
     if cap < width:
@@ -1659,6 +1684,7 @@
         axes, shards, cap, weights, vectors, packed_rows, pick, extra, notes
     )
     small = lax.dynamic_slice(gs, (0, lanes), (8, part))
+    gq, go, gu, gd = (g.astype(jnp.float32) for g in (gq, go, gu, gd))
     totals = (gq, go, gu, gd, small[0], small[1], small[2])
 
     def place_rows(rows, held):
@@ -1670,17 +1696,20 @@
         return place_rows(landed[:, :cap], tokens), place_rows(landed[:, cap:], cotangent)
 
     def entire(landed, rows):
-        positions = jnp.arange(SEQ_MAX, dtype=jnp.int32)
-        onehot = (routes[:, None] == positions[None, :]).astype(jnp.bfloat16)
-        placed = []
-        for r, held in ((rows[:CAP], tokens), (rows[CAP:], cotangent)):
-            spread = jnp.einsum("cp,cd->pd", onehot, r, preferred_element_type=jnp.float32)
-            spread = lax.all_to_all(
-                spread.astype(jnp.bfloat16)[None, None], "fsdp", split_axis=2, concat_axis=1, tiled=True
-            )
-            kept = jnp.where(touched[..., None], spread[0], held[0])
-            placed.append(jnp.where(living[..., None], kept, jnp.zeros_like(kept))[None])
-        return tuple(placed)
+        def go(i, held):
+            rows, placed = held
+            j = (place - i) % shards
+            done = []
+            for k, (t, whole) in enumerate(zip((tokens, cotangent), placed)):
+                spread = jnp.einsum(
+                    "cp,cd->pd", chosen(j), rows[k * CAP : k * CAP + CAP], preferred_element_type=jnp.float32
+                ).astype(jnp.bfloat16)
+                kept = jnp.where(lax.dynamic_index_in_dim(touched, j, 0, keepdims=False)[:, None], spread, t[0, j])
+                kept = jnp.where(lax.dynamic_index_in_dim(living, j, 0, keepdims=False)[:, None], kept, jnp.zeros_like(kept))
+                done.append(lax.dynamic_update_slice(whole, kept[None, None], (0, j, 0, 0)))
+            return lax.ppermute(rows, "fsdp", ring), tuple(done)
+
+        return lax.fori_loop(0, shards, go, (rows, (jnp.zeros_like(tokens), jnp.zeros_like(cotangent))))[1]
 
     if cap < width:
         back_out, back_grad = lax.cond(crowded, entire, compact, landed, new_rows)

time: 351 us -> 317 us (0.903); the launches traced: 355 us -> 317 us
  Pallas kernels: 322 us -> 284 us
  other arithmetic: 9.29 us -> 16.2 us
  local copies, waits for them, and re-layouts: 8.17 us -> 2.98 us
    pallas_call x1, Pallas kernels: 322 us -> 284 us  [whole_block(): pl.pallas_call(functools.partial(block_kernel, axes, n, cap), out_shape=o...]
    convert_element_type x0 -> x4, other arithmetic: none -> 6.91 us  [wide_body(): gq, go, gu, gd = (g.astype(jnp.float32) for g in (gq, go, gu, gd))]
    unnamed x22 -> x32, local copies, waits for them, and re-layouts: 4.57 us -> 0.08 us
where the time goes in v4:
time: 317 us
  Pallas kernels  284 us (90%)
  other arithmetic  16.2 us (5%)
  matrix products  7.57 us (2%)
  between operations  4.91 us (2%)
    pallas_call x1, Pallas kernels, whole_block(): pl.pallas_call(functools.partial(block_kernel, axes, n, cap), out_shape=o...  284 us
    convert_element_type x4, other arithmetic, wide_body(): gq, go, gu, gd = (g.astype(jnp.float32) for g in (gq, go, gu, gd))  6.91 us
  transfers between devices with their start and end apart: 1, of which 0 were waited for; matrix products, arithmetic and copies ran while one was open for 2% of the time, Pallas kernels for 0%

profile of v4, /device:TPU:0, one launch (start us, length us, event | category | flops | bytes accessed | tf_op | source)
XLA Modules:
  0.0 316.8 jit_solution(11972694886193029147)
XLA Ops:
  0.6 0.0 copy-start.1
  0.7 0.9 iota_compare_fusion.6
  1.5 0.9 select_reduce_fusion.1
  2.4 0.8 select_reduce_fusion
  3.2 0.1 add_select_fusion
  3.3 0.3 convert_reduce_fusion.2
  3.7 0.6 reduce_max.16
  5.0 0.6 collective-permute-start.2
  5.5 0.6 dynamic_slice.86
  7.5 0.0 copy-start.6
  7.5 0.7 convert_reduce_fusion
  8.1 0.7 broadcast_compare_fusion
  10.1 0.2 convert_reduce_fusion.3
  10.3 0.1 slice_reduce_fusion
  10.4 0.6 subtract_select_fusion
  11.0 0.7 fusion.47
  11.7 2.0 fusion.40
  13.7 0.4 fusion.43
  14.1 0.0 copy-start.13
  14.1 0.0 copy-start.14
  14.1 0.0 copy-start.15
  14.1 1.3 pad_maximum_fusion.refs_5_
  15.4 0.2 iota_compare_fusion
  15.7 0.2 dynamic_update_slice.23.refs_4_
  15.8 0.0 copy-start.11
  15.8 0.0 collective-permute-done.2
  15.9 0.6 reduce_max.20
  17.1 0.8 fusion.46.refs_6_
  18.0 0.0 copy-done.11
  18.0 0.9 conditional.2
  18.0 0.9 broadcast.249
  18.8 0.6 broadcast_in_dim.222.refs_8_
  19.4 284.5 %whole_block.1 = (bf16[64,3072]{1,0:T(8,128)(2,1)}, bf16[64,1024]{1,0:T(8,128)(2,1)}, bf16[64,4096]{1,0:T(8,128)(2,1)}, bf16[256,1024]{1,0:T(8,128)(2,1)}, f32[8...) custom-call(bf16[64,3072]{1,0:T(8,128)(2,1)} %refs_0_.1, bf16[64,1024]{1,0:T(8,128)(2,1)} %refs_1_.1, ...), custom_call_target="tpu_custom_call" | custom-call | tf_op jit(solution)/shard_map/whole_block/pallas_call | solution.py:1328
  303.9 0.0 copy-start.2
  304.0 0.0 copy-start.3
  304.0 0.0 copy-start.4
  304.0 2.2 convert_element_type.108
  306.2 2.1 convert_element_type.109
  308.4 0.9 convert_element_type.106
  309.3 1.6 convert_element_type.107
  310.9 0.0 copy-done.12
  310.9 0.1 constant_dynamic-slice_fusion.2
  311.0 0.5 slice_bitcast_fusion
  311.5 0.0 copy-done.3
  311.5 0.0 copy-done.4
  311.6 5.2 %conditional.3 = (bf16[1,16,64,1024]{3,2,1,0:T(8,128)(2,1)}, bf16[1,16,64,1024]{3,2,1,0:T(8,128)(2,1)}) conditional(s32[]{:T(128)} %convert_element_type.97, (pred[16,64]{1,0:T(8,128)(4,1)S(1)}, pred[16,64]{1,0:T(8,128)(4,1)S(1)}, bf16[16,48,1024]{2,1,0:T(8,128)(2,1)S(1)}, bf16[16,24,64]{2,1,0:T(8,128)(2,1)S(1)}, ...), branch_computations={%region_12.13_spmd, %region_13.16_spmd} | conditional | flops 106954752 | bytes 10166288 | solution.py:1715
  311.6 2.0 fusion.1
  313.6 3.2 %fusion.3 = bf16[1,16,64,1024]{3,2,1,0:T(8,128)(2,1)} fusion(bf16[1,16,64,1024]{3,2,1,0:T(8,128)(2,1)} %get-tuple-element.482, pred[16,64]{1,0:T(8,128)(4,1)S(1)} %get-tuple-element.479, pred[16,64]{1,0:T(8,128)(4,1)S(1)} %get-tuple-element.478, bf16[16,24,64]{2,1,0:T(8,128)(2,1)S(1)} %get-tuple-element.480, bf16[16,48,1024]{2,1,0:T(8,128)(2,1)S(1)} %get-tuple-element.481), kind=kOutput, calls=%fused_computation.5 | convolution fusion | flops 53477376 | bytes 5083136 | tf_op jit(solution)/shard_map/cond/branch_0_fun/jip,jid->jpd/dot_general | solution.py:1691
  (28 shorter events, 0.1 us)
Async XLA Ops:
  0.6 13.1 %copy-start.1 = (bf16[1,16,64,1024]{3,2,1,0:T(8,128)(2,1)S(1)}, bf16[1,16,64,1024]{3,2,1,0:T(8,128)(2,1)}, u32[]{:S(2)}) copy-start(bf16[1,16,64,1024]{3,2,1,0:T(8,128)(2,1)} %param.21) | copy-start | bytes 6291460
  3.3 14.7 %copy-start.10 = (s32[16,128]{1,0:T(8,128)}, s32[16,128]{1,0:T(8,128)S(1)}, u32[]{:S(2)}) copy-start(s32[16,128]{1,0:T(8,128)S(1)} %get-tuple-element.601) | copy-start | bytes 24580
  5.0 10.9 %collective-permute-start.2 = (f32[8,128]{1,0:T(8,128)S(1)}, f32[8,128]{1,0:T(8,128)S(1)}, u32[]{:S(2)}, u32[]{:S(2)}) collective-permute-start(f32[8,128]{1,0:T(8,128)S(1)} %broadcast_in_dim.218), channel_id=1, source_target_pairs={{0,1},{1,0},{2,3},{3,2},{4,5},{5,4},{6,7},{7,6},{8,9},{9,8},{10,11... | collective-permute-start | bytes 12296 | tf_op jit(solution)/shard_map/ppermute | solution.py:1656
  7.5 10.5 %copy-start.6 = (s32[64]{0:T(128)}, s32[64]{0:T(128)S(1)}, u32[]{:S(2)}) copy-start(s32[64]{0:T(128)S(1)} %iota_add_fusion.1) | copy-start | bytes 772
  14.1 1.5 copy-start.13
  14.1 1.5 copy-start.14
  14.1 1.5 copy-start.15
  15.8 2.1 copy-start.11
  303.9 4.5 %copy-start.5 = (bf16[64,3072]{1,0:T(8,128)(2,1)S(1)}, bf16[64,3072]{1,0:T(8,128)(2,1)}, u32[]{:S(2)}) copy-start(bf16[64,3072]{1,0:T(8,128)(2,1)} %get-tuple-element.528) | copy-start | bytes 1179652
  303.9 7.0 %copy-start.12 = (f32[8,128]{1,0:T(8,128)S(1)}, f32[8,128]{1,0:T(8,128)}, u32[]{:S(2)}) copy-start(f32[8,128]{1,0:T(8,128)} %get-tuple-element.532) | copy-start | bytes 12292
  303.9 7.6 %copy-start = (bf16[256,1024]{1,0:T(8,128)(2,1)S(1)}, bf16[256,1024]{1,0:T(8,128)(2,1)}, u32[]{:S(2)}) copy-start(bf16[256,1024]{1,0:T(8,128)(2,1)} %get-tuple-element.525) | copy-start | bytes 1572868
  303.9 7.6 %copy-start.2 = (bf16[1,16,64,1024]{3,2,1,0:T(8,128)(2,1)S(1)}, bf16[1,16,64,1024]{3,2,1,0:T(8,128)(2,1)}, u32[]{:S(2)}) copy-start(bf16[1,16,64,1024]{3,2,1,0:T(8,128)(2,1)} %param.21) | copy-start | bytes 6291460
  304.0 7.6 %copy-start.3 = (bf16[16,48,1024]{2,1,0:T(8,128)(2,1)S(1)}, bf16[16,48,1024]{2,1,0:T(8,128)(2,1)}, u32[]{:S(2)}) copy-start(bf16[16,48,1024]{2,1,0:T(8,128)(2,1)} %get-tuple-element.524) | copy-start | bytes 4718596
  304.0 7.6 %copy-start.4 = (bf16[16,24,64]{2,1,0:T(8,128)(2,1)S(1)}, bf16[16,24,64]{2,1,0:T(8,128)(2,1)}, u32[]{:S(2)}) copy-start(bf16[16,24,64]{2,1,0:T(8,128)(2,1)} %fusion.47) | copy-start | bytes 147460
  304.0 7.6 %copy-start.7 = (s32[64]{0:T(128)S(1)}, s32[64]{0:T(128)}, u32[]{:S(2)}) copy-start(s32[64]{0:T(128)} %copy-done.6) | copy-start | bytes 772
  304.0 7.6 %copy-start.8 = (pred[16,64]{1,0:T(8,128)(4,1)S(1)}, pred[16,64]{1,0:T(8,128)(4,1)}, u32[]{:S(2)}) copy-start(pred[16,64]{1,0:T(8,128)(4,1)} %broadcast_compare_fusion) | copy-start | bytes 3076
  304.0 7.6 %copy-start.9 = (pred[16,64]{1,0:T(8,128)(4,1)S(1)}, pred[16,64]{1,0:T(8,128)(4,1)}, u32[]{:S(2)}) copy-start(pred[16,64]{1,0:T(8,128)(4,1)} %get-tuple-element.599) | copy-start | bytes 3076

commit v5 on v4

--- a/solution.py
+++ b/solution.py
@@ -606,18 +606,18 @@
 
 
 EARLY, AT0, AT1, CUT, SPLIT = 30, 4, 85, 50, False
-AHEAD = 2
-ROWS_IN, ROWS_OUT, ORDER = (0, 100), 4, ()
+AHEAD = 1
+ROWS_IN, ROWS_OUT, ORDER = (0, 100), 5, ()
 
 
 def first_shares(axes, vectors):
     a, b, c = axes
     half = D // 2
     return [
-        ((b, c, a), [Part(1, 0, D // 8), Part(4, 0, vectors)]),
-        ((c, b, a), [Part(0, 0, D // 8)]),
-        ((a, b, c), [Part(0, D // 8, half + 3 * D // 8)]),
-        ((a, c, b), [Part(0, D, half), Part(1, D // 8, 3 * D // 8)]),
+        ((b, c, a), [Part(1, 0, D // 4), Part(4, 0, vectors)]),
+        ((c, b, a), [Part(0, 0, D // 4)]),
+        ((a, b, c), [Part(0, D // 4, half + D // 4)]),
+        ((a, c, b), [Part(0, D, half), Part(1, D // 4, D // 4)]),
     ]
 
 
@@ -1252,7 +1252,7 @@
     final = [to_pair(acc[k].at[me], ref) for k, ref in enumerate((r.FQ, r.FO, r.FU, r.FD))]
 
     def give(k, side, ref):
-        value = ref[...]
+        value = ref[...].astype(jnp.float32)
         if k == 0:
             for j in range(3):
                 r.gq[:, pl.ds(pl.multiple_of(j * D + side * half, 128), half)] = value[:, j * half : (j + 1) * half]
@@ -1286,7 +1286,7 @@
     R, F = weights[0].shape[0], weights[3].shape[0]
     vmem = pl.BlockSpec(memory_space=pltpu.VMEM)
     anywhere = pl.BlockSpec(memory_space=ANY)
-    out = [jax.ShapeDtypeStruct(w.shape, bf) for w in shards]
+    out = [jax.ShapeDtypeStruct(w.shape, f32) for w in shards]
     out += [
         jax.ShapeDtypeStruct((8, 128), f32),
         jax.ShapeDtypeStruct(rows_in.shape, bf),
@@ -1684,7 +1684,6 @@
         axes, shards, cap, weights, vectors, packed_rows, pick, extra, notes
     )
     small = lax.dynamic_slice(gs, (0, lanes), (8, part))
-    gq, go, gu, gd = (g.astype(jnp.float32) for g in (gq, go, gu, gd))
     totals = (gq, go, gu, gd, small[0], small[1], small[2])
 
     def place_rows(rows, held):

time: 317 us -> 312 us (0.984)
  other arithmetic: 16.2 us -> 9.31 us
  local copies, waits for them, and re-layouts: 2.98 us -> 8.18 us
  Pallas kernels: 284 us -> 279 us
    convert_element_type x4 -> x0, other arithmetic: 6.91 us -> none  [wide_body(): gq, go, gu, gd = (g.astype(jnp.float32) for g in (gq, go, gu, gd))]
    pallas_call x1, Pallas kernels: 284 us -> 279 us  [whole_block(): pl.pallas_call(functools.partial(block_kernel, axes, n, cap), out_shape=o...]
    unnamed x32 -> x24, local copies, waits for them, and re-layouts: 0.08 us -> 4.58 us
where the time goes in v5:
time: 312 us; the launch traced here: 310 us
  Pallas kernels  279 us (89%)
  other arithmetic  9.31 us (3%)
  matrix products  8.49 us (3%)
  local copies, waits for them, and re-layouts  8.18 us (3%)
  between operations  4.81 us (2%)
    pallas_call x1, Pallas kernels, whole_block(): pl.pallas_call(functools.partial(block_kernel, axes, n, cap), out_shape=o...  279 us
  transfers between devices with their start and end apart: 1, of which 0 were waited for; matrix products, arithmetic and copies ran while one was open for 2% of the time, Pallas kernels for 0%

profile of v5, /device:TPU:0, one launch (start us, length us, event | category | flops | bytes accessed | tf_op | source)
XLA Modules:
  0.0 310.1 jit_solution(1390588095579242421)
XLA Ops:
  0.6 0.0 copy-start.2
  0.7 0.9 iota_compare_fusion.6
  1.5 0.9 select_reduce_fusion.1
  2.4 0.8 select_reduce_fusion
  3.2 0.1 add_select_fusion
  3.3 0.0 copy-start.12
  3.3 0.3 convert_reduce_fusion.2
  3.7 0.6 reduce_max.16
  5.0 0.6 collective-permute-start.2
  5.5 0.6 dynamic_slice.86
  7.4 0.7 broadcast_compare_fusion
  8.1 0.7 convert_reduce_fusion
  10.1 0.2 convert_reduce_fusion.3
  10.3 0.1 slice_reduce_fusion
  10.4 0.6 subtract_select_fusion
  11.0 0.7 fusion.47
  11.7 2.0 fusion.43
  13.7 0.4 fusion.40
  14.1 0.0 copy-start.14
  14.1 0.0 copy-start.15
  14.1 0.0 copy-start.16
  14.1 1.3 pad_maximum_fusion.refs_5_
  15.4 0.2 iota_compare_fusion
  15.6 0.0 copy-done.14
  15.6 0.0 copy-done.15
  15.6 0.0 copy-done.16
  15.7 0.2 dynamic_update_slice.23.refs_4_
  15.8 0.0 copy-start.13
  15.8 0.0 collective-permute-done.2
  15.8 0.6 reduce_max.20
  17.1 0.8 fusion.46.refs_6_
  17.9 0.0 copy-done.12
  17.9 0.0 copy-done.13
  17.9 0.9 conditional.2
  17.9 0.9 broadcast.249
  18.8 0.6 broadcast_in_dim.222.refs_8_
  19.4 278.7 %whole_block.1 = (f32[64,3072]{1,0:T(8,128)}, f32[64,1024]{1,0:T(8,128)}, f32[64,4096]{1,0:T(8,128)}, f32[256,1024]{1,0:T(8,128)}, f32[8,128]{1,0:T(8,128)}, /*i...) custom-call(bf16[64,3072]{1,0:T(8,128)(2,1)} %refs_0_.1, bf16[64,1024]{1,0:T(8,128)(2,1)} %refs_1_.1, ...), custom_call_target="tpu_custom_call" | custom-call | tf_op jit(solution)/shard_map/whole_block/pallas_call | solution.py:1328
  298.1 0.8 constant_dynamic-slice_fusion.2
  298.8 0.5 slice_bitcast_fusion
  299.4 6.2 %conditional.3 = (bf16[1,16,64,1024]{3,2,1,0:T(8,128)(2,1)}, bf16[1,16,64,1024]{3,2,1,0:T(8,128)(2,1)}) conditional(s32[]{:T(128)} %convert_element_type.85, (pred[16,64]{1,0:T(8,128)(4,1)}, pred[16,64]{1,0:T(8,128)(4,1)}, bf16[16,48,1024]{2,1,0:T(8,128)(2,1)}, bf16[16,24,64]{2,1,0:T(8,128)(2,1)}, bf16[1,16,64,1024]{3,2,1,0:T(8,128)(2,1)}, ...), branch_computations={%region_12.13_spmd, %region_13.16_spmd} | conditional | flops 106954752 | bytes 25051292 | solution.py:1714
  299.4 0.0 copy-start.6
  299.4 0.0 copy-start.10
  299.4 4.1 %fusion.3 = bf16[1,16,64,1024]{3,2,1,0:T(8,128)(2,1)} fusion(bf16[1,16,64,1024]{3,2,1,0:T(8,128)(2,1)} %get-tuple-element.482, pred[16,64]{1,0:T(8,128)(4,1)} %get-tuple-element.479, pred[16,64]{1,0:T(8,128)(4,1)} %get-tuple-element.478, bf16[16,24,64]{2,1,0:T(8,128)(2,1)} %get-tuple-element.480, bf16[16,48,1024]{2,1,0:T(8,128)(2,1)} %get-tuple-element.481), kind=kOutput, calls=%fused_computation.5 | convolution fusion | flops 53477376 | bytes 5083136 | tf_op jit(solution)/shard_map/cond/branch_0_fun/jip,jid->jpd/dot_general | solution.py:1690
  303.5 2.0 fusion.1
  305.5 0.9 copy.52
  306.4 1.7 copy.53
  308.1 1.0 copy.54
  309.1 1.0 copy.55
  (26 shorter events, 0.1 us)
Async XLA Ops:
  0.6 13.0 %copy-start.2 = (bf16[1,16,64,1024]{3,2,1,0:T(8,128)(2,1)S(1)}, bf16[1,16,64,1024]{3,2,1,0:T(8,128)(2,1)}, u32[]{:S(2)}) copy-start(bf16[1,16,64,1024]{3,2,1,0:T(8,128)(2,1)} %param.20) | copy-start | bytes 6291460
  3.3 14.6 %copy-start.12 = (s32[16,128]{1,0:T(8,128)}, s32[16,128]{1,0:T(8,128)S(1)}, u32[]{:S(2)}) copy-start(s32[16,128]{1,0:T(8,128)S(1)} %get-tuple-element.601) | copy-start | bytes 24580
  5.0 10.9 %collective-permute-start.2 = (f32[8,128]{1,0:T(8,128)S(1)}, f32[8,128]{1,0:T(8,128)S(1)}, u32[]{:S(2)}, u32[]{:S(2)}) collective-permute-start(f32[8,128]{1,0:T(8,128)S(1)} %broadcast_in_dim.218), channel_id=1, source_target_pairs={{0,1},{1,0},{2,3},{3,2},{4,5},{5,4},{6,7},{7,6},{8,9},{9,8},{10,11... | collective-permute-start | bytes 12296 | tf_op jit(solution)/shard_map/ppermute | solution.py:1656
  7.4 10.5 %copy-start.8 = (s32[64]{0:T(128)}, s32[64]{0:T(128)S(1)}, u32[]{:S(2)}) copy-start(s32[64]{0:T(128)S(1)} %iota_add_fusion.1) | copy-start | bytes 772
  14.1 1.5 copy-start.14
  14.1 1.5 copy-start.15
  14.1 1.5 copy-start.16
  15.8 2.1 copy-start.13
  299.4 6.2 %copy-start.7 = (f32[64,3072]{1,0:T(8,128)S(1)}, f32[64,3072]{1,0:T(8,128)}, u32[]{:S(2)}) copy-start(f32[64,3072]{1,0:T(8,128)} %get-tuple-element.818) | copy-start | bytes 2359300
  299.4 4.2 %copy-start.1 = (bf16[1,16,64,1024]{3,2,1,0:T(8,128)(2,1)S(1)}, bf16[1,16,64,1024]{3,2,1,0:T(8,128)(2,1)}, u32[]{:S(2)}) copy-start(bf16[1,16,64,1024]{3,2,1,0:T(8,128)(2,1)} %get-tuple-element.483) | copy-start | bytes 6291460 | tf_op jit(solution)/shard_map/cond
  299.4 4.2 %copy-start.3 = (bf16[16,48,1024]{2,1,0:T(8,128)(2,1)S(1)}, bf16[16,48,1024]{2,1,0:T(8,128)(2,1)}, u32[]{:S(2)}) copy-start(bf16[16,48,1024]{2,1,0:T(8,128)(2,1)} %get-tuple-element.481) | copy-start | bytes 4718596 | tf_op jit(solution)/shard_map/cond
  299.4 4.2 %copy-start.6 = (bf16[16,24,64]{2,1,0:T(8,128)(2,1)S(1)}, bf16[16,24,64]{2,1,0:T(8,128)(2,1)}, u32[]{:S(2)}) copy-start(bf16[16,24,64]{2,1,0:T(8,128)(2,1)} %get-tuple-element.480) | copy-start | bytes 147460 | tf_op jit(solution)/shard_map/cond
  299.4 4.1 %copy-start.10 = (pred[16,64]{1,0:T(8,128)(4,1)S(1)}, pred[16,64]{1,0:T(8,128)(4,1)}, u32[]{:S(2)}) copy-start(pred[16,64]{1,0:T(8,128)(4,1)} %get-tuple-element.478) | copy-start | bytes 3076 | tf_op jit(solution)/shard_map/cond
  299.4 4.1 %copy-start.11 = (pred[16,64]{1,0:T(8,128)(4,1)S(1)}, pred[16,64]{1,0:T(8,128)(4,1)}, u32[]{:S(2)}) copy-start(pred[16,64]{1,0:T(8,128)(4,1)} %get-tuple-element.479) | copy-start | bytes 3076 | tf_op jit(solution)/shard_map/cond
  305.5 2.6 copy-start.5
  305.5 3.6 %copy-start.4 = (f32[256,1024]{1,0:T(8,128)S(1)}, f32[256,1024]{1,0:T(8,128)}, u32[]{:S(2)}) copy-start(f32[256,1024]{1,0:T(8,128)} %get-tuple-element.821) | copy-start | bytes 3145732

commit v6 on v5

--- a/solution.py
+++ b/solution.py
@@ -605,7 +605,7 @@
         return ref.at[block, :, pl.ds(self.offset, self.width)]
 
 
-EARLY, AT0, AT1, CUT, SPLIT = 30, 4, 85, 50, False
+EARLY, AT0, AT1, CUT, SPLIT = 30, 4, 85, 45, False
 AHEAD = 1
 ROWS_IN, ROWS_OUT, ORDER = (0, 100), 5, ()
 

time: 312 us -> 315 us (level)
  Pallas kernels: 279 us -> 283 us
    pallas_call x1, Pallas kernels: 279 us -> 283 us  [whole_block(): pl.pallas_call(functools.partial(block_kernel, axes, n, cap), out_shape=o...]
where the time goes in v6:
time: 315 us
  Pallas kernels  283 us (90%)
  other arithmetic  9.31 us (3%)
  matrix products  8.5 us (3%)
  local copies, waits for them, and re-layouts  8.18 us (3%)
  between operations  4.81 us (2%)
    pallas_call x1, Pallas kernels, whole_block(): pl.pallas_call(functools.partial(block_kernel, axes, n, cap), out_shape=o...  283 us
  transfers between devices with their start and end apart: 1, of which 0 were waited for; matrix products, arithmetic and copies ran while one was open for 2% of the time, Pallas kernels for 0%

profile of v6, /device:TPU:0, one launch (start us, length us, event | category | flops | bytes accessed | tf_op | source)
XLA Modules:
  0.0 314.5 jit_solution(1754388931190330535)
XLA Ops:
  0.6 0.0 copy-start.2
  0.7 0.9 iota_compare_fusion.6
  1.5 0.9 select_reduce_fusion.1
  2.4 0.8 select_reduce_fusion
  3.2 0.1 add_select_fusion
  3.3 0.0 copy-start.12
  3.3 0.3 convert_reduce_fusion.2
  3.7 0.6 reduce_max.16
  5.0 0.6 collective-permute-start.2
  5.5 0.6 dynamic_slice.86
  7.4 0.0 copy-start.8
  7.4 0.7 broadcast_compare_fusion
  8.1 0.7 convert_reduce_fusion
  10.1 0.2 convert_reduce_fusion.3
  10.3 0.1 slice_reduce_fusion
  10.4 0.6 subtract_select_fusion
  11.0 0.7 fusion.47
  11.7 2.0 fusion.43
  13.7 0.0 copy-done.2
  13.7 0.4 fusion.40
  14.1 0.0 copy-start.14
  14.1 0.0 copy-start.15
  14.1 0.0 copy-start.16
  14.1 1.3 pad_maximum_fusion.refs_5_
  15.4 0.2 iota_compare_fusion
  15.6 0.0 copy-done.14
  15.6 0.0 copy-done.15
  15.6 0.0 copy-done.16
  15.7 0.2 dynamic_update_slice.23.refs_4_
  15.8 0.0 copy-start.13
  15.8 0.0 collective-permute-done.2
  15.8 0.6 reduce_max.20
  17.1 0.8 fusion.46.refs_6_
  17.9 0.9 conditional.2
  17.9 0.9 broadcast.249
  18.8 0.6 broadcast_in_dim.222.refs_8_
  19.4 283.1 %whole_block.1 = (f32[64,3072]{1,0:T(8,128)}, f32[64,1024]{1,0:T(8,128)}, f32[64,4096]{1,0:T(8,128)}, f32[256,1024]{1,0:T(8,128)}, f32[8,128]{1,0:T(8,128)}, /*i...) custom-call(bf16[64,3072]{1,0:T(8,128)(2,1)} %refs_0_.1, bf16[64,1024]{1,0:T(8,128)(2,1)} %refs_1_.1, ...), custom_call_target="tpu_custom_call" | custom-call | tf_op jit(solution)/shard_map/whole_block/pallas_call | solution.py:1328
  302.5 0.8 constant_dynamic-slice_fusion.2
  303.3 0.5 slice_bitcast_fusion
  303.8 6.2 %conditional.3 = (bf16[1,16,64,1024]{3,2,1,0:T(8,128)(2,1)}, bf16[1,16,64,1024]{3,2,1,0:T(8,128)(2,1)}) conditional(s32[]{:T(128)} %convert_element_type.85, (pred[16,64]{1,0:T(8,128)(4,1)}, pred[16,64]{1,0:T(8,128)(4,1)}, bf16[16,48,1024]{2,1,0:T(8,128)(2,1)}, bf16[16,24,64]{2,1,0:T(8,128)(2,1)}, bf16[1,16,64,1024]{3,2,1,0:T(8,128)(2,1)}, ...), branch_computations={%region_12.13_spmd, %region_13.16_spmd} | conditional | flops 106954752 | bytes 25051292 | solution.py:1714
  303.8 0.0 copy-start.6
  303.8 4.1 %fusion.3 = bf16[1,16,64,1024]{3,2,1,0:T(8,128)(2,1)} fusion(bf16[1,16,64,1024]{3,2,1,0:T(8,128)(2,1)} %get-tuple-element.482, pred[16,64]{1,0:T(8,128)(4,1)} %get-tuple-element.479, pred[16,64]{1,0:T(8,128)(4,1)} %get-tuple-element.478, bf16[16,24,64]{2,1,0:T(8,128)(2,1)} %get-tuple-element.480, bf16[16,48,1024]{2,1,0:T(8,128)(2,1)} %get-tuple-element.481), kind=kOutput, calls=%fused_computation.5 | convolution fusion | flops 53477376 | bytes 5083136 | tf_op jit(solution)/shard_map/cond/branch_0_fun/jip,jid->jpd/dot_general | solution.py:1690
  308.0 2.0 fusion.1
  310.0 0.9 copy.52
  310.9 1.7 copy.53
  312.6 1.0 copy.54
  313.6 0.0 copy-done.4
  313.6 1.0 copy.55
  (26 shorter events, 0.1 us)
Async XLA Ops:
  0.6 13.0 %copy-start.2 = (bf16[1,16,64,1024]{3,2,1,0:T(8,128)(2,1)S(1)}, bf16[1,16,64,1024]{3,2,1,0:T(8,128)(2,1)}, u32[]{:S(2)}) copy-start(bf16[1,16,64,1024]{3,2,1,0:T(8,128)(2,1)} %param.20) | copy-start | bytes 6291460
  3.3 14.6 %copy-start.12 = (s32[16,128]{1,0:T(8,128)}, s32[16,128]{1,0:T(8,128)S(1)}, u32[]{:S(2)}) copy-start(s32[16,128]{1,0:T(8,128)S(1)} %get-tuple-element.601) | copy-start | bytes 24580
  5.0 10.9 %collective-permute-start.2 = (f32[8,128]{1,0:T(8,128)S(1)}, f32[8,128]{1,0:T(8,128)S(1)}, u32[]{:S(2)}, u32[]{:S(2)}) collective-permute-start(f32[8,128]{1,0:T(8,128)S(1)} %broadcast_in_dim.218), channel_id=1, source_target_pairs={{0,1},{1,0},{2,3},{3,2},{4,5},{5,4},{6,7},{7,6},{8,9},{9,8},{10,11... | collective-permute-start | bytes 12296 | tf_op jit(solution)/shard_map/ppermute | solution.py:1656
  7.4 10.5 %copy-start.8 = (s32[64]{0:T(128)}, s32[64]{0:T(128)S(1)}, u32[]{:S(2)}) copy-start(s32[64]{0:T(128)S(1)} %iota_add_fusion.1) | copy-start | bytes 772
  14.1 1.5 copy-start.14
  14.1 1.5 copy-start.15
  14.1 1.5 copy-start.16
  15.8 2.1 copy-start.13
  303.8 6.2 %copy-start.7 = (f32[64,3072]{1,0:T(8,128)S(1)}, f32[64,3072]{1,0:T(8,128)}, u32[]{:S(2)}) copy-start(f32[64,3072]{1,0:T(8,128)} %get-tuple-element.818) | copy-start | bytes 2359300
  303.8 4.2 %copy-start.1 = (bf16[1,16,64,1024]{3,2,1,0:T(8,128)(2,1)S(1)}, bf16[1,16,64,1024]{3,2,1,0:T(8,128)(2,1)}, u32[]{:S(2)}) copy-start(bf16[1,16,64,1024]{3,2,1,0:T(8,128)(2,1)} %get-tuple-element.483) | copy-start | bytes 6291460 | tf_op jit(solution)/shard_map/cond
  303.8 4.2 %copy-start.3 = (bf16[16,48,1024]{2,1,0:T(8,128)(2,1)S(1)}, bf16[16,48,1024]{2,1,0:T(8,128)(2,1)}, u32[]{:S(2)}) copy-start(bf16[16,48,1024]{2,1,0:T(8,128)(2,1)} %get-tuple-element.481) | copy-start | bytes 4718596 | tf_op jit(solution)/shard_map/cond
  303.8 4.2 %copy-start.6 = (bf16[16,24,64]{2,1,0:T(8,128)(2,1)S(1)}, bf16[16,24,64]{2,1,0:T(8,128)(2,1)}, u32[]{:S(2)}) copy-start(bf16[16,24,64]{2,1,0:T(8,128)(2,1)} %get-tuple-element.480) | copy-start | bytes 147460 | tf_op jit(solution)/shard_map/cond
  303.8 4.2 %copy-start.10 = (pred[16,64]{1,0:T(8,128)(4,1)S(1)}, pred[16,64]{1,0:T(8,128)(4,1)}, u32[]{:S(2)}) copy-start(pred[16,64]{1,0:T(8,128)(4,1)} %get-tuple-element.478) | copy-start | bytes 3076 | tf_op jit(solution)/shard_map/cond
  303.8 4.2 %copy-start.11 = (pred[16,64]{1,0:T(8,128)(4,1)S(1)}, pred[16,64]{1,0:T(8,128)(4,1)}, u32[]{:S(2)}) copy-start(pred[16,64]{1,0:T(8,128)(4,1)} %get-tuple-element.479) | copy-start | bytes 3076 | tf_op jit(solution)/shard_map/cond
  310.0 2.6 copy-start.5
  310.0 3.6 %copy-start.4 = (f32[256,1024]{1,0:T(8,128)S(1)}, f32[256,1024]{1,0:T(8,128)}, u32[]{:S(2)}) copy-start(f32[256,1024]{1,0:T(8,128)} %get-tuple-element.821) | copy-start | bytes 3145732
